TPU v7x, 32 devices: a whole 2x2x4 slice. The times are simulated.
32 devices in a mesh: chan: 8 (over z, y), tm: 4 (over x, core).
Axes of the slice: x: 2, y: 2, z: 4, core: 2. Of those that a mesh axis runs over, the one named last changes fastest.
Arguments:
- filterbank: bfloat16 [4096, 32768], P('chan', 'tm'), may hold values from -6 to 6
- chan_delay: int32 [4096], P('chan'), may hold values from 0 to 128, as said below
- sub_delay: int32 [64, 64], replicated, may hold values from 0 to 896, as said below
- box_width: int32 [4], replicated, may hold values from 1 to 32, as said below
Outputs:
- ffa_out: float32 [64, 16, 2048], P('chan', None, 'tm')
- box_out: float32 [64, 16, 4, 2048], P('chan', None, None, 'tm')
Inputs may be any that keep to these rules, and one draw needn't show every extreme that they name: `chan_delay`: the value 128 occurs in every draw. `sub_delay`: the value 896 occurs in every draw. `box_width`: the value 32 occurs in every draw.
All inputs are finite; a program needn't handle non-finite values.
Results may differ from a plain program's by a relative error of at most 0.0003.
Values may be sent and summed in bfloat16 or wider, within the bound.
No kernel may reach another device: no remote copies, remote signals or barrier semaphores. Data moves between devices by JAX's collectives and lax.ppermute only.
A program may use at most 128 MiB of HBM per device.

v0:
```python
import functools
import math

import jax
import jax.numpy as jnp
from jax import lax
from jax.experimental import pallas as pl
from jax.experimental.pallas import tpu as pltpu
from jax.sharding import PartitionSpec as P

NCHAN = 4096
NSUB = 64
NDM = 64
NBIN = 2048
LEVELS = 4
MAXW = 32
D1MAX = 128
D2MAX = 896

LANES = 128
F32 = jnp.float32
GROUP = 2**LEVELS
ROW_BLOCKS = NBIN // LANES
LEAD = (D1MAX + D2MAX) // LANES
VMEM_LIMIT = 48 << 20
SCALE = 2.0 ** (-LEVELS / 2) / math.sqrt(NCHAN)


def lane_iota(rows):
    return lax.broadcasted_iota(jnp.int32, (rows, LANES), 1)


def column_exponent(peak):
    return jnp.floor(jnp.log2(jnp.maximum(peak, 2.0**-110))) - 14.0


def scaled(values, exponent):
    return jnp.clip(jnp.round(values * jnp.exp2(-exponent)), -32767.0, 32767.0)


def to_i16(values):
    return values.astype(jnp.int32).astype(jnp.int16)


def pairs(size, flip):
    return [(i, i ^ flip) for i in range(size)]


def subband_kernel(chans, blocks, subs, delay_ref, x_ref, out_ref, sums):
    sub = pl.program_id(0)
    lane = lane_iota(8)
    row = lax.broadcasted_iota(jnp.int32, (8, LANES), 0)
    tiles = chans // 8
    where_from, from_next = [], []
    for tile in range(tiles):
        delay = jnp.zeros((8, LANES), jnp.int32)
        for i in range(8):
            delay = jnp.where(row == i, delay_ref[sub * chans + tile * 8 + i], delay)
        where_from.append((lane + delay) & (LANES - 1))
        from_next.append(lane < delay)

    def load(block):
        loaded = []
        for pair in range(tiles // 2):
            both = x_ref[16 * pair : 16 * pair + 16, block * LANES : (block + 1) * LANES]
            both = both.astype(F32)
            loaded += [both[:8], both[8:]]
        return loaded

    def emit(block, here, after):
        terms = []
        for tile in range(tiles):
            mixed = jnp.where(from_next[tile], after[tile], here[tile])
            terms.append(
                jnp.take_along_axis(
                    mixed, where_from[tile], axis=1, mode="promise_in_bounds"
                )
            )
        while len(terms) > 1:
            terms = [a + b for a, b in zip(terms[::2], terms[1::2])]
        total = jnp.sum(terms[0], axis=0, keepdims=True)
        sums[pl.ds((block + 1) * subs + sub, 1), :] = total

    zero = [jnp.zeros((8, LANES), F32)] * tiles
    here = zero
    for block in range(-1, blocks):
        after = load(block + 1) if block + 1 < blocks else zero
        emit(block, here, after)
        here = after

    @pl.when(sub == subs - 1)
    def _():
        rows = (blocks + 1) * subs
        values = sums[...].reshape(blocks + 1, subs, LANES)
        exponent = column_exponent(jnp.max(jnp.abs(values), axis=0))
        out_ref[0:rows, :] = to_i16(scaled(values, exponent[None]).reshape(rows, LANES))
        out_ref[rows : rows + subs, :] = to_i16(exponent)


def subband_sums(filterbank, chan_delay, subs):
    chans_here, samples = filterbank.shape
    chans, blocks = chans_here // subs, samples // LANES
    rows = (blocks + 2) * subs
    return pl.pallas_call(
        functools.partial(subband_kernel, chans, blocks, subs),
        grid=(subs,),
        in_specs=[
            pl.BlockSpec(memory_space=pltpu.SMEM),
            pl.BlockSpec((chans, samples), lambda i: (i, 0)),
        ],
        out_specs=pl.BlockSpec((rows, LANES), lambda i: (0, 0)),
        out_shape=jax.ShapeDtypeStruct((rows, LANES), jnp.int16),
        scratch_shapes=[pltpu.VMEM(((blocks + 1) * subs, LANES), F32)],
        compiler_params=pltpu.CompilerParams(vmem_limit_bytes=VMEM_LIMIT),
        name="subbands",
    )(chan_delay, filterbank)


def trial_kernel(blocks, subs, trials, flips, coded, n_in, delay_ref, *refs):
    parts, outs = refs[:n_in], refs[n_in : n_in + len(flips)]
    spread, acc = refs[n_in + len(flips) :]
    chan = lax.axis_index("chan")
    out_blocks = LEAD + blocks
    depth = out_blocks + LEAD + 1
    for at, part in enumerate(parts):
        base = at * depth * subs
        rows = (blocks + 1) * subs
        scale = jnp.exp2(part[rows : rows + subs, :].astype(F32))
        lead = (LEAD - 1) * subs
        spread[base : base + lead, :] = jnp.zeros((lead, LANES), F32)
        tail = base + lead + rows
        spread[tail : base + depth * subs, :] = jnp.zeros(
            (depth * subs - lead - rows, LANES), F32
        )
        values = part[0:rows, :].astype(F32).reshape(blocks + 1, subs, LANES)
        spread[base + lead : tail, :] = (values * scale[None]).reshape(rows, LANES)

    lane = lane_iota(out_blocks)

    def one_trial(trial, owner, out):
        total = jnp.zeros((out_blocks, LANES), F32)
        for at in range(n_in):
            for sub in range(subs):
                delay = delay_ref[owner * trials + trial, (chan ^ at) * subs + sub]
                shift = delay & (LANES - 1)
                first = at * depth * subs + (delay >> 7) * subs + sub
                here = spread[pl.ds(first, out_blocks, stride=subs), :]
                after = spread[pl.ds(first + subs, out_blocks, stride=subs), :]
                mixed = jnp.where(lane < shift, after, here)
                total = total + pltpu.roll(mixed, (LANES - shift) & (LANES - 1), 1)
        out[pl.ds(trial, out_blocks, stride=trials), :] = total

    rows = out_blocks * trials
    for flip, out in zip(flips, outs):
        target = acc if coded else out

        @pl.loop(0, trials)
        def _(trial):
            one_trial(trial, chan ^ flip, target)

        if coded:
            values = acc[...].reshape(out_blocks, trials, LANES)
            exponent = column_exponent(jnp.max(jnp.abs(values), axis=0))
            out[0:rows, :] = to_i16(
                scaled(values, exponent[None]).reshape(rows, LANES)
            )
            out[rows : rows + trials, :] = to_i16(exponent)


def trial_sums(parts, sub_delay, blocks, subs, trials, flips, coded):
    out_blocks = LEAD + blocks
    depth = out_blocks + LEAD + 1
    rows = out_blocks * trials
    out = jax.ShapeDtypeStruct(
        (rows + trials if coded else rows, LANES), jnp.int16 if coded else F32
    )
    vmem = pl.BlockSpec(memory_space=pltpu.VMEM)
    return pl.pallas_call(
        functools.partial(
            trial_kernel, blocks, subs, trials, flips, coded, len(parts)
        ),
        in_specs=[pl.BlockSpec(memory_space=pltpu.SMEM)] + [vmem] * len(parts),
        out_specs=[vmem] * len(flips),
        out_shape=[out] * len(flips),
        scratch_shapes=[
            pltpu.VMEM((len(parts) * depth * subs, LANES), F32),
            pltpu.VMEM((rows, LANES), F32),
        ],
        compiler_params=pltpu.CompilerParams(vmem_limit_bytes=VMEM_LIMIT),
        name="trials_coded" if coded else "trials",
    )(sub_delay, *parts)


def cut_kernel(blocks, trials, owners, n_far, own_ref, *refs):
    far, mine, sends = refs[:n_far], refs[n_far], refs[n_far + 1 : n_far + owners]
    series, whole, piece = refs[n_far + owners :]
    here = lax.axis_index("tm")
    out_blocks = LEAD + blocks
    rows = out_blocks * trials
    total = own_ref[...].reshape(out_blocks, trials, LANES)
    for part in far:
        scale = jnp.exp2(part[rows : rows + trials, :].astype(F32))
        values = part[0:rows, :].astype(F32).reshape(out_blocks, trials, LANES)
        total = total + values * scale[None]
    total = total * SCALE
    ahead = (ROW_BLOCKS - LEAD) * trials
    exponent = column_exponent(jnp.max(jnp.abs(total), axis=0))
    for target, values in ((series, total), (whole, scaled(total, exponent[None]))):
        target[0:ahead, :] = jnp.zeros((ahead, LANES), F32)
        target[ahead : ahead + rows, :] = values.reshape(rows, LANES)
    periods = blocks // ROW_BLOCKS
    bin_blocks = ROW_BLOCKS // owners
    for flip in range(owners):
        source, target = (series, mine) if flip == 0 else (whole, piece)
        at = 0
        for period in range(periods + 1):
            for j in range(bin_blocks + 1):
                block = ((here ^ flip) * bin_blocks + j) & (ROW_BLOCKS - 1)
                first = (period * ROW_BLOCKS + block) * trials
                target[at : at + trials, :] = source[pl.ds(first, trials), :]
                at += trials
        if flip:
            sends[flip - 1][0:at, :] = to_i16(piece[...])
            sends[flip - 1][at : at + trials, :] = to_i16(exponent)


def cut_by_phase(own, far, blocks, trials, owners):
    out_blocks = LEAD + blocks
    periods = blocks // ROW_BLOCKS
    bin_blocks = ROW_BLOCKS // owners
    rows = (periods + 1) * (bin_blocks + 1) * trials
    vmem = pl.BlockSpec(memory_space=pltpu.VMEM)
    held = (out_blocks + ROW_BLOCKS - LEAD) * trials
    return pl.pallas_call(
        functools.partial(cut_kernel, blocks, trials, owners, len(far)),
        in_specs=[vmem] * (1 + len(far)),
        out_specs=[vmem] * owners,
        out_shape=[jax.ShapeDtypeStruct((rows, LANES), F32)]
        + [jax.ShapeDtypeStruct((rows + trials, LANES), jnp.int16)] * (owners - 1),
        scratch_shapes=[
            pltpu.VMEM((held, LANES), F32),
            pltpu.VMEM((held, LANES), F32),
            pltpu.VMEM((rows, LANES), F32),
        ],
        compiler_params=pltpu.CompilerParams(vmem_limit_bytes=VMEM_LIMIT),
        name="cut",
    )(own, *far)


def fold_kernel(periods, trials, owners, widths, width_ref, mine_ref, *refs):
    parts, (ffa_ref, box_ref) = refs[: owners - 1], refs[owners - 1 : owners + 1]
    rows_in, code, folded = refs[owners + 1 :]
    here = lax.axis_index("tm")
    bin_blocks = ROW_BLOCKS // owners
    row_len = (bin_blocks + 1) * trials
    held = periods * row_len
    rows_in[0:row_len, :] = jnp.zeros((row_len, LANES), F32)
    for flip in range(owners):
        if flip == 0:
            rest = mine_ref[row_len : row_len + held, :]
        else:
            part = parts[flip - 1]
            total = row_len + held
            scale = jnp.exp2(part[total : total + trials, :].astype(F32))
            values = part[0:total, :].astype(F32)
            values = values.reshape(total // trials, trials, LANES) * scale[None]
            code[flip - 1] = values.reshape(total, LANES)
            rest = code[flip - 1, row_len : row_len + held, :]
        first = (here ^ flip) * held + row_len
        rows_in[pl.ds(first, held), :] = rest
    for flip in range(owners):
        early = mine_ref[0:row_len, :] if flip == 0 else code[flip - 1, 0:row_len, :]
        first = (here ^ flip) * held
        rows_in[pl.ds(first, row_len), :] += early

    tap = lax.broadcasted_iota(jnp.int32, (2 * LANES, LANES), 0) - lax.broadcasted_iota(
        jnp.int32, (2 * LANES, LANES), 1
    )
    bands, weights = [], []
    for w in range(widths):
        width = width_ref[w]
        inside = jnp.logical_and(tap >= 0, tap < width)
        bands.append(jnp.where(inside, 1.0, 0.0).astype(jnp.bfloat16))
        weights.append(1.0 / jnp.sqrt(jnp.full((trials, LANES), width, jnp.int32).astype(F32)))
    band = jnp.concatenate(bands, axis=1)
    lane = lane_iota(trials)
    row_count = owners * periods

    def moved(row, by):
        if by == 0:
            return row
        rolled = [pltpu.roll(block, LANES - by, 1) for block in row]
        out = []
        for b in range(bin_blocks + 1):
            after = rolled[min(b + 1, bin_blocks)]
            out.append(jnp.where(lane < LANES - by, rolled[b], after))
        return out

    for group in range(row_count // GROUP):
        rows = []
        for r in range(GROUP):
            at = (1 + group * GROUP + r) * row_len
            rows.append(
                [
                    rows_in[at + b * trials : at + (b + 1) * trials, :]
                    for b in range(bin_blocks + 1)
                ]
            )
        for level in range(LEVELS):
            half = 2**level
            new = []
            for start in range(0, GROUP, 2 * half):
                for j in range(2 * half):
                    upper = rows[start + j // 2]
                    lower = moved(rows[start + half + j // 2], (j + 1) // 2)
                    new.append([u + low for u, low in zip(upper, lower)])
            rows = new
        for r in range(GROUP):
            row = group * GROUP + r
            for b in range(bin_blocks + 1):
                at = (b * GROUP + r) * trials
                folded[at : at + trials, :] = rows[r][b]
                if b < bin_blocks:
                    first = (row // 8 * bin_blocks + b) * 8 + row % 8
                    step = row_count * bin_blocks
                    ffa_ref[pl.ds(first, trials, stride=step), :] = rows[r][b]
        span = GROUP * trials
        for b in range(bin_blocks):
            left = jnp.concatenate(
                [folded[i * span : (i + 1) * span, :] for i in (b, b + 1)], axis=1
            )
            product = None
            for _ in range(3):
                high = left.astype(jnp.bfloat16)
                left = left - high.astype(F32)
                term = jnp.dot(high, band, preferred_element_type=F32)
                product = term if product is None else product + term
            for r in range(GROUP):
                row = group * GROUP + r
                for w in range(widths):
                    value = product[
                        r * trials : (r + 1) * trials, w * LANES : (w + 1) * LANES
                    ]
                    first = (row * bin_blocks + b) * widths + w
                    step = row_count * bin_blocks * widths
                    box_ref[pl.ds(first, trials, stride=step), :] = value * weights[w]


def fold_and_box(mine, parts, box_width, periods, trials, owners):
    bin_blocks = ROW_BLOCKS // owners
    widths = box_width.shape[0]
    row_count = owners * periods
    row_len = (bin_blocks + 1) * trials
    ffa_rows = trials * row_count * bin_blocks
    vmem = pl.BlockSpec(memory_space=pltpu.VMEM)
    ffa, box = pl.pallas_call(
        functools.partial(fold_kernel, periods, trials, owners, widths),
        in_specs=[pl.BlockSpec(memory_space=pltpu.SMEM)] + [vmem] * owners,
        out_specs=[vmem, vmem],
        out_shape=[
            jax.ShapeDtypeStruct((ffa_rows, LANES), F32),
            jax.ShapeDtypeStruct((ffa_rows * widths, LANES), F32),
        ],
        scratch_shapes=[
            pltpu.VMEM(((row_count + 1) * row_len, LANES), F32),
            pltpu.VMEM((max(owners - 1, 1), (periods + 1) * row_len, LANES), F32),
            pltpu.VMEM((GROUP * row_len, LANES), F32),
        ],
        compiler_params=pltpu.CompilerParams(vmem_limit_bytes=VMEM_LIMIT),
        name="fold",
    )(box_width, mine, *parts)
    bins = bin_blocks * LANES
    ffa = ffa.reshape(trials, row_count // 8, bin_blocks, 8, LANES)
    ffa = ffa.transpose(0, 1, 3, 2, 4).reshape(trials, row_count, bins)
    box = box.reshape(trials, row_count, bin_blocks, widths, LANES)
    box = box.transpose(0, 1, 3, 2, 4).reshape(trials, row_count, widths, bins)
    return ffa, box


def per_device(filterbank, chan_delay, sub_delay, box_width):
    chan_size, owners = lax.axis_size("chan"), lax.axis_size("tm")
    samples = filterbank.shape[1]
    subs, trials = NSUB // chan_size, NDM // chan_size
    blocks, periods = samples // LANES, samples // NBIN
    quad = math.gcd(chan_size, 4)
    own = subband_sums(filterbank, chan_delay, subs)
    parts = [own] + [
        lax.ppermute(own, "chan", pairs(chan_size, flip)) for flip in range(1, quad)
    ]
    sizes = (blocks, subs, trials)
    flips = tuple(range(quad, chan_size, quad))
    far = trial_sums(parts, sub_delay, *sizes, flips, True) if flips else []
    far = [
        lax.ppermute(part, "chan", pairs(chan_size, flip))
        for part, flip in zip(far, flips)
    ]
    (near,) = trial_sums(parts, sub_delay, *sizes, (0,), False)
    mine, *sends = cut_by_phase(near, far, blocks, trials, owners)
    got = [
        lax.ppermute(send, "tm", pairs(owners, flip + 1))
        for flip, send in enumerate(sends)
    ]
    return fold_and_box(mine, got, box_width, periods, trials, owners)


def solution(mesh):
    placed = (P("chan", "tm"), P("chan"), P(), P())
    return jax.shard_map(
        per_device,
        mesh=mesh,
        in_specs=placed,
        out_specs=(P("chan", None, "tm"), P("chan", None, None, "tm")),
        check_vma=False,
    )
```

profile of v0, /device:TPU:0, one launch (start us, length us, event | category | flops | bytes accessed | tf_op | source)
XLA Modules:
  0.0 44.8 jit_solution(13635819797368004464)
XLA Ops:
  0.6 0.0 copy-start
  0.6 0.0 copy-start.1
  0.7 0.7 %copy-done.1 = s32[512]{0:T(512)S(1)} copy-done((s32[512]{0:T(512)S(1)}, s32[512]{0:T(512)}, u32[]{:S(2)}) %copy-start.1) | copy-done | bytes 2072
  1.3 9.4 %subbands.1.refs_0_ = s16[528,128]{1,0:T(8,128)(2,1)S(1)} custom-call(s32[512]{0:T(512)S(1)} %copy-done.1, bf16[512,8192]{1,0:T(8,128)(2,1)} %x_ref.1), custom_call_target="tpu_custom_call" | custom-call | tf_op jit(solution)/shard_map/subbands/pallas_call | solution.py:104
  10.8 4.0 %collective-permute-start.2 = (s16[528,128]{1,0:T(8,128)(2,1)S(1)}, s16[528,128]{1,0:T(8,128)(2,1)S(1)}, u32[]{:S(2)}, u32[]{:S(2)}) collective-permute-start(s16[528,128]{1,0:T(8,128)(2,1)S(1)} %subbands.1.refs_0_), channel_id=1, source_target_pairs={{0,12},{4,8},{8,4},{12,0},{16,28},{20,24},{24,20},{28,16},{1,13},{... | collective-permute-start | bytes 405512 | tf_op jit(solution)/shard_map/ppermute | solution.py:388
  14.8 0.4 %collective-permute-start.1 = (s16[528,128]{1,0:T(8,128)(2,1)S(1)}, s16[528,128]{1,0:T(8,128)(2,1)S(1)}, u32[]{:S(2)}, u32[]{:S(2)}) collective-permute-start(s16[528,128]{1,0:T(8,128)(2,1)S(1)} %subbands.1.refs_0_), channel_id=1, source_target_pairs={{0,8},{4,12},{8,0},{12,4},{16,24},{20,28},{24,16},{28,20},{1,9},{5... | collective-permute-start | bytes 405512 | tf_op jit(solution)/shard_map/ppermute | solution.py:388
  15.2 0.2 collective-permute-start
  15.4 3.8 %collective-permute-done.2.refs_3_ = s16[528,128]{1,0:T(8,128)(2,1)S(1)} collective-permute-done((s16[528,128]{1,0:T(8,128)(2,1)S(1)}, s16[528,128]{1,0:T(8,128)(2,1)S(1)}, u32[]{:S(2)}, u32[]{:S(2)}) %collective-permute-start.2) | collective-permute-done | bytes 135200 | tf_op jit(solution)/shard_map/ppermute | solution.py:388
  19.2 2.2 %collective-permute-done.1.refs_2_ = s16[528,128]{1,0:T(8,128)(2,1)S(1)} collective-permute-done((s16[528,128]{1,0:T(8,128)(2,1)S(1)}, s16[528,128]{1,0:T(8,128)(2,1)S(1)}, u32[]{:S(2)}, u32[]{:S(2)}) %collective-permute-start.1) | collective-permute-done | bytes 135200 | tf_op jit(solution)/shard_map/ppermute | solution.py:388
  21.4 0.0 collective-permute-done.refs_1_
  21.4 0.0 copy-done
  21.4 5.6 %trials_coded.1 = s16[584,128]{1,0:T(8,128)(2,1)S(1)} custom-call(s32[64,64]{1,0:T(8,128)S(1)} %copy-done, s16[528,128]{1,0:T(8,128)(2,1)S(1)} %subbands.1.refs_0_, s16[528,128]{1,0:T(8,128)(2,1)S(1)} %collective-permute-done.refs_1_, s16[528,128]{1,0:T(8,128)(2,1)S(1)} %collective-permute-done.1.refs_2_, s16[528,128]{1,0:T(8,128)(2,1)S(1)} %collective-permute-done.2.refs_3_), custom_call_target="tpu_custom_call" | custom-call | tf_op jit(solution)/shard_map/trials_coded/pallas_call | solution.py:178
  27.1 2.7 %collective-permute-start.3 = (s16[584,128]{1,0:T(8,128)(2,1)S(1)}, s16[584,128]{1,0:T(8,128)(2,1)S(1)}, u32[]{:S(2)}, u32[]{:S(2)}) collective-permute-start(s16[584,128]{1,0:T(8,128)(2,1)S(1)} %trials_coded.1), channel_id=1, source_target_pairs={{0,16},{4,20},{8,24},{12,28},{16,0},{20,4},{24,8},{28,12},{1,17},{... | collective-permute-start | bytes 448520 | tf_op jit(solution)/shard_map/ppermute | solution.py:394
  29.7 5.5 %trials.1.own_ref = f32[576,128]{1,0:T(8,128)S(1)} custom-call(s32[64,64]{1,0:T(8,128)S(1)} %copy-done, s16[528,128]{1,0:T(8,128)(2,1)S(1)} %subbands.1.refs_0_, s16[528,128]{1,0:T(8,128)(2,1)S(1)} %collective-permute-done.refs_1_, s16[528,128]{1,0:T(8,128)(2,1)S(1)} %collective-permute-done.1.refs_2_, s16[528,128]{1,0:T(8,128)(2,1)S(1)} %collective-permute-done.2.refs_3_), custom_call_target="tpu_custom_call" | custom-call | tf_op jit(solution)/shard_map/trials/pallas_call | solution.py:178
  35.2 1.1 %collective-permute-done.3.refs_0_ = s16[584,128]{1,0:T(8,128)(2,1)S(1)} collective-permute-done((s16[584,128]{1,0:T(8,128)(2,1)S(1)}, s16[584,128]{1,0:T(8,128)(2,1)S(1)}, u32[]{:S(2)}, u32[]{:S(2)}) %collective-permute-start.3) | collective-permute-done | bytes 149536 | tf_op jit(solution)/shard_map/ppermute | solution.py:394
  36.3 0.2 cut.1
  36.5 0.1 collective-permute-start.4
  36.5 1.6 %collective-permute-start.5 = (s16[208,128]{1,0:T(8,128)(2,1)S(1)}, s16[208,128]{1,0:T(8,128)(2,1)S(1)}, u32[]{:S(2)}, u32[]{:S(2)}) collective-permute-start(s16[208,128]{1,0:T(8,128)(2,1)S(1)} %get-tuple-element.10), channel_id=1, source_target_pairs={{0,2},{1,3},{2,0},{3,1},{4,6},{5,7},{6,4},{7,5},{8,10},{9,11},{10,... | collective-permute-start | bytes 159752 | tf_op jit(solution)/shard_map/ppermute | solution.py:400
  38.1 0.3 collective-permute-start.6
  38.4 0.0 collective-permute-done.4.refs_0_
  38.4 2.4 %collective-permute-done.5.refs_1_ = s16[208,128]{1,0:T(8,128)(2,1)S(1)} collective-permute-done((s16[208,128]{1,0:T(8,128)(2,1)S(1)}, s16[208,128]{1,0:T(8,128)(2,1)S(1)}, u32[]{:S(2)}, u32[]{:S(2)}) %collective-permute-start.5) | collective-permute-done | bytes 53280 | tf_op jit(solution)/shard_map/ppermute | solution.py:400
  40.8 1.1 %collective-permute-done.6.refs_2_ = s16[208,128]{1,0:T(8,128)(2,1)S(1)} collective-permute-done((s16[208,128]{1,0:T(8,128)(2,1)S(1)}, s16[208,128]{1,0:T(8,128)(2,1)S(1)}, u32[]{:S(2)}, u32[]{:S(2)}) %collective-permute-start.6) | collective-permute-done | bytes 53280 | tf_op jit(solution)/shard_map/ppermute | solution.py:400
  41.9 0.0 copy-done.2
  41.9 2.9 %fold.1 = (f32[512,128]{1,0:T(8,128)}, f32[2048,128]{1,0:T(8,128)}) custom-call(s32[4]{0:T(128)S(1)} %copy-done.2, f32[200,128]{1,0:T(8,128)S(1)} %get-tuple-element.8.mine_ref, s16[208,128]{1,0:T(8,128)(2,1)S(1)} %collective-permute-done.4.refs_0_, s16[208,128]{1,0:T(8,128)(2,1)S(1)} %collective-permute-done.5.refs_1_, ...), custom_call_target="tpu_custom_call" | custom-call | tf_op jit(solution)/shard_map/fold/pallas_call | solution.py:356
  (1 shorter events, 0.0 us)
Async XLA Ops:
  0.6 20.8 %copy-start = (s32[64,64]{1,0:T(8,128)S(1)}, s32[64,64]{1,0:T(8,128)}, u32[]{:S(2)}) copy-start(s32[64,64]{1,0:T(8,128)} %delay_ref.5) | copy-start | bytes 49156
  0.6 0.7 %copy-start.1 = (s32[512]{0:T(512)S(1)}, s32[512]{0:T(512)}, u32[]{:S(2)}) copy-start(s32[512]{0:T(512)} %delay_ref.3) | copy-start | bytes 6148
  1.3 40.6 %copy-start.2 = (s32[4]{0:T(128)S(1)}, s32[4]{0:T(128)}, u32[]{:S(2)}) copy-start(s32[4]{0:T(128)} %width_ref.1) | copy-start | bytes 52
  10.8 8.5 %collective-permute-start.2 = (s16[528,128]{1,0:T(8,128)(2,1)S(1)}, s16[528,128]{1,0:T(8,128)(2,1)S(1)}, u32[]{:S(2)}, u32[]{:S(2)}) collective-permute-start(s16[528,128]{1,0:T(8,128)(2,1)S(1)} %subbands.1.refs_0_), channel_id=1, source_target_pairs={{0,12},{4,8},{8,4},{12,0},{16,28},{20,24},{24,20},{28,16},{1,13},{... | collective-permute-start | bytes 405512 | tf_op jit(solution)/shard_map/ppermute | solution.py:388
  14.8 6.6 %collective-permute-start.1 = (s16[528,128]{1,0:T(8,128)(2,1)S(1)}, s16[528,128]{1,0:T(8,128)(2,1)S(1)}, u32[]{:S(2)}, u32[]{:S(2)}) collective-permute-start(s16[528,128]{1,0:T(8,128)(2,1)S(1)} %subbands.1.refs_0_), channel_id=1, source_target_pairs={{0,8},{4,12},{8,0},{12,4},{16,24},{20,28},{24,16},{28,20},{1,9},{5... | collective-permute-start | bytes 405512 | tf_op jit(solution)/shard_map/ppermute | solution.py:388
  15.2 6.2 %collective-permute-start = (s16[528,128]{1,0:T(8,128)(2,1)S(1)}, s16[528,128]{1,0:T(8,128)(2,1)S(1)}, u32[]{:S(2)}, u32[]{:S(2)}) collective-permute-start(s16[528,128]{1,0:T(8,128)(2,1)S(1)} %subbands.1.refs_0_), channel_id=1, source_target_pairs={{0,4},{4,0},{8,12},{12,8},{16,20},{20,16},{24,28},{28,24},{1,5},{5... | collective-permute-start | bytes 405512 | tf_op jit(solution)/shard_map/ppermute | solution.py:388
  27.1 9.2 %collective-permute-start.3 = (s16[584,128]{1,0:T(8,128)(2,1)S(1)}, s16[584,128]{1,0:T(8,128)(2,1)S(1)}, u32[]{:S(2)}, u32[]{:S(2)}) collective-permute-start(s16[584,128]{1,0:T(8,128)(2,1)S(1)} %trials_coded.1), channel_id=1, source_target_pairs={{0,16},{4,20},{8,24},{12,28},{16,0},{20,4},{24,8},{28,12},{1,17},{... | collective-permute-start | bytes 448520 | tf_op jit(solution)/shard_map/ppermute | solution.py:394
  36.5 1.9 %collective-permute-start.4 = (s16[208,128]{1,0:T(8,128)(2,1)S(1)}, s16[208,128]{1,0:T(8,128)(2,1)S(1)}, u32[]{:S(2)}, u32[]{:S(2)}) collective-permute-start(s16[208,128]{1,0:T(8,128)(2,1)S(1)} %get-tuple-element.9), channel_id=1, source_target_pairs={{0,1},{1,0},{2,3},{3,2},{4,5},{5,4},{6,7},{7,6},{8,9},{9,8},{10,11... | collective-permute-start | bytes 159752 | tf_op jit(solution)/shard_map/ppermute | solution.py:400
  36.5 4.2 %collective-permute-start.5 = (s16[208,128]{1,0:T(8,128)(2,1)S(1)}, s16[208,128]{1,0:T(8,128)(2,1)S(1)}, u32[]{:S(2)}, u32[]{:S(2)}) collective-permute-start(s16[208,128]{1,0:T(8,128)(2,1)S(1)} %get-tuple-element.10), channel_id=1, source_target_pairs={{0,2},{1,3},{2,0},{3,1},{4,6},{5,7},{6,4},{7,5},{8,10},{9,11},{10,... | collective-permute-start | bytes 159752 | tf_op jit(solution)/shard_map/ppermute | solution.py:400
  38.1 3.8 %collective-permute-start.6 = (s16[208,128]{1,0:T(8,128)(2,1)S(1)}, s16[208,128]{1,0:T(8,128)(2,1)S(1)}, u32[]{:S(2)}, u32[]{:S(2)}) collective-permute-start(s16[208,128]{1,0:T(8,128)(2,1)S(1)} %get-tuple-element.11), channel_id=1, source_target_pairs={{0,3},{1,2},{2,1},{3,0},{4,7},{5,6},{6,5},{7,4},{8,11},{9,10},{10,... | collective-permute-start | bytes 159752 | tf_op jit(solution)/shard_map/ppermute | solution.py:400
where the time goes:
time: 45.2 us; the launch traced here: 44.8 us
  Pallas kernels  23.7 us (52%)
  waiting for transfers between devices  10.5 us (23%)
  starting transfers between devices  9.27 us (21%)
  local copies, waits for them, and re-layouts  0.69 us (2%)
  between operations  0.69 us (2%)
    pallas_call x2, Pallas kernels, trial_sums(): pl.pallas_call(functools.partial(trial_kernel, blocks, subs, trials, flip...  11.1 us
    pallas_call x1, Pallas kernels, subband_sums(): pl.pallas_call(functools.partial(subband_kernel, chans, blocks, subs), gr...  9.41 us
    ppermute x3, waiting for transfers between devices, per_device(): lax.ppermute(own, 'chan', pairs(chan_size, flip))  6 us
    ppermute x3, starting transfers between devices, per_device(): lax.ppermute(own, 'chan', pairs(chan_size, flip))  4.69 us
    ppermute x3, waiting for transfers between devices, per_device(): lax.ppermute(send, 'tm', pairs(owners, flip + 1))  3.48 us
    pallas_call x1, Pallas kernels, fold_and_box(): pl.pallas_call(functools.partial(fold_kernel, periods, trials, owners, wi...  2.94 us
    ppermute x1, starting transfers between devices, per_device(): lax.ppermute(part, 'chan', pairs(chan_size, flip))  2.65 us
    ppermute x3, starting transfers between devices, per_device(): lax.ppermute(send, 'tm', pairs(owners, flip + 1))  1.93 us
  transfers between devices with their start and end apart: 7, of which 5 were waited for; matrix products, arithmetic and copies ran while one was open for 0% of the time, Pallas kernels for 12%

commit v1 on v0

--- a/solution.py
+++ b/solution.py
@@ -46,55 +46,62 @@
     return [(i, i ^ flip) for i in range(size)]
 
 
-def subband_kernel(chans, blocks, subs, delay_ref, x_ref, out_ref, sums):
-    sub = pl.program_id(0)
+def subband_kernel(chans, blocks, subs, delay_hbm, x_hbm, out_ref, *scratch):
+    delay_ref, x_ref, turned, late, sums, x_sem, delay_sem = scratch
+    delay_copy = pltpu.make_async_copy(delay_hbm, delay_ref, delay_sem)
+    delay_copy.start()
+
+    def x_copy(sub):
+        return pltpu.make_async_copy(
+            x_hbm.at[pl.ds(sub * chans, chans), :], x_ref.at[sub], x_sem.at[sub]
+        )
+
+    for sub in range(subs):
+        x_copy(sub).start()
+    delay_copy.wait()
     lane = lane_iota(8)
-    row = lax.broadcasted_iota(jnp.int32, (8, LANES), 0)
-    tiles = chans // 8
-    where_from, from_next = [], []
-    for tile in range(tiles):
-        delay = jnp.zeros((8, LANES), jnp.int32)
-        for i in range(8):
-            delay = jnp.where(row == i, delay_ref[sub * chans + tile * 8 + i], delay)
-        where_from.append((lane + delay) & (LANES - 1))
-        from_next.append(lane < delay)
-
-    def load(block):
-        loaded = []
-        for pair in range(tiles // 2):
-            both = x_ref[16 * pair : 16 * pair + 16, block * LANES : (block + 1) * LANES]
-            both = both.astype(F32)
-            loaded += [both[:8], both[8:]]
-        return loaded
-
-    def emit(block, here, after):
-        terms = []
-        for tile in range(tiles):
-            mixed = jnp.where(from_next[tile], after[tile], here[tile])
-            terms.append(
-                jnp.take_along_axis(
-                    mixed, where_from[tile], axis=1, mode="promise_in_bounds"
-                )
+    tiles = blocks // 8
+
+    @pl.loop(0, subs)
+    def _(sub):
+        x_copy(sub).wait()
+        here = [jnp.zeros((8, LANES), F32)] * tiles
+        before = [jnp.zeros((8, LANES), F32)] * tiles
+        for octet in range(chans // 8):
+            if octet % 2 == 0:
+                for block in range(blocks):
+                    both = x_ref[
+                        sub,
+                        8 * octet : 8 * octet + 16,
+                        block * LANES : (block + 1) * LANES,
+                    ].astype(F32)
+                    for k in range(2):
+                        at = ((octet + k) * blocks + block) * 8
+                        turned[at : at + 8, :] = both[8 * k : 8 * k + 8]
+            for i in range(8):
+                delay = delay_ref[sub * chans + octet * 8 + i]
+                shift = (2 * LANES - delay) & (LANES - 1)
+                stays = lane < LANES - delay
+                for t in range(tiles):
+                    first = (octet * blocks + t * 8) * 8 + i
+                    value = turned[pl.ds(first, 8, stride=8), :]
+                    value = pltpu.roll(value, shift, 1)
+                    here[t] = here[t] + jnp.where(stays, value, 0.0)
+                    before[t] = before[t] + jnp.where(stays, 0.0, value)
+        for t in range(tiles):
+            late[8 * t : 8 * t + 8, :] = before[t]
+        late[blocks : blocks + 8, :] = jnp.zeros((8, LANES), F32)
+        sums[pl.ds(sub, 1), :] = late[0:1, :]
+        for t in range(tiles):
+            sums[pl.ds((8 * t + 1) * subs + sub, 8, stride=subs), :] = (
+                here[t] + late[8 * t + 1 : 8 * t + 9, :]
             )
-        while len(terms) > 1:
-            terms = [a + b for a, b in zip(terms[::2], terms[1::2])]
-        total = jnp.sum(terms[0], axis=0, keepdims=True)
-        sums[pl.ds((block + 1) * subs + sub, 1), :] = total
-
-    zero = [jnp.zeros((8, LANES), F32)] * tiles
-    here = zero
-    for block in range(-1, blocks):
-        after = load(block + 1) if block + 1 < blocks else zero
-        emit(block, here, after)
-        here = after
-
-    @pl.when(sub == subs - 1)
-    def _():
-        rows = (blocks + 1) * subs
-        values = sums[...].reshape(blocks + 1, subs, LANES)
-        exponent = column_exponent(jnp.max(jnp.abs(values), axis=0))
-        out_ref[0:rows, :] = to_i16(scaled(values, exponent[None]).reshape(rows, LANES))
-        out_ref[rows : rows + subs, :] = to_i16(exponent)
+
+    rows = (blocks + 1) * subs
+    values = sums[...].reshape(blocks + 1, subs, LANES)
+    exponent = column_exponent(jnp.max(jnp.abs(values), axis=0))
+    out_ref[0:rows, :] = to_i16(scaled(values, exponent[None]).reshape(rows, LANES))
+    out_ref[rows : rows + subs, :] = to_i16(exponent)
 
 
 def subband_sums(filterbank, chan_delay, subs):
@@ -103,25 +110,33 @@
     rows = (blocks + 2) * subs
     return pl.pallas_call(
         functools.partial(subband_kernel, chans, blocks, subs),
-        grid=(subs,),
-        in_specs=[
-            pl.BlockSpec(memory_space=pltpu.SMEM),
-            pl.BlockSpec((chans, samples), lambda i: (i, 0)),
+        in_specs=[pl.BlockSpec(memory_space=pltpu.HBM)] * 2,
+        out_specs=pl.BlockSpec(memory_space=pltpu.VMEM),
+        out_shape=jax.ShapeDtypeStruct((rows, LANES), jnp.int16),
+        scratch_shapes=[
+            pltpu.SMEM((chans_here,), jnp.int32),
+            pltpu.VMEM((subs, chans, samples), filterbank.dtype),
+            pltpu.VMEM((chans * blocks, LANES), F32),
+            pltpu.VMEM((blocks + 8, LANES), F32),
+            pltpu.VMEM(((blocks + 1) * subs, LANES), F32),
+            pltpu.SemaphoreType.DMA((subs,)),
+            pltpu.SemaphoreType.DMA(()),
         ],
-        out_specs=pl.BlockSpec((rows, LANES), lambda i: (0, 0)),
-        out_shape=jax.ShapeDtypeStruct((rows, LANES), jnp.int16),
-        scratch_shapes=[pltpu.VMEM(((blocks + 1) * subs, LANES), F32)],
         compiler_params=pltpu.CompilerParams(vmem_limit_bytes=VMEM_LIMIT),
         name="subbands",
     )(chan_delay, filterbank)
 
 
-def trial_kernel(blocks, subs, trials, flips, coded, n_in, delay_ref, *refs):
-    parts, outs = refs[:n_in], refs[n_in : n_in + len(flips)]
-    spread, acc = refs[n_in + len(flips) :]
+def trial_kernel(blocks, subs, trials, origins, flips, primed, coded, delay_ref, *refs):
+    refs = list(refs)
+    take = lambda n: [refs.pop(0) for _ in range(n)]
+    parts = take(len(origins))
+    priors = take(len(flips)) if primed else []
+    outs = take(len(flips))
+    spread, late, acc = refs
     chan = lax.axis_index("chan")
     out_blocks = LEAD + blocks
-    depth = out_blocks + LEAD + 1
+    depth = out_blocks + LEAD
     for at, part in enumerate(parts):
         base = at * depth * subs
         rows = (blocks + 1) * subs
@@ -135,28 +150,39 @@
         values = part[0:rows, :].astype(F32).reshape(blocks + 1, subs, LANES)
         spread[base + lead : tail, :] = (values * scale[None]).reshape(rows, LANES)
 
-    lane = lane_iota(out_blocks)
-
-    def one_trial(trial, owner, out):
-        total = jnp.zeros((out_blocks, LANES), F32)
-        for at in range(n_in):
+    lane = lane_iota(8)
+    tiles = out_blocks // 8
+
+    def one_trial(trial, owner, prior, out):
+        here = [jnp.zeros((8, LANES), F32)] * tiles
+        before = [jnp.zeros((8, LANES), F32)] * tiles
+        for at, origin in enumerate(origins):
             for sub in range(subs):
-                delay = delay_ref[owner * trials + trial, (chan ^ at) * subs + sub]
+                delay = delay_ref[owner * trials + trial, (chan ^ origin) * subs + sub]
                 shift = delay & (LANES - 1)
-                first = at * depth * subs + (delay >> 7) * subs + sub
-                here = spread[pl.ds(first, out_blocks, stride=subs), :]
-                after = spread[pl.ds(first + subs, out_blocks, stride=subs), :]
-                mixed = jnp.where(lane < shift, after, here)
-                total = total + pltpu.roll(mixed, (LANES - shift) & (LANES - 1), 1)
-        out[pl.ds(trial, out_blocks, stride=trials), :] = total
+                stays = lane < LANES - shift
+                back = (LANES - shift) & (LANES - 1)
+                for t in range(tiles):
+                    first = (at * depth + (delay >> 7) + 8 * t) * subs + sub
+                    value = spread[pl.ds(first, 8, stride=subs), :]
+                    value = pltpu.roll(value, back, 1)
+                    here[t] = here[t] + jnp.where(stays, value, 0.0)
+                    before[t] = before[t] + jnp.where(stays, 0.0, value)
+        for t in range(tiles):
+            late[8 * t : 8 * t + 8, :] = before[t]
+        late[out_blocks : out_blocks + 8, :] = jnp.zeros((8, LANES), F32)
+        for t in range(tiles):
+            rows = pl.ds(8 * t * trials + trial, 8, stride=trials)
+            value = here[t] + late[8 * t + 1 : 8 * t + 9, :]
+            out[rows, :] = value if prior is None else value + prior[rows, :]
 
     rows = out_blocks * trials
-    for flip, out in zip(flips, outs):
+    for i, (flip, out) in enumerate(zip(flips, outs)):
         target = acc if coded else out
 
         @pl.loop(0, trials)
         def _(trial):
-            one_trial(trial, chan ^ flip, target)
+            one_trial(trial, chan ^ flip, priors[i] if primed else None, target)
 
         if coded:
             values = acc[...].reshape(out_blocks, trials, LANES)
@@ -167,28 +193,33 @@
             out[rows : rows + trials, :] = to_i16(exponent)
 
 
-def trial_sums(parts, sub_delay, blocks, subs, trials, flips, coded):
+def trial_sums(parts, origins, sub_delay, sizes, flips, priors=None, coded=False):
+    if not flips:
+        return []
+    blocks, subs, trials = sizes
     out_blocks = LEAD + blocks
-    depth = out_blocks + LEAD + 1
+    depth = out_blocks + LEAD
     rows = out_blocks * trials
     out = jax.ShapeDtypeStruct(
         (rows + trials if coded else rows, LANES), jnp.int16 if coded else F32
     )
     vmem = pl.BlockSpec(memory_space=pltpu.VMEM)
+    arrays = [*parts, *(priors or [])]
     return pl.pallas_call(
         functools.partial(
-            trial_kernel, blocks, subs, trials, flips, coded, len(parts)
+            trial_kernel, *sizes, tuple(origins), tuple(flips), bool(priors), coded
         ),
-        in_specs=[pl.BlockSpec(memory_space=pltpu.SMEM)] + [vmem] * len(parts),
+        in_specs=[pl.BlockSpec(memory_space=pltpu.SMEM)] + [vmem] * len(arrays),
         out_specs=[vmem] * len(flips),
         out_shape=[out] * len(flips),
         scratch_shapes=[
             pltpu.VMEM((len(parts) * depth * subs, LANES), F32),
+            pltpu.VMEM((out_blocks + 8, LANES), F32),
             pltpu.VMEM((rows, LANES), F32),
         ],
         compiler_params=pltpu.CompilerParams(vmem_limit_bytes=VMEM_LIMIT),
         name="trials_coded" if coded else "trials",
-    )(sub_delay, *parts)
+    )(sub_delay, *arrays)
 
 
 def cut_kernel(blocks, trials, owners, n_far, own_ref, *refs):
@@ -384,17 +415,23 @@
     blocks, periods = samples // LANES, samples // NBIN
     quad = math.gcd(chan_size, 4)
     own = subband_sums(filterbank, chan_delay, subs)
-    parts = [own] + [
-        lax.ppermute(own, "chan", pairs(chan_size, flip)) for flip in range(1, quad)
-    ]
+    part = {0: own}
+    for flip in range(1, quad):
+        part[flip] = lax.ppermute(own, "chan", pairs(chan_size, flip))
     sizes = (blocks, subs, trials)
     flips = tuple(range(quad, chan_size, quad))
-    far = trial_sums(parts, sub_delay, *sizes, flips, True) if flips else []
+    sums = trial_sums([own], (0,), sub_delay, sizes, (*flips, 0))
+    rest = tuple(range(1, quad))
+    if quad == 4:
+        sums = trial_sums([part[2]], (2,), sub_delay, sizes, (*flips, 0), sums)
+        rest = (1, 3)
+    last = [part[flip] for flip in rest]
+    far = trial_sums(last, rest, sub_delay, sizes, flips, sums[:-1], True)
     far = [
-        lax.ppermute(part, "chan", pairs(chan_size, flip))
-        for part, flip in zip(far, flips)
+        lax.ppermute(send, "chan", pairs(chan_size, flip))
+        for send, flip in zip(far, flips)
     ]
-    (near,) = trial_sums(parts, sub_delay, *sizes, (0,), False)
+    (near,) = trial_sums(last, rest, sub_delay, sizes, (0,), sums[-1:])
     mine, *sends = cut_by_phase(near, far, blocks, trials, owners)
     got = [
         lax.ppermute(send, "tm", pairs(owners, flip + 1))

time: 45.2 us -> 41.1 us (0.909)
  waiting for transfers between devices: 10.5 us -> 6.77 us
  Pallas kernels: 23.7 us -> 23.1 us
    ppermute x4, waiting for transfers between devices: 7.05 us -> 3.24 us  [the longest x1 3.24 us: per_device(): lax.ppermute(send, 'chan', pairs(chan_size, flip))]
    pallas_call x3 -> x5, Pallas kernels: 20.5 us -> 20 us  [the longest x4 13.4 us: trial_sums(): pl.pallas_call(functools.partial(trial_kernel, *sizes, tuple(origins), tu...]
  transfers between devices with their start and end apart: 7 -> 7, of which waited for: 5 -> 3; matrix products, arithmetic and copies ran while one was open for 0% -> 0% of each run, Pallas kernels for 12% -> 25%
where the time goes in v1:
time: 41.1 us; the launch traced here: 40.9 us
  Pallas kernels  23.1 us (56%)
  starting transfers between devices  9.59 us (23%)
  waiting for transfers between devices  6.77 us (16%)
  between operations  0.72 us (2%)
  local copies, waits for them, and re-layouts  0.69 us (2%)
    pallas_call x4, Pallas kernels, trial_sums(): pl.pallas_call(functools.partial(trial_kernel, *sizes, tuple(origins), tu...  13.4 us
    pallas_call x1, Pallas kernels, subband_sums(): pl.pallas_call(functools.partial(subband_kernel, chans, blocks, subs), in...  6.54 us
    ppermute x3, starting transfers between devices, per_device(): part[flip] = lax.ppermute(own, 'chan', pairs(chan_size, flip))  4.63 us
    ppermute x3, waiting for transfers between devices, per_device(): lax.ppermute(send, 'tm', pairs(owners, flip + 1))  3.53 us
    ppermute x1, waiting for transfers between devices, per_device(): lax.ppermute(send, 'chan', pairs(chan_size, flip))  3.24 us
    ppermute x1, starting transfers between devices, per_device(): lax.ppermute(send, 'chan', pairs(chan_size, flip))  3.03 us
    pallas_call x1, Pallas kernels, fold_and_box(): pl.pallas_call(functools.partial(fold_kernel, periods, trials, owners, wi...  2.94 us
    ppermute x3, starting transfers between devices, per_device(): lax.ppermute(send, 'tm', pairs(owners, flip + 1))  1.93 us
  transfers between devices with their start and end apart: 7, of which 3 were waited for; matrix products, arithmetic and copies ran while one was open for 0% of the time, Pallas kernels for 25%

profile of v1, /device:TPU:0, one launch (start us, length us, event | category | flops | bytes accessed | tf_op | source)
XLA Modules:
  0.0 40.9 jit_solution(9406713568468940491)
XLA Ops:
  0.6 0.0 copy-start
  0.6 0.0 copy-start.1
  0.7 0.7 %copy-done.1 = s32[512]{0:T(512)S(1)} copy-done((s32[512]{0:T(512)S(1)}, s32[512]{0:T(512)}, u32[]{:S(2)}) %copy-start.1) | copy-done | bytes 2072
  1.3 6.5 %subbands.1.refs_0_ = s16[528,128]{1,0:T(8,128)(2,1)S(1)} custom-call(s32[512]{0:T(512)S(1)} %copy-done.1, bf16[512,8192]{1,0:T(8,128)(2,1)} %x_hbm.1), custom_call_target="tpu_custom_call" | custom-call | tf_op jit(solution)/shard_map/subbands/pallas_call | solution.py:111
  7.9 3.1 %collective-permute-start.2 = (s16[528,128]{1,0:T(8,128)(2,1)S(1)}, s16[528,128]{1,0:T(8,128)(2,1)S(1)}, u32[]{:S(2)}, u32[]{:S(2)}) collective-permute-start(s16[528,128]{1,0:T(8,128)(2,1)S(1)} %subbands.1.refs_0_), channel_id=1, source_target_pairs={{0,8},{4,12},{8,0},{12,4},{16,24},{20,28},{24,16},{28,20},{1,9},{5... | collective-permute-start | bytes 405512 | tf_op jit(solution)/shard_map/ppermute | solution.py:420
  11.0 1.5 %collective-permute-start = (s16[528,128]{1,0:T(8,128)(2,1)S(1)}, s16[528,128]{1,0:T(8,128)(2,1)S(1)}, u32[]{:S(2)}, u32[]{:S(2)}) collective-permute-start(s16[528,128]{1,0:T(8,128)(2,1)S(1)} %subbands.1.refs_0_), channel_id=1, source_target_pairs={{0,4},{4,0},{8,12},{12,8},{16,20},{20,16},{24,28},{28,24},{1,5},{5... | collective-permute-start | bytes 405512 | tf_op jit(solution)/shard_map/ppermute | solution.py:420
  12.5 0.0 collective-permute-start.1
  12.5 3.7 %trials.3 = (f32[576,128]{1,0:T(8,128)S(1)}, f32[576,128]{1,0:T(8,128)S(1)}) custom-call(s32[64,64]{1,0:T(8,128)S(1)} %copy-done, s16[528,128]{1,0:T(8,128)(2,1)S(1)} %subbands.1.refs_0_), custom_call_target="tpu_custom_call" | custom-call | tf_op jit(solution)/shard_map/trials/pallas_call | solution.py:208
  16.2 0.0 collective-permute-done.2.refs_0_
  16.2 3.7 %trials.4 = (f32[576,128]{1,0:T(8,128)S(1)}, f32[576,128]{1,0:T(8,128)S(1)}) custom-call(s32[64,64]{1,0:T(8,128)S(1)} %copy-done, s16[528,128]{1,0:T(8,128)(2,1)S(1)} %collective-permute-done.2.refs_0_, f32[576,128]{1,0:T(8,128)S(1)} %get-tuple-element.12.refs_1_, f32[576,128]{1,0:T(8,128)S(1)} %get-tuple-element.13.refs_2_), custom_call_target="tpu_custom_call" | custom-call | tf_op jit(solution)/shard_map/trials/pallas_call | solution.py:208
  19.8 0.0 collective-permute-done.refs_0_
  19.9 0.0 collective-permute-done.1.refs_1_
  19.9 3.1 %trials_coded.1 = s16[584,128]{1,0:T(8,128)(2,1)S(1)} custom-call(s32[64,64]{1,0:T(8,128)S(1)} %copy-done, s16[528,128]{1,0:T(8,128)(2,1)S(1)} %collective-permute-done.refs_0_, s16[528,128]{1,0:T(8,128)(2,1)S(1)} %collective-permute-done.1.refs_1_, f32[576,128]{1,0:T(8,128)S(1)} %get-tuple-element.15.refs_2_), custom_call_target="tpu_custom_call" | custom-call | tf_op jit(solution)/shard_map/trials_coded/pallas_call | solution.py:208
  23.0 3.0 %collective-permute-start.3 = (s16[584,128]{1,0:T(8,128)(2,1)S(1)}, s16[584,128]{1,0:T(8,128)(2,1)S(1)}, u32[]{:S(2)}, u32[]{:S(2)}) collective-permute-start(s16[584,128]{1,0:T(8,128)(2,1)S(1)} %trials_coded.1), channel_id=1, source_target_pairs={{0,16},{4,20},{8,24},{12,28},{16,0},{20,4},{24,8},{28,12},{1,17},{... | collective-permute-start | bytes 448520 | tf_op jit(solution)/shard_map/ppermute | solution.py:431
  26.0 3.0 %trials.5.own_ref = f32[576,128]{1,0:T(8,128)S(1)} custom-call(s32[64,64]{1,0:T(8,128)S(1)} %copy-done, s16[528,128]{1,0:T(8,128)(2,1)S(1)} %collective-permute-done.refs_0_, s16[528,128]{1,0:T(8,128)(2,1)S(1)} %collective-permute-done.1.refs_1_, f32[576,128]{1,0:T(8,128)S(1)} %get-tuple-element.14.refs_2_), custom_call_target="tpu_custom_call" | custom-call | tf_op jit(solution)/shard_map/trials/pallas_call | solution.py:208
  29.0 3.2 %collective-permute-done.3.refs_0_ = s16[584,128]{1,0:T(8,128)(2,1)S(1)} collective-permute-done((s16[584,128]{1,0:T(8,128)(2,1)S(1)}, s16[584,128]{1,0:T(8,128)(2,1)S(1)}, u32[]{:S(2)}, u32[]{:S(2)}) %collective-permute-start.3) | collective-permute-done | bytes 149536 | tf_op jit(solution)/shard_map/ppermute | solution.py:431
  32.3 0.2 cut.1
  32.5 0.1 collective-permute-start.4
  32.5 1.6 %collective-permute-start.5 = (s16[208,128]{1,0:T(8,128)(2,1)S(1)}, s16[208,128]{1,0:T(8,128)(2,1)S(1)}, u32[]{:S(2)}, u32[]{:S(2)}) collective-permute-start(s16[208,128]{1,0:T(8,128)(2,1)S(1)} %get-tuple-element.18), channel_id=1, source_target_pairs={{0,2},{1,3},{2,0},{3,1},{4,6},{5,7},{6,4},{7,5},{8,10},{9,11},{10,... | collective-permute-start | bytes 159752 | tf_op jit(solution)/shard_map/ppermute | solution.py:437
  34.1 0.3 collective-permute-start.6
  34.4 0.0 collective-permute-done.4.refs_0_
  34.4 2.4 %collective-permute-done.5.refs_1_ = s16[208,128]{1,0:T(8,128)(2,1)S(1)} collective-permute-done((s16[208,128]{1,0:T(8,128)(2,1)S(1)}, s16[208,128]{1,0:T(8,128)(2,1)S(1)}, u32[]{:S(2)}, u32[]{:S(2)}) %collective-permute-start.5) | collective-permute-done | bytes 53280 | tf_op jit(solution)/shard_map/ppermute | solution.py:437
  36.8 1.1 %collective-permute-done.6.refs_2_ = s16[208,128]{1,0:T(8,128)(2,1)S(1)} collective-permute-done((s16[208,128]{1,0:T(8,128)(2,1)S(1)}, s16[208,128]{1,0:T(8,128)(2,1)S(1)}, u32[]{:S(2)}, u32[]{:S(2)}) %collective-permute-start.6) | collective-permute-done | bytes 53280 | tf_op jit(solution)/shard_map/ppermute | solution.py:437
  37.9 2.9 %fold.1 = (f32[512,128]{1,0:T(8,128)}, f32[2048,128]{1,0:T(8,128)}) custom-call(s32[4]{0:T(128)S(1)} %copy-done.2, f32[200,128]{1,0:T(8,128)S(1)} %get-tuple-element.16.mine_ref, s16[208,128]{1,0:T(8,128)(2,1)S(1)} %collective-permute-done.4.refs_0_, s16[208,128]{1,0:T(8,128)(2,1)S(1)} %collective-permute-done.5.refs_1_, ...), custom_call_target="tpu_custom_call" | custom-call | tf_op jit(solution)/shard_map/fold/pallas_call | solution.py:387
  (3 shorter events, 0.0 us)
Async XLA Ops:
  0.6 11.9 %copy-start = (s32[64,64]{1,0:T(8,128)S(1)}, s32[64,64]{1,0:T(8,128)}, u32[]{:S(2)}) copy-start(s32[64,64]{1,0:T(8,128)} %delay_ref.7) | copy-start | bytes 49156
  0.6 0.7 %copy-start.1 = (s32[512]{0:T(512)S(1)}, s32[512]{0:T(512)}, u32[]{:S(2)}) copy-start(s32[512]{0:T(512)} %delay_hbm.1) | copy-start | bytes 6148
  1.3 36.6 %copy-start.2 = (s32[4]{0:T(128)S(1)}, s32[4]{0:T(128)}, u32[]{:S(2)}) copy-start(s32[4]{0:T(128)} %width_ref.1) | copy-start | bytes 52
  7.9 8.3 %collective-permute-start.2 = (s16[528,128]{1,0:T(8,128)(2,1)S(1)}, s16[528,128]{1,0:T(8,128)(2,1)S(1)}, u32[]{:S(2)}, u32[]{:S(2)}) collective-permute-start(s16[528,128]{1,0:T(8,128)(2,1)S(1)} %subbands.1.refs_0_), channel_id=1, source_target_pairs={{0,8},{4,12},{8,0},{12,4},{16,24},{20,28},{24,16},{28,20},{1,9},{5... | collective-permute-start | bytes 405512 | tf_op jit(solution)/shard_map/ppermute | solution.py:420
  11.0 8.9 %collective-permute-start = (s16[528,128]{1,0:T(8,128)(2,1)S(1)}, s16[528,128]{1,0:T(8,128)(2,1)S(1)}, u32[]{:S(2)}, u32[]{:S(2)}) collective-permute-start(s16[528,128]{1,0:T(8,128)(2,1)S(1)} %subbands.1.refs_0_), channel_id=1, source_target_pairs={{0,4},{4,0},{8,12},{12,8},{16,20},{20,16},{24,28},{28,24},{1,5},{5... | collective-permute-start | bytes 405512 | tf_op jit(solution)/shard_map/ppermute | solution.py:420
  12.5 7.4 %collective-permute-start.1 = (s16[528,128]{1,0:T(8,128)(2,1)S(1)}, s16[528,128]{1,0:T(8,128)(2,1)S(1)}, u32[]{:S(2)}, u32[]{:S(2)}) collective-permute-start(s16[528,128]{1,0:T(8,128)(2,1)S(1)} %subbands.1.refs_0_), channel_id=1, source_target_pairs={{0,12},{4,8},{8,4},{12,0},{16,28},{20,24},{24,20},{28,16},{1,13},{... | collective-permute-start | bytes 405512 | tf_op jit(solution)/shard_map/ppermute | solution.py:420
  23.0 9.3 %collective-permute-start.3 = (s16[584,128]{1,0:T(8,128)(2,1)S(1)}, s16[584,128]{1,0:T(8,128)(2,1)S(1)}, u32[]{:S(2)}, u32[]{:S(2)}) collective-permute-start(s16[584,128]{1,0:T(8,128)(2,1)S(1)} %trials_coded.1), channel_id=1, source_target_pairs={{0,16},{4,20},{8,24},{12,28},{16,0},{20,4},{24,8},{28,12},{1,17},{... | collective-permute-start | bytes 448520 | tf_op jit(solution)/shard_map/ppermute | solution.py:431
  32.5 1.9 %collective-permute-start.4 = (s16[208,128]{1,0:T(8,128)(2,1)S(1)}, s16[208,128]{1,0:T(8,128)(2,1)S(1)}, u32[]{:S(2)}, u32[]{:S(2)}) collective-permute-start(s16[208,128]{1,0:T(8,128)(2,1)S(1)} %get-tuple-element.17), channel_id=1, source_target_pairs={{0,1},{1,0},{2,3},{3,2},{4,5},{5,4},{6,7},{7,6},{8,9},{9,8},{10,11... | collective-permute-start | bytes 159752 | tf_op jit(solution)/shard_map/ppermute | solution.py:437
  32.5 4.2 %collective-permute-start.5 = (s16[208,128]{1,0:T(8,128)(2,1)S(1)}, s16[208,128]{1,0:T(8,128)(2,1)S(1)}, u32[]{:S(2)}, u32[]{:S(2)}) collective-permute-start(s16[208,128]{1,0:T(8,128)(2,1)S(1)} %get-tuple-element.18), channel_id=1, source_target_pairs={{0,2},{1,3},{2,0},{3,1},{4,6},{5,7},{6,4},{7,5},{8,10},{9,11},{10,... | collective-permute-start | bytes 159752 | tf_op jit(solution)/shard_map/ppermute | solution.py:437
  34.1 3.8 %collective-permute-start.6 = (s16[208,128]{1,0:T(8,128)(2,1)S(1)}, s16[208,128]{1,0:T(8,128)(2,1)S(1)}, u32[]{:S(2)}, u32[]{:S(2)}) collective-permute-start(s16[208,128]{1,0:T(8,128)(2,1)S(1)} %get-tuple-element.19), channel_id=1, source_target_pairs={{0,3},{1,2},{2,1},{3,0},{4,7},{5,6},{6,5},{7,4},{8,11},{9,10},{10,... | collective-permute-start | bytes 159752 | tf_op jit(solution)/shard_map/ppermute | solution.py:437

commit v2 on v1

--- a/solution.py
+++ b/solution.py
@@ -124,7 +124,7 @@
         ],
         compiler_params=pltpu.CompilerParams(vmem_limit_bytes=VMEM_LIMIT),
         name="subbands",
-    )(chan_delay, filterbank)
+    )(pltpu.with_memory_space_constraint(chan_delay, pltpu.HBM), filterbank)
 
 
 def trial_kernel(blocks, subs, trials, origins, flips, primed, coded, delay_ref, *refs):
@@ -180,7 +180,7 @@
     for i, (flip, out) in enumerate(zip(flips, outs)):
         target = acc if coded else out
 
-        @pl.loop(0, trials)
+        @pl.loop(0, trials, unroll=trials)
         def _(trial):
             one_trial(trial, chan ^ flip, priors[i] if primed else None, target)
 
@@ -420,18 +420,22 @@
         part[flip] = lax.ppermute(own, "chan", pairs(chan_size, flip))
     sizes = (blocks, subs, trials)
     flips = tuple(range(quad, chan_size, quad))
-    sums = trial_sums([own], (0,), sub_delay, sizes, (*flips, 0))
-    rest = tuple(range(1, quad))
-    if quad == 4:
-        sums = trial_sums([part[2]], (2,), sub_delay, sizes, (*flips, 0), sums)
-        rest = (1, 3)
-    last = [part[flip] for flip in rest]
-    far = trial_sums(last, rest, sub_delay, sizes, flips, sums[:-1], True)
+    order = [0, 2, 1, 3] if quad == 4 else list(range(quad))
+    *early, final = order
+    far, near = None, None
+    for origin in early:
+        both = origin == 0
+        sums = trial_sums(
+            [part[origin]], (origin,), sub_delay, sizes, (*flips, 0) if both else flips, far
+        )
+        far, near = (sums[:-1], sums[-1:]) if both else (sums, near)
+    far = trial_sums([part[final]], (final,), sub_delay, sizes, flips, far, True)
     far = [
         lax.ppermute(send, "chan", pairs(chan_size, flip))
         for send, flip in zip(far, flips)
     ]
-    (near,) = trial_sums(last, rest, sub_delay, sizes, (0,), sums[-1:])
+    rest = tuple(order[1:])
+    (near,) = trial_sums([part[o] for o in rest], rest, sub_delay, sizes, (0,), near)
     mine, *sends = cut_by_phase(near, far, blocks, trials, owners)
     got = [
         lax.ppermute(send, "tm", pairs(owners, flip + 1))

time: 41.1 us -> 38.3 us (0.932)
  Pallas kernels: 23.1 us -> 20.9 us
  local copies, waits for them, and re-layouts: 0.69 us -> 0.01 us
  waiting for transfers between devices: 6.77 us -> 7.32 us
    pallas_call x4 -> x5, Pallas kernels: 13.4 us -> 11.2 us  [trial_sums(): pl.pallas_call(functools.partial(trial_kernel, *sizes, tuple(origins), tu...]
    ppermute x3, waiting for transfers between devices: 0.01 us -> 2.07 us  [per_device(): part[flip] = lax.ppermute(own, 'chan', pairs(chan_size, flip))]
    ppermute x1, waiting for transfers between devices: 3.24 us -> 1.77 us  [per_device(): lax.ppermute(send, 'chan', pairs(chan_size, flip))]
    unnamed x6 -> x4, local copies, waits for them, and re-layouts: 0.69 us -> 0.01 us
  transfers between devices with their start and end apart: 7 -> 7, of which waited for: 3 -> 4; matrix products, arithmetic and copies ran while one was open for 0% -> 0% of each run, Pallas kernels for 25% -> 24%
where the time goes in v2:
time: 38.3 us; the launch traced here: 38.1 us
  Pallas kernels  20.9 us (55%)
  starting transfers between devices  9.22 us (24%)
  waiting for transfers between devices  7.32 us (19%)
  between operations  0.72 us (2%)
    pallas_call x5, Pallas kernels, trial_sums(): pl.pallas_call(functools.partial(trial_kernel, *sizes, tuple(origins), tu...  11.2 us
    pallas_call x1, Pallas kernels, subband_sums(): pl.pallas_call(functools.partial(subband_kernel, chans, blocks, subs), in...  6.53 us
    ppermute x3, starting transfers between devices, per_device(): part[flip] = lax.ppermute(own, 'chan', pairs(chan_size, flip))  4.63 us
    ppermute x3, waiting for transfers between devices, per_device(): lax.ppermute(send, 'tm', pairs(owners, flip + 1))  3.48 us
    pallas_call x1, Pallas kernels, fold_and_box(): pl.pallas_call(functools.partial(fold_kernel, periods, trials, owners, wi...  2.95 us
    ppermute x1, starting transfers between devices, per_device(): lax.ppermute(send, 'chan', pairs(chan_size, flip))  2.65 us
    ppermute x3, waiting for transfers between devices, per_device(): part[flip] = lax.ppermute(own, 'chan', pairs(chan_size, flip))  2.07 us
    ppermute x3, starting transfers between devices, per_device(): lax.ppermute(send, 'tm', pairs(owners, flip + 1))  1.93 us
  transfers between devices with their start and end apart: 7, of which 4 were waited for; matrix products, arithmetic and copies ran while one was open for 0% of the time, Pallas kernels for 24%

profile of v2, /device:TPU:0, one launch (start us, length us, event | category | flops | bytes accessed | tf_op | source)
XLA Modules:
  0.0 38.1 jit_solution(5642546169944419461)
XLA Ops:
  0.6 0.0 copy-start
  0.6 0.0 copy-start.1
  0.7 6.5 %subbands.1.refs_0_ = s16[528,128]{1,0:T(8,128)(2,1)S(1)} custom-call(s32[512]{0:T(512)} %delay_hbm.1, bf16[512,8192]{1,0:T(8,128)(2,1)} %x_hbm.1), custom_call_target="tpu_custom_call" | custom-call | tf_op jit(solution)/shard_map/subbands/pallas_call | solution.py:111
  7.2 3.1 %collective-permute-start = (s16[528,128]{1,0:T(8,128)(2,1)S(1)}, s16[528,128]{1,0:T(8,128)(2,1)S(1)}, u32[]{:S(2)}, u32[]{:S(2)}) collective-permute-start(s16[528,128]{1,0:T(8,128)(2,1)S(1)} %subbands.1.refs_0_), channel_id=1, source_target_pairs={{0,8},{4,12},{8,0},{12,4},{16,24},{20,28},{24,16},{28,20},{1,9},{5... | collective-permute-start | bytes 405512 | tf_op jit(solution)/shard_map/ppermute | solution.py:420
  10.3 1.5 %collective-permute-start.1 = (s16[528,128]{1,0:T(8,128)(2,1)S(1)}, s16[528,128]{1,0:T(8,128)(2,1)S(1)}, u32[]{:S(2)}, u32[]{:S(2)}) collective-permute-start(s16[528,128]{1,0:T(8,128)(2,1)S(1)} %subbands.1.refs_0_), channel_id=1, source_target_pairs={{0,4},{4,0},{8,12},{12,8},{16,20},{20,16},{24,28},{28,24},{1,5},{5... | collective-permute-start | bytes 405512 | tf_op jit(solution)/shard_map/ppermute | solution.py:420
  11.8 0.0 collective-permute-start.2
  11.8 2.5 %trials.4 = (f32[576,128]{1,0:T(8,128)S(1)}, f32[576,128]{1,0:T(8,128)S(1)}) custom-call(s32[64,64]{1,0:T(8,128)S(1)} %copy-done, s16[528,128]{1,0:T(8,128)(2,1)S(1)} %subbands.1.refs_0_), custom_call_target="tpu_custom_call" | custom-call | tf_op jit(solution)/shard_map/trials/pallas_call | solution.py:208
  14.3 0.0 collective-permute-done.refs_0_
  14.3 1.8 %trials.6.refs_1_ = f32[576,128]{1,0:T(8,128)S(1)} custom-call(s32[64,64]{1,0:T(8,128)S(1)} %copy-done, s16[528,128]{1,0:T(8,128)(2,1)S(1)} %collective-permute-done.refs_0_, f32[576,128]{1,0:T(8,128)S(1)} %get-tuple-element.11.refs_1_), custom_call_target="tpu_custom_call" | custom-call | tf_op jit(solution)/shard_map/trials/pallas_call | solution.py:208
  16.2 2.1 %collective-permute-done.1.refs_1_.refs_0_ = s16[528,128]{1,0:T(8,128)(2,1)S(1)} collective-permute-done((s16[528,128]{1,0:T(8,128)(2,1)S(1)}, s16[528,128]{1,0:T(8,128)(2,1)S(1)}, u32[]{:S(2)}, u32[]{:S(2)}) %collective-permute-start.1) | collective-permute-done | bytes 135200 | tf_op jit(solution)/shard_map/ppermute | solution.py:420
  18.2 1.8 %trials.7.refs_1_ = f32[576,128]{1,0:T(8,128)S(1)} custom-call(s32[64,64]{1,0:T(8,128)S(1)} %copy-done, s16[528,128]{1,0:T(8,128)(2,1)S(1)} %collective-permute-done.1.refs_1_.refs_0_, f32[576,128]{1,0:T(8,128)S(1)} %trials.6.refs_1_), custom_call_target="tpu_custom_call" | custom-call | tf_op jit(solution)/shard_map/trials/pallas_call | solution.py:208
  20.1 0.0 collective-permute-done.2.refs_2_.refs_0_
  20.1 1.9 %trials_coded.1 = s16[584,128]{1,0:T(8,128)(2,1)S(1)} custom-call(s32[64,64]{1,0:T(8,128)S(1)} %copy-done, s16[528,128]{1,0:T(8,128)(2,1)S(1)} %collective-permute-done.2.refs_2_.refs_0_, f32[576,128]{1,0:T(8,128)S(1)} %trials.7.refs_1_), custom_call_target="tpu_custom_call" | custom-call | tf_op jit(solution)/shard_map/trials_coded/pallas_call | solution.py:208
  22.0 2.7 %collective-permute-start.3 = (s16[584,128]{1,0:T(8,128)(2,1)S(1)}, s16[584,128]{1,0:T(8,128)(2,1)S(1)}, u32[]{:S(2)}, u32[]{:S(2)}) collective-permute-start(s16[584,128]{1,0:T(8,128)(2,1)S(1)} %trials_coded.1), channel_id=1, source_target_pairs={{0,16},{4,20},{8,24},{12,28},{16,0},{20,4},{24,8},{28,12},{1,17},{... | collective-permute-start | bytes 448520 | tf_op jit(solution)/shard_map/ppermute | solution.py:434
  24.7 3.1 %trials.5.own_ref = f32[576,128]{1,0:T(8,128)S(1)} custom-call(s32[64,64]{1,0:T(8,128)S(1)} %copy-done, s16[528,128]{1,0:T(8,128)(2,1)S(1)} %collective-permute-done.refs_0_, s16[528,128]{1,0:T(8,128)(2,1)S(1)} %collective-permute-done.1.refs_1_.refs_0_, s16[528,128]{1,0:T(8,128)(2,1)S(1)} %collective-permute-done.2.refs_2_.refs_0_, ...), custom_call_target="tpu_custom_call" | custom-call | tf_op jit(solution)/shard_map/trials/pallas_call | solution.py:208
  27.8 1.8 %collective-permute-done.3.refs_0_ = s16[584,128]{1,0:T(8,128)(2,1)S(1)} collective-permute-done((s16[584,128]{1,0:T(8,128)(2,1)S(1)}, s16[584,128]{1,0:T(8,128)(2,1)S(1)}, u32[]{:S(2)}, u32[]{:S(2)}) %collective-permute-start.3) | collective-permute-done | bytes 149536 | tf_op jit(solution)/shard_map/ppermute | solution.py:434
  29.6 0.2 cut.1
  29.8 0.1 collective-permute-start.4
  29.8 1.6 %collective-permute-start.5 = (s16[208,128]{1,0:T(8,128)(2,1)S(1)}, s16[208,128]{1,0:T(8,128)(2,1)S(1)}, u32[]{:S(2)}, u32[]{:S(2)}) collective-permute-start(s16[208,128]{1,0:T(8,128)(2,1)S(1)} %get-tuple-element.14), channel_id=1, source_target_pairs={{0,2},{1,3},{2,0},{3,1},{4,6},{5,7},{6,4},{7,5},{8,10},{9,11},{10,... | collective-permute-start | bytes 159752 | tf_op jit(solution)/shard_map/ppermute | solution.py:441
  31.4 0.3 collective-permute-start.6
  31.7 0.0 collective-permute-done.4.refs_0_
  31.7 2.4 %collective-permute-done.5.refs_1_ = s16[208,128]{1,0:T(8,128)(2,1)S(1)} collective-permute-done((s16[208,128]{1,0:T(8,128)(2,1)S(1)}, s16[208,128]{1,0:T(8,128)(2,1)S(1)}, u32[]{:S(2)}, u32[]{:S(2)}) %collective-permute-start.5) | collective-permute-done | bytes 53280 | tf_op jit(solution)/shard_map/ppermute | solution.py:441
  34.1 1.1 %collective-permute-done.6.refs_2_ = s16[208,128]{1,0:T(8,128)(2,1)S(1)} collective-permute-done((s16[208,128]{1,0:T(8,128)(2,1)S(1)}, s16[208,128]{1,0:T(8,128)(2,1)S(1)}, u32[]{:S(2)}, u32[]{:S(2)}) %collective-permute-start.6) | collective-permute-done | bytes 53280 | tf_op jit(solution)/shard_map/ppermute | solution.py:441
  35.2 2.9 %fold.1 = (f32[512,128]{1,0:T(8,128)}, f32[2048,128]{1,0:T(8,128)}) custom-call(s32[4]{0:T(128)S(1)} %copy-done.1, f32[200,128]{1,0:T(8,128)S(1)} %get-tuple-element.12.mine_ref, s16[208,128]{1,0:T(8,128)(2,1)S(1)} %collective-permute-done.4.refs_0_, s16[208,128]{1,0:T(8,128)(2,1)S(1)} %collective-permute-done.5.refs_1_, ...), custom_call_target="tpu_custom_call" | custom-call | tf_op jit(solution)/shard_map/fold/pallas_call | solution.py:387
  (2 shorter events, 0.0 us)
Async XLA Ops:
  0.6 11.2 %copy-start = (s32[64,64]{1,0:T(8,128)S(1)}, s32[64,64]{1,0:T(8,128)}, u32[]{:S(2)}) copy-start(s32[64,64]{1,0:T(8,128)} %delay_ref.9) | copy-start | bytes 49156
  0.6 34.5 %copy-start.1 = (s32[4]{0:T(128)S(1)}, s32[4]{0:T(128)}, u32[]{:S(2)}) copy-start(s32[4]{0:T(128)} %width_ref.1) | copy-start | bytes 52
  7.2 7.1 %collective-permute-start = (s16[528,128]{1,0:T(8,128)(2,1)S(1)}, s16[528,128]{1,0:T(8,128)(2,1)S(1)}, u32[]{:S(2)}, u32[]{:S(2)}) collective-permute-start(s16[528,128]{1,0:T(8,128)(2,1)S(1)} %subbands.1.refs_0_), channel_id=1, source_target_pairs={{0,8},{4,12},{8,0},{12,4},{16,24},{20,28},{24,16},{28,20},{1,9},{5... | collective-permute-start | bytes 405512 | tf_op jit(solution)/shard_map/ppermute | solution.py:420
  10.3 7.9 %collective-permute-start.1 = (s16[528,128]{1,0:T(8,128)(2,1)S(1)}, s16[528,128]{1,0:T(8,128)(2,1)S(1)}, u32[]{:S(2)}, u32[]{:S(2)}) collective-permute-start(s16[528,128]{1,0:T(8,128)(2,1)S(1)} %subbands.1.refs_0_), channel_id=1, source_target_pairs={{0,4},{4,0},{8,12},{12,8},{16,20},{20,16},{24,28},{28,24},{1,5},{5... | collective-permute-start | bytes 405512 | tf_op jit(solution)/shard_map/ppermute | solution.py:420
  11.8 8.3 %collective-permute-start.2 = (s16[528,128]{1,0:T(8,128)(2,1)S(1)}, s16[528,128]{1,0:T(8,128)(2,1)S(1)}, u32[]{:S(2)}, u32[]{:S(2)}) collective-permute-start(s16[528,128]{1,0:T(8,128)(2,1)S(1)} %subbands.1.refs_0_), channel_id=1, source_target_pairs={{0,12},{4,8},{8,4},{12,0},{16,28},{20,24},{24,20},{28,16},{1,13},{... | collective-permute-start | bytes 405512 | tf_op jit(solution)/shard_map/ppermute | solution.py:420
  22.0 7.5 %collective-permute-start.3 = (s16[584,128]{1,0:T(8,128)(2,1)S(1)}, s16[584,128]{1,0:T(8,128)(2,1)S(1)}, u32[]{:S(2)}, u32[]{:S(2)}) collective-permute-start(s16[584,128]{1,0:T(8,128)(2,1)S(1)} %trials_coded.1), channel_id=1, source_target_pairs={{0,16},{4,20},{8,24},{12,28},{16,0},{20,4},{24,8},{28,12},{1,17},{... | collective-permute-start | bytes 448520 | tf_op jit(solution)/shard_map/ppermute | solution.py:434
  29.8 1.9 %collective-permute-start.4 = (s16[208,128]{1,0:T(8,128)(2,1)S(1)}, s16[208,128]{1,0:T(8,128)(2,1)S(1)}, u32[]{:S(2)}, u32[]{:S(2)}) collective-permute-start(s16[208,128]{1,0:T(8,128)(2,1)S(1)} %get-tuple-element.13), channel_id=1, source_target_pairs={{0,1},{1,0},{2,3},{3,2},{4,5},{5,4},{6,7},{7,6},{8,9},{9,8},{10,11... | collective-permute-start | bytes 159752 | tf_op jit(solution)/shard_map/ppermute | solution.py:441
  29.8 4.2 %collective-permute-start.5 = (s16[208,128]{1,0:T(8,128)(2,1)S(1)}, s16[208,128]{1,0:T(8,128)(2,1)S(1)}, u32[]{:S(2)}, u32[]{:S(2)}) collective-permute-start(s16[208,128]{1,0:T(8,128)(2,1)S(1)} %get-tuple-element.14), channel_id=1, source_target_pairs={{0,2},{1,3},{2,0},{3,1},{4,6},{5,7},{6,4},{7,5},{8,10},{9,11},{10,... | collective-permute-start | bytes 159752 | tf_op jit(solution)/shard_map/ppermute | solution.py:441
  31.4 3.8 %collective-permute-start.6 = (s16[208,128]{1,0:T(8,128)(2,1)S(1)}, s16[208,128]{1,0:T(8,128)(2,1)S(1)}, u32[]{:S(2)}, u32[]{:S(2)}) collective-permute-start(s16[208,128]{1,0:T(8,128)(2,1)S(1)} %get-tuple-element.15), channel_id=1, source_target_pairs={{0,3},{1,2},{2,1},{3,0},{4,7},{5,6},{6,5},{7,4},{8,11},{9,10},{10,... | collective-permute-start | bytes 159752 | tf_op jit(solution)/shard_map/ppermute | solution.py:441

commit v3 on v2

--- a/solution.py
+++ b/solution.py
@@ -127,14 +127,28 @@
     )(pltpu.with_memory_space_constraint(chan_delay, pltpu.HBM), filterbank)
 
 
-def trial_kernel(blocks, subs, trials, origins, flips, primed, coded, delay_ref, *refs):
+def trial_kernel(blocks, subs, trials, origins, flips, primed, coded, delays, *refs):
     refs = list(refs)
     take = lambda n: [refs.pop(0) for _ in range(n)]
     parts = take(len(origins))
     priors = take(len(flips)) if primed else []
     outs = take(len(flips))
-    spread, late, acc = refs
+    spread, late, acc, delay_ref, delay_sem = refs
     chan = lax.axis_index("chan")
+    fetched = delay_ref.shape[1]
+    copies, offset = [], []
+    for i, flip in enumerate(flips):
+        wanted = (chan ^ flip) * trials
+        first = wanted // fetched * fetched
+        offset.append(wanted - first)
+        copies.append(
+            pltpu.make_async_copy(
+                delays.at[pl.ds(pl.multiple_of(first, 8), fetched), :],
+                delay_ref.at[i],
+                delay_sem.at[i],
+            )
+        )
+        copies[i].start()
     out_blocks = LEAD + blocks
     depth = out_blocks + LEAD
     for at, part in enumerate(parts):
@@ -153,12 +167,15 @@
     lane = lane_iota(8)
     tiles = out_blocks // 8
 
-    def one_trial(trial, owner, prior, out):
+    for copy in copies:
+        copy.wait()
+
+    def one_trial(trial, i, prior, out):
         here = [jnp.zeros((8, LANES), F32)] * tiles
         before = [jnp.zeros((8, LANES), F32)] * tiles
         for at, origin in enumerate(origins):
             for sub in range(subs):
-                delay = delay_ref[owner * trials + trial, (chan ^ origin) * subs + sub]
+                delay = delay_ref[i, offset[i] + trial, (chan ^ origin) * subs + sub]
                 shift = delay & (LANES - 1)
                 stays = lane < LANES - shift
                 back = (LANES - shift) & (LANES - 1)
@@ -182,7 +199,7 @@
 
         @pl.loop(0, trials, unroll=trials)
         def _(trial):
-            one_trial(trial, chan ^ flip, priors[i] if primed else None, target)
+            one_trial(trial, i, priors[i] if primed else None, target)
 
         if coded:
             values = acc[...].reshape(out_blocks, trials, LANES)
@@ -209,13 +226,15 @@
         functools.partial(
             trial_kernel, *sizes, tuple(origins), tuple(flips), bool(priors), coded
         ),
-        in_specs=[pl.BlockSpec(memory_space=pltpu.SMEM)] + [vmem] * len(arrays),
+        in_specs=[pl.BlockSpec(memory_space=pl.ANY)] + [vmem] * len(arrays),
         out_specs=[vmem] * len(flips),
         out_shape=[out] * len(flips),
         scratch_shapes=[
             pltpu.VMEM((len(parts) * depth * subs, LANES), F32),
             pltpu.VMEM((out_blocks + 8, LANES), F32),
             pltpu.VMEM((rows, LANES), F32),
+            pltpu.SMEM((len(flips), max(trials, 8), sub_delay.shape[1]), jnp.int32),
+            pltpu.SemaphoreType.DMA((len(flips),)),
         ],
         compiler_params=pltpu.CompilerParams(vmem_limit_bytes=VMEM_LIMIT),
         name="trials_coded" if coded else "trials",
@@ -420,8 +439,7 @@
         part[flip] = lax.ppermute(own, "chan", pairs(chan_size, flip))
     sizes = (blocks, subs, trials)
     flips = tuple(range(quad, chan_size, quad))
-    order = [0, 2, 1, 3] if quad == 4 else list(range(quad))
-    *early, final = order
+    early, final = ((0, 2), (1, 3)) if quad == 4 else ((0,), tuple(range(1, quad)))
     far, near = None, None
     for origin in early:
         both = origin == 0
@@ -429,12 +447,13 @@
             [part[origin]], (origin,), sub_delay, sizes, (*flips, 0) if both else flips, far
         )
         far, near = (sums[:-1], sums[-1:]) if both else (sums, near)
-    far = trial_sums([part[final]], (final,), sub_delay, sizes, flips, far, True)
+    last = [part[origin] for origin in final]
+    far = trial_sums(last, final, sub_delay, sizes, flips, far, True)
     far = [
         lax.ppermute(send, "chan", pairs(chan_size, flip))
         for send, flip in zip(far, flips)
     ]
-    rest = tuple(order[1:])
+    rest = (*early[1:], *final)
     (near,) = trial_sums([part[o] for o in rest], rest, sub_delay, sizes, (0,), near)
     mine, *sends = cut_by_phase(near, far, blocks, trials, owners)
     got = [

time: 38.3 us -> 39.1 us (1.021)
  waiting for transfers between devices: 7.32 us -> 11.3 us
  Pallas kernels: 20.9 us -> 17.8 us
    pallas_call x5 -> x4, Pallas kernels: 11.2 us -> 8.09 us  [trial_sums(): pl.pallas_call(functools.partial(trial_kernel, *sizes, tuple(origins), tu...]
    ppermute x1, waiting for transfers between devices: 1.77 us -> 3.77 us  [per_device(): lax.ppermute(send, 'chan', pairs(chan_size, flip))]
    ppermute x3, waiting for transfers between devices: 2.07 us -> 4.06 us  [per_device(): part[flip] = lax.ppermute(own, 'chan', pairs(chan_size, flip))]
  transfers between devices with their start and end apart: 7 -> 7, of which waited for: 4 -> 6; matrix products, arithmetic and copies ran while one was open for 0% -> 0% of each run, Pallas kernels for 24% -> 15%
where the time goes in v3:
time: 39.1 us; the launch traced here: 39 us
  Pallas kernels  17.8 us (46%)
  waiting for transfers between devices  11.3 us (29%)
  starting transfers between devices  9.22 us (24%)
  between operations  0.71 us (2%)
    pallas_call x4, Pallas kernels, trial_sums(): pl.pallas_call(functools.partial(trial_kernel, *sizes, tuple(origins), tu...  8.09 us
    pallas_call x1, Pallas kernels, subband_sums(): pl.pallas_call(functools.partial(subband_kernel, chans, blocks, subs), in...  6.53 us
    ppermute x3, starting transfers between devices, per_device(): part[flip] = lax.ppermute(own, 'chan', pairs(chan_size, flip))  4.63 us
    ppermute x3, waiting for transfers between devices, per_device(): part[flip] = lax.ppermute(own, 'chan', pairs(chan_size, flip))  4.06 us
    ppermute x1, waiting for transfers between devices, per_device(): lax.ppermute(send, 'chan', pairs(chan_size, flip))  3.77 us
    ppermute x3, waiting for transfers between devices, per_device(): lax.ppermute(send, 'tm', pairs(owners, flip + 1))  3.48 us
    pallas_call x1, Pallas kernels, fold_and_box(): pl.pallas_call(functools.partial(fold_kernel, periods, trials, owners, wi...  2.94 us
    ppermute x1, starting transfers between devices, per_device(): lax.ppermute(send, 'chan', pairs(chan_size, flip))  2.65 us
  transfers between devices with their start and end apart: 7, of which 6 were waited for; matrix products, arithmetic and copies ran while one was open for 0% of the time, Pallas kernels for 15%

profile of v3, /device:TPU:0, one launch (start us, length us, event | category | flops | bytes accessed | tf_op | source)
XLA Modules:
  0.0 39.0 jit_solution(9559088637605514346)
XLA Ops:
  0.6 0.0 copy-start
  0.6 0.0 copy-start.1
  0.7 6.5 %subbands.1.refs_0_ = s16[528,128]{1,0:T(8,128)(2,1)S(1)} custom-call(s32[512]{0:T(512)} %delay_hbm.1, bf16[512,8192]{1,0:T(8,128)(2,1)} %x_hbm.1), custom_call_target="tpu_custom_call" | custom-call | tf_op jit(solution)/shard_map/subbands/pallas_call | solution.py:111
  7.2 3.1 %collective-permute-start = (s16[528,128]{1,0:T(8,128)(2,1)S(1)}, s16[528,128]{1,0:T(8,128)(2,1)S(1)}, u32[]{:S(2)}, u32[]{:S(2)}) collective-permute-start(s16[528,128]{1,0:T(8,128)(2,1)S(1)} %subbands.1.refs_0_), channel_id=1, source_target_pairs={{0,8},{4,12},{8,0},{12,4},{16,24},{20,28},{24,16},{28,20},{1,9},{5... | collective-permute-start | bytes 405512 | tf_op jit(solution)/shard_map/ppermute | solution.py:439
  10.3 1.4 %collective-permute-start.2 = (s16[528,128]{1,0:T(8,128)(2,1)S(1)}, s16[528,128]{1,0:T(8,128)(2,1)S(1)}, u32[]{:S(2)}, u32[]{:S(2)}) collective-permute-start(s16[528,128]{1,0:T(8,128)(2,1)S(1)} %subbands.1.refs_0_), channel_id=1, source_target_pairs={{0,12},{4,8},{8,4},{12,0},{16,28},{20,24},{24,20},{28,16},{1,13},{... | collective-permute-start | bytes 405512 | tf_op jit(solution)/shard_map/ppermute | solution.py:439
  11.7 0.1 collective-permute-start.1
  11.8 0.0 copy-done
  11.8 2.1 %trials.3 = (f32[576,128]{1,0:T(8,128)S(1)}, f32[576,128]{1,0:T(8,128)S(1)}) custom-call(s32[64,64]{1,0:T(8,128)S(1)} %copy-done, s16[528,128]{1,0:T(8,128)(2,1)S(1)} %subbands.1.refs_0_), custom_call_target="tpu_custom_call" | custom-call | tf_op jit(solution)/shard_map/trials/pallas_call | solution.py:225
  13.9 0.4 collective-permute-done.refs_0_
  14.3 1.4 %trials.5.refs_2_ = f32[576,128]{1,0:T(8,128)S(1)} custom-call(s32[64,64]{1,0:T(8,128)S(1)} %copy-done, s16[528,128]{1,0:T(8,128)(2,1)S(1)} %collective-permute-done.refs_0_, f32[576,128]{1,0:T(8,128)S(1)} %get-tuple-element.11.refs_1_), custom_call_target="tpu_custom_call" | custom-call | tf_op jit(solution)/shard_map/trials/pallas_call | solution.py:225
  15.7 2.3 %collective-permute-done.2.refs_2_.refs_1_ = s16[528,128]{1,0:T(8,128)(2,1)S(1)} collective-permute-done((s16[528,128]{1,0:T(8,128)(2,1)S(1)}, s16[528,128]{1,0:T(8,128)(2,1)S(1)}, u32[]{:S(2)}, u32[]{:S(2)}) %collective-permute-start.2) | collective-permute-done | bytes 135200 | tf_op jit(solution)/shard_map/ppermute | solution.py:439
  18.0 1.4 %collective-permute-done.1.refs_1_.refs_0_ = s16[528,128]{1,0:T(8,128)(2,1)S(1)} collective-permute-done((s16[528,128]{1,0:T(8,128)(2,1)S(1)}, s16[528,128]{1,0:T(8,128)(2,1)S(1)}, u32[]{:S(2)}, u32[]{:S(2)}) %collective-permute-start.1) | collective-permute-done | bytes 135200 | tf_op jit(solution)/shard_map/ppermute | solution.py:439
  19.4 2.1 %trials_coded.1 = s16[584,128]{1,0:T(8,128)(2,1)S(1)} custom-call(s32[64,64]{1,0:T(8,128)S(1)} %copy-done, s16[528,128]{1,0:T(8,128)(2,1)S(1)} %collective-permute-done.1.refs_1_.refs_0_, s16[528,128]{1,0:T(8,128)(2,1)S(1)} %collective-permute-done.2.refs_2_.refs_1_, f32[576,128]{1,0:T(8,128)S(1)} %trials.5.refs_2_), custom_call_target="tpu_custom_call" | custom-call | tf_op jit(solution)/shard_map/trials_coded/pallas_call | solution.py:225
  21.4 2.7 %collective-permute-start.3 = (s16[584,128]{1,0:T(8,128)(2,1)S(1)}, s16[584,128]{1,0:T(8,128)(2,1)S(1)}, u32[]{:S(2)}, u32[]{:S(2)}) collective-permute-start(s16[584,128]{1,0:T(8,128)(2,1)S(1)} %trials_coded.1), channel_id=1, source_target_pairs={{0,16},{4,20},{8,24},{12,28},{16,0},{20,4},{24,8},{28,12},{1,17},{... | collective-permute-start | bytes 448520 | tf_op jit(solution)/shard_map/ppermute | solution.py:453
  24.1 2.6 %trials.4.own_ref = f32[576,128]{1,0:T(8,128)S(1)} custom-call(s32[64,64]{1,0:T(8,128)S(1)} %copy-done, s16[528,128]{1,0:T(8,128)(2,1)S(1)} %collective-permute-done.refs_0_, s16[528,128]{1,0:T(8,128)(2,1)S(1)} %collective-permute-done.1.refs_1_.refs_0_, s16[528,128]{1,0:T(8,128)(2,1)S(1)} %collective-permute-done.2.refs_2_.refs_1_, ...), custom_call_target="tpu_custom_call" | custom-call | tf_op jit(solution)/shard_map/trials/pallas_call | solution.py:225
  26.7 3.8 %collective-permute-done.3.refs_0_ = s16[584,128]{1,0:T(8,128)(2,1)S(1)} collective-permute-done((s16[584,128]{1,0:T(8,128)(2,1)S(1)}, s16[584,128]{1,0:T(8,128)(2,1)S(1)}, u32[]{:S(2)}, u32[]{:S(2)}) %collective-permute-start.3) | collective-permute-done | bytes 149536 | tf_op jit(solution)/shard_map/ppermute | solution.py:453
  30.4 0.2 cut.1
  30.6 0.1 collective-permute-start.4
  30.7 1.6 %collective-permute-start.5 = (s16[208,128]{1,0:T(8,128)(2,1)S(1)}, s16[208,128]{1,0:T(8,128)(2,1)S(1)}, u32[]{:S(2)}, u32[]{:S(2)}) collective-permute-start(s16[208,128]{1,0:T(8,128)(2,1)S(1)} %get-tuple-element.14), channel_id=1, source_target_pairs={{0,2},{1,3},{2,0},{3,1},{4,6},{5,7},{6,4},{7,5},{8,10},{9,11},{10,... | collective-permute-start | bytes 159752 | tf_op jit(solution)/shard_map/ppermute | solution.py:460
  32.3 0.3 collective-permute-start.6
  32.6 0.0 collective-permute-done.4.refs_0_
  32.6 2.4 %collective-permute-done.5.refs_1_ = s16[208,128]{1,0:T(8,128)(2,1)S(1)} collective-permute-done((s16[208,128]{1,0:T(8,128)(2,1)S(1)}, s16[208,128]{1,0:T(8,128)(2,1)S(1)}, u32[]{:S(2)}, u32[]{:S(2)}) %collective-permute-start.5) | collective-permute-done | bytes 53280 | tf_op jit(solution)/shard_map/ppermute | solution.py:460
  35.0 1.1 %collective-permute-done.6.refs_2_ = s16[208,128]{1,0:T(8,128)(2,1)S(1)} collective-permute-done((s16[208,128]{1,0:T(8,128)(2,1)S(1)}, s16[208,128]{1,0:T(8,128)(2,1)S(1)}, u32[]{:S(2)}, u32[]{:S(2)}) %collective-permute-start.6) | collective-permute-done | bytes 53280 | tf_op jit(solution)/shard_map/ppermute | solution.py:460
  36.1 2.9 %fold.1 = (f32[512,128]{1,0:T(8,128)}, f32[2048,128]{1,0:T(8,128)}) custom-call(s32[4]{0:T(128)S(1)} %copy-done.1, f32[200,128]{1,0:T(8,128)S(1)} %get-tuple-element.12.mine_ref, s16[208,128]{1,0:T(8,128)(2,1)S(1)} %collective-permute-done.4.refs_0_, s16[208,128]{1,0:T(8,128)(2,1)S(1)} %collective-permute-done.5.refs_1_, ...), custom_call_target="tpu_custom_call" | custom-call | tf_op jit(solution)/shard_map/fold/pallas_call | solution.py:406
  (1 shorter events, 0.0 us)
Async XLA Ops:
  0.6 11.2 %copy-start = (s32[64,64]{1,0:T(8,128)S(1)}, s32[64,64]{1,0:T(8,128)}, u32[]{:S(2)}) copy-start(s32[64,64]{1,0:T(8,128)} %delays.7) | copy-start | bytes 49156
  0.6 35.4 %copy-start.1 = (s32[4]{0:T(128)S(1)}, s32[4]{0:T(128)}, u32[]{:S(2)}) copy-start(s32[4]{0:T(128)} %width_ref.1) | copy-start | bytes 52
  7.2 7.1 %collective-permute-start = (s16[528,128]{1,0:T(8,128)(2,1)S(1)}, s16[528,128]{1,0:T(8,128)(2,1)S(1)}, u32[]{:S(2)}, u32[]{:S(2)}) collective-permute-start(s16[528,128]{1,0:T(8,128)(2,1)S(1)} %subbands.1.refs_0_), channel_id=1, source_target_pairs={{0,8},{4,12},{8,0},{12,4},{16,24},{20,28},{24,16},{28,20},{1,9},{5... | collective-permute-start | bytes 405512 | tf_op jit(solution)/shard_map/ppermute | solution.py:439
  10.3 7.7 %collective-permute-start.2 = (s16[528,128]{1,0:T(8,128)(2,1)S(1)}, s16[528,128]{1,0:T(8,128)(2,1)S(1)}, u32[]{:S(2)}, u32[]{:S(2)}) collective-permute-start(s16[528,128]{1,0:T(8,128)(2,1)S(1)} %subbands.1.refs_0_), channel_id=1, source_target_pairs={{0,12},{4,8},{8,4},{12,0},{16,28},{20,24},{24,20},{28,16},{1,13},{... | collective-permute-start | bytes 405512 | tf_op jit(solution)/shard_map/ppermute | solution.py:439
  11.7 7.7 %collective-permute-start.1 = (s16[528,128]{1,0:T(8,128)(2,1)S(1)}, s16[528,128]{1,0:T(8,128)(2,1)S(1)}, u32[]{:S(2)}, u32[]{:S(2)}) collective-permute-start(s16[528,128]{1,0:T(8,128)(2,1)S(1)} %subbands.1.refs_0_), channel_id=1, source_target_pairs={{0,4},{4,0},{8,12},{12,8},{16,20},{20,16},{24,28},{28,24},{1,5},{5... | collective-permute-start | bytes 405512 | tf_op jit(solution)/shard_map/ppermute | solution.py:439
  21.4 9.0 %collective-permute-start.3 = (s16[584,128]{1,0:T(8,128)(2,1)S(1)}, s16[584,128]{1,0:T(8,128)(2,1)S(1)}, u32[]{:S(2)}, u32[]{:S(2)}) collective-permute-start(s16[584,128]{1,0:T(8,128)(2,1)S(1)} %trials_coded.1), channel_id=1, source_target_pairs={{0,16},{4,20},{8,24},{12,28},{16,0},{20,4},{24,8},{28,12},{1,17},{... | collective-permute-start | bytes 448520 | tf_op jit(solution)/shard_map/ppermute | solution.py:453
  30.6 1.9 %collective-permute-start.4 = (s16[208,128]{1,0:T(8,128)(2,1)S(1)}, s16[208,128]{1,0:T(8,128)(2,1)S(1)}, u32[]{:S(2)}, u32[]{:S(2)}) collective-permute-start(s16[208,128]{1,0:T(8,128)(2,1)S(1)} %get-tuple-element.13), channel_id=1, source_target_pairs={{0,1},{1,0},{2,3},{3,2},{4,5},{5,4},{6,7},{7,6},{8,9},{9,8},{10,11... | collective-permute-start | bytes 159752 | tf_op jit(solution)/shard_map/ppermute | solution.py:460
  30.7 4.2 %collective-permute-start.5 = (s16[208,128]{1,0:T(8,128)(2,1)S(1)}, s16[208,128]{1,0:T(8,128)(2,1)S(1)}, u32[]{:S(2)}, u32[]{:S(2)}) collective-permute-start(s16[208,128]{1,0:T(8,128)(2,1)S(1)} %get-tuple-element.14), channel_id=1, source_target_pairs={{0,2},{1,3},{2,0},{3,1},{4,6},{5,7},{6,4},{7,5},{8,10},{9,11},{10,... | collective-permute-start | bytes 159752 | tf_op jit(solution)/shard_map/ppermute | solution.py:460
  32.3 3.8 %collective-permute-start.6 = (s16[208,128]{1,0:T(8,128)(2,1)S(1)}, s16[208,128]{1,0:T(8,128)(2,1)S(1)}, u32[]{:S(2)}, u32[]{:S(2)}) collective-permute-start(s16[208,128]{1,0:T(8,128)(2,1)S(1)} %get-tuple-element.15), channel_id=1, source_target_pairs={{0,3},{1,2},{2,1},{3,0},{4,7},{5,6},{6,5},{7,4},{8,11},{9,10},{10,... | collective-permute-start | bytes 159752 | tf_op jit(solution)/shard_map/ppermute | solution.py:460

commit v4 on v3

--- a/solution.py
+++ b/solution.py
@@ -22,6 +22,7 @@
 GROUP = 2**LEVELS
 ROW_BLOCKS = NBIN // LANES
 LEAD = (D1MAX + D2MAX) // LANES
+BOX_ROWS = 4
 VMEM_LIMIT = 48 << 20
 SCALE = 2.0 ** (-LEVELS / 2) / math.sqrt(NCHAN)
 
@@ -61,6 +62,7 @@
     delay_copy.wait()
     lane = lane_iota(8)
     tiles = blocks // 8
+    pitch = blocks + 4
 
     @pl.loop(0, subs)
     def _(sub):
@@ -76,18 +78,31 @@
                         block * LANES : (block + 1) * LANES,
                     ].astype(F32)
                     for k in range(2):
-                        at = ((octet + k) * blocks + block) * 8
-                        turned[at : at + 8, :] = both[8 * k : 8 * k + 8]
+                        base = (octet + k) * pitch * 8
+                        if (octet + k) % 4 == 0:
+                            at = pl.ds(base + block * 8, 8)
+                        else:
+                            at = pl.ds(base + block, 8, stride=pitch)
+                        turned[at, :] = both[8 * k : 8 * k + 8]
             for i in range(8):
                 delay = delay_ref[sub * chans + octet * 8 + i]
                 shift = (2 * LANES - delay) & (LANES - 1)
                 stays = lane < LANES - delay
+                values = []
                 for t in range(tiles):
-                    first = (octet * blocks + t * 8) * 8 + i
-                    value = turned[pl.ds(first, 8, stride=8), :]
-                    value = pltpu.roll(value, shift, 1)
-                    here[t] = here[t] + jnp.where(stays, value, 0.0)
-                    before[t] = before[t] + jnp.where(stays, 0.0, value)
+                    base = octet * pitch * 8
+                    if octet % 4 == 0:
+                        at = pl.ds(base + t * 64 + i, 8, stride=8)
+                    else:
+                        at = pl.ds(base + i * pitch + t * 8, 8)
+                    values.append(turned[at, :])
+                for t in range(0, tiles, 2):
+                    both = jnp.concatenate(values[t : t + 2], axis=0)
+                    both = pltpu.roll(both.astype(x_ref.dtype), shift, 1).astype(F32)
+                    for k in range(2):
+                        value = both[8 * k : 8 * k + 8]
+                        here[t + k] = here[t + k] + jnp.where(stays, value, 0.0)
+                        before[t + k] = before[t + k] + jnp.where(stays, 0.0, value)
         for t in range(tiles):
             late[8 * t : 8 * t + 8, :] = before[t]
         late[blocks : blocks + 8, :] = jnp.zeros((8, LANES), F32)
@@ -116,7 +131,7 @@
         scratch_shapes=[
             pltpu.SMEM((chans_here,), jnp.int32),
             pltpu.VMEM((subs, chans, samples), filterbank.dtype),
-            pltpu.VMEM((chans * blocks, LANES), F32),
+            pltpu.VMEM((chans * (blocks + 4), LANES), F32),
             pltpu.VMEM((blocks + 8, LANES), F32),
             pltpu.VMEM(((blocks + 1) * subs, LANES), F32),
             pltpu.SemaphoreType.DMA((subs,)),
@@ -127,12 +142,30 @@
     )(pltpu.with_memory_space_constraint(chan_delay, pltpu.HBM), filterbank)
 
 
-def trial_kernel(blocks, subs, trials, origins, flips, primed, coded, delays, *refs):
+def box_taps(width_ref, band_ref, weight_ref):
+    ahead = lax.broadcasted_iota(
+        jnp.int32, (2 * LANES, LANES), 0
+    ) - lax.broadcasted_iota(jnp.int32, (2 * LANES, LANES), 1)
+    for w in range(width_ref.shape[0]):
+        width = width_ref[w]
+        inside = jnp.logical_and(ahead >= 0, ahead < width)
+        inside = jnp.where(inside, 1.0, 0.0).astype(band_ref.dtype)
+        band_ref[:, w * LANES : (w + 1) * LANES] = inside
+        count = jnp.full((8, LANES), width, jnp.int32).astype(F32)
+        weight_ref[8 * w : 8 * w + 8, :] = 1.0 / jnp.sqrt(count)
+
+
+def trial_kernel(
+    blocks, subs, trials, origins, flips, primed, coded, taps, delays, *refs
+):
     refs = list(refs)
     take = lambda n: [refs.pop(0) for _ in range(n)]
     parts = take(len(origins))
     priors = take(len(flips)) if primed else []
+    width_ref = take(1)[0] if taps else None
     outs = take(len(flips))
+    if taps:
+        box_taps(width_ref, *take(2))
     spread, late, acc, delay_ref, delay_sem = refs
     chan = lax.axis_index("chan")
     fetched = delay_ref.shape[1]
@@ -210,7 +243,9 @@
             out[rows : rows + trials, :] = to_i16(exponent)
 
 
-def trial_sums(parts, origins, sub_delay, sizes, flips, priors=None, coded=False):
+def trial_sums(
+    parts, origins, sub_delay, sizes, flips, priors=None, coded=False, box_width=None
+):
     if not flips:
         return []
     blocks, subs, trials = sizes
@@ -222,13 +257,22 @@
     )
     vmem = pl.BlockSpec(memory_space=pltpu.VMEM)
     arrays = [*parts, *(priors or [])]
+    in_specs = [pl.BlockSpec(memory_space=pl.ANY)] + [vmem] * len(arrays)
+    outs = [out] * len(flips)
+    taps = box_width is not None
+    if taps:
+        widths = box_width.shape[0]
+        arrays.append(box_width)
+        in_specs.append(pl.BlockSpec(memory_space=pltpu.SMEM))
+        outs.append(jax.ShapeDtypeStruct((2 * LANES, widths * LANES), jnp.bfloat16))
+        outs.append(jax.ShapeDtypeStruct((widths * 8, LANES), F32))
     return pl.pallas_call(
         functools.partial(
-            trial_kernel, *sizes, tuple(origins), tuple(flips), bool(priors), coded
+            trial_kernel, *sizes, tuple(origins), tuple(flips), bool(priors), coded, taps
         ),
-        in_specs=[pl.BlockSpec(memory_space=pl.ANY)] + [vmem] * len(arrays),
-        out_specs=[vmem] * len(flips),
-        out_shape=[out] * len(flips),
+        in_specs=in_specs,
+        out_specs=[vmem] * len(outs),
+        out_shape=outs,
         scratch_shapes=[
             pltpu.VMEM((len(parts) * depth * subs, LANES), F32),
             pltpu.VMEM((out_blocks + 8, LANES), F32),
@@ -297,9 +341,9 @@
     )(own, *far)
 
 
-def fold_kernel(periods, trials, owners, widths, width_ref, mine_ref, *refs):
-    parts, (ffa_ref, box_ref) = refs[: owners - 1], refs[owners - 1 : owners + 1]
-    rows_in, code, folded = refs[owners + 1 :]
+def fold_kernel(periods, trials, owners, widths, band_ref, weight_ref, mine_ref, *refs):
+    parts, (ffa_hbm, box_hbm) = refs[: owners - 1], refs[owners - 1 : owners + 1]
+    rows_in, code, left, ffa_ref, box_ref, ffa_sem, box_sem = refs[owners + 1 :]
     here = lax.axis_index("tm")
     bin_blocks = ROW_BLOCKS // owners
     row_len = (bin_blocks + 1) * trials
@@ -323,18 +367,11 @@
         first = (here ^ flip) * held
         rows_in[pl.ds(first, row_len), :] += early
 
-    tap = lax.broadcasted_iota(jnp.int32, (2 * LANES, LANES), 0) - lax.broadcasted_iota(
-        jnp.int32, (2 * LANES, LANES), 1
-    )
-    bands, weights = [], []
-    for w in range(widths):
-        width = width_ref[w]
-        inside = jnp.logical_and(tap >= 0, tap < width)
-        bands.append(jnp.where(inside, 1.0, 0.0).astype(jnp.bfloat16))
-        weights.append(1.0 / jnp.sqrt(jnp.full((trials, LANES), width, jnp.int32).astype(F32)))
-    band = jnp.concatenate(bands, axis=1)
+    band = band_ref[...]
+    weights = [weight_ref[8 * w : 8 * w + trials, :] for w in range(widths)]
     lane = lane_iota(trials)
     row_count = owners * periods
+    copies = []
 
     def moved(row, by):
         if by == 0:
@@ -345,6 +382,15 @@
             after = rolled[min(b + 1, bin_blocks)]
             out.append(jnp.where(lane < LANES - by, rolled[b], after))
         return out
+
+    def leave(held_ref, hbm, sem, per_trial, first, size):
+        for k in range(trials):
+            at = pl.ds(k * per_trial + first, size)
+            piece = k * (per_trial // size) + first // size
+            copies.append(
+                pltpu.make_async_copy(held_ref.at[at, :], hbm.at[at, :], sem.at[piece])
+            )
+            copies[-1].start()
 
     for group in range(row_count // GROUP):
         rows = []
@@ -367,58 +413,67 @@
             rows = new
         for r in range(GROUP):
             row = group * GROUP + r
-            for b in range(bin_blocks + 1):
-                at = (b * GROUP + r) * trials
-                folded[at : at + trials, :] = rows[r][b]
-                if b < bin_blocks:
-                    first = (row // 8 * bin_blocks + b) * 8 + row % 8
-                    step = row_count * bin_blocks
-                    ffa_ref[pl.ds(first, trials, stride=step), :] = rows[r][b]
-        span = GROUP * trials
-        for b in range(bin_blocks):
-            left = jnp.concatenate(
-                [folded[i * span : (i + 1) * span, :] for i in (b, b + 1)], axis=1
-            )
+            for b in range(bin_blocks):
+                at = (r * bin_blocks + b) * trials
+                left[at : at + trials, 0:LANES] = rows[r][b]
+                left[at : at + trials, LANES : 2 * LANES] = rows[r][b + 1]
+                first = (row // 8 * bin_blocks + b) * 8 + row % 8
+                step = row_count * bin_blocks
+                ffa_ref[pl.ds(first, trials, stride=step), :] = rows[r][b]
+        per_trial = row_count * bin_blocks
+        size = GROUP * bin_blocks
+        leave(ffa_ref, ffa_hbm, ffa_sem, per_trial, group * size, size)
+        for start in range(0, GROUP, BOX_ROWS):
+            lines = bin_blocks * trials
+            rest = left[start * lines : (start + BOX_ROWS) * lines, :]
             product = None
-            for _ in range(3):
-                high = left.astype(jnp.bfloat16)
-                left = left - high.astype(F32)
+            for _ in range(2):
+                high = rest.astype(jnp.bfloat16)
+                rest = rest - high.astype(F32)
                 term = jnp.dot(high, band, preferred_element_type=F32)
                 product = term if product is None else product + term
-            for r in range(GROUP):
-                row = group * GROUP + r
+            step = row_count * bin_blocks * widths
+            for i in range(BOX_ROWS * bin_blocks):
                 for w in range(widths):
                     value = product[
-                        r * trials : (r + 1) * trials, w * LANES : (w + 1) * LANES
+                        i * trials : (i + 1) * trials, w * LANES : (w + 1) * LANES
                     ]
-                    first = (row * bin_blocks + b) * widths + w
-                    step = row_count * bin_blocks * widths
+                    line = (group * GROUP + start) * bin_blocks + i
+                    first = line * widths + w
                     box_ref[pl.ds(first, trials, stride=step), :] = value * weights[w]
-
-
-def fold_and_box(mine, parts, box_width, periods, trials, owners):
+            size = BOX_ROWS * bin_blocks * widths
+            leave(box_ref, box_hbm, box_sem, step, (group * GROUP + start) // BOX_ROWS * size, size)
+    for copy in copies:
+        copy.wait()
+
+
+def fold_and_box(mine, parts, taps, periods, trials, owners):
     bin_blocks = ROW_BLOCKS // owners
-    widths = box_width.shape[0]
+    widths = taps[0].shape[1] // LANES
     row_count = owners * periods
     row_len = (bin_blocks + 1) * trials
     ffa_rows = trials * row_count * bin_blocks
+    ffa_shape = jax.ShapeDtypeStruct((ffa_rows, LANES), F32)
+    box_shape = jax.ShapeDtypeStruct((ffa_rows * widths, LANES), F32)
     vmem = pl.BlockSpec(memory_space=pltpu.VMEM)
+    anywhere = pl.BlockSpec(memory_space=pl.ANY)
     ffa, box = pl.pallas_call(
         functools.partial(fold_kernel, periods, trials, owners, widths),
-        in_specs=[pl.BlockSpec(memory_space=pltpu.SMEM)] + [vmem] * owners,
-        out_specs=[vmem, vmem],
-        out_shape=[
-            jax.ShapeDtypeStruct((ffa_rows, LANES), F32),
-            jax.ShapeDtypeStruct((ffa_rows * widths, LANES), F32),
-        ],
+        in_specs=[vmem] * (2 + owners),
+        out_specs=[anywhere, anywhere],
+        out_shape=[ffa_shape, box_shape],
         scratch_shapes=[
             pltpu.VMEM(((row_count + 1) * row_len, LANES), F32),
             pltpu.VMEM((max(owners - 1, 1), (periods + 1) * row_len, LANES), F32),
-            pltpu.VMEM((GROUP * row_len, LANES), F32),
+            pltpu.VMEM((GROUP * bin_blocks * trials, 2 * LANES), F32),
+            pltpu.VMEM(ffa_shape.shape, F32),
+            pltpu.VMEM(box_shape.shape, F32),
+            pltpu.SemaphoreType.DMA((trials * row_count // GROUP,)),
+            pltpu.SemaphoreType.DMA((trials * row_count // BOX_ROWS,)),
         ],
         compiler_params=pltpu.CompilerParams(vmem_limit_bytes=VMEM_LIMIT),
         name="fold",
-    )(box_width, mine, *parts)
+    )(*taps, mine, *parts)
     bins = bin_blocks * LANES
     ffa = ffa.reshape(trials, row_count // 8, bin_blocks, 8, LANES)
     ffa = ffa.transpose(0, 1, 3, 2, 4).reshape(trials, row_count, bins)
@@ -439,7 +494,7 @@
         part[flip] = lax.ppermute(own, "chan", pairs(chan_size, flip))
     sizes = (blocks, subs, trials)
     flips = tuple(range(quad, chan_size, quad))
-    early, final = ((0, 2), (1, 3)) if quad == 4 else ((0,), tuple(range(1, quad)))
+    early, final = ((0, 2, 1), (3,)) if quad == 4 else ((0,), tuple(range(1, quad)))
     far, near = None, None
     for origin in early:
         both = origin == 0
@@ -454,13 +509,15 @@
         for send, flip in zip(far, flips)
     ]
     rest = (*early[1:], *final)
-    (near,) = trial_sums([part[o] for o in rest], rest, sub_delay, sizes, (0,), near)
+    near, *taps = trial_sums(
+        [part[o] for o in rest], rest, sub_delay, sizes, (0,), near, box_width=box_width
+    )
     mine, *sends = cut_by_phase(near, far, blocks, trials, owners)
     got = [
         lax.ppermute(send, "tm", pairs(owners, flip + 1))
         for flip, send in enumerate(sends)
     ]
-    return fold_and_box(mine, got, box_width, periods, trials, owners)
+    return fold_and_box(mine, got, taps, periods, trials, owners)
 
 
 def solution(mesh):

time: 39.1 us -> 35.8 us (0.916)
  waiting for transfers between devices: 11.3 us -> 7.71 us
    ppermute x1, waiting for transfers between devices: 3.77 us -> 1.29 us  [per_device(): lax.ppermute(send, 'chan', pairs(chan_size, flip))]
    pallas_call x4 -> x5, Pallas kernels: 8.09 us -> 9.38 us  [trial_sums(): pl.pallas_call(functools.partial(trial_kernel, *sizes, tuple(origins), tu...]
    ppermute x3, waiting for transfers between devices: 4.06 us -> 2.94 us  [per_device(): part[flip] = lax.ppermute(own, 'chan', pairs(chan_size, flip))]
    pallas_call x1, Pallas kernels: 2.94 us -> 2.34 us  [fold_and_box(): pl.pallas_call(functools.partial(fold_kernel, periods, trials, owners, wi...]
    pallas_call x1, Pallas kernels: 6.53 us -> 6.07 us  [subband_sums(): pl.pallas_call(functools.partial(subband_kernel, chans, blocks, subs), in...]
  transfers between devices with their start and end apart: 7 -> 7, of which waited for: 6 -> 5; matrix products, arithmetic and copies ran while one was open for 0% -> 0% of each run, Pallas kernels for 15% -> 22%
where the time goes in v4:
time: 35.8 us; the launch traced here: 35.6 us
  Pallas kernels  18 us (50%)
  starting transfers between devices  9.22 us (26%)
  waiting for transfers between devices  7.71 us (22%)
  between operations  0.72 us (2%)
    pallas_call x5, Pallas kernels, trial_sums(): pl.pallas_call(functools.partial(trial_kernel, *sizes, tuple(origins), tu...  9.38 us
    pallas_call x1, Pallas kernels, subband_sums(): pl.pallas_call(functools.partial(subband_kernel, chans, blocks, subs), in...  6.07 us
    ppermute x3, starting transfers between devices, per_device(): part[flip] = lax.ppermute(own, 'chan', pairs(chan_size, flip))  4.63 us
    ppermute x3, waiting for transfers between devices, per_device(): lax.ppermute(send, 'tm', pairs(owners, flip + 1))  3.48 us
    ppermute x3, waiting for transfers between devices, per_device(): part[flip] = lax.ppermute(own, 'chan', pairs(chan_size, flip))  2.94 us
    ppermute x1, starting transfers between devices, per_device(): lax.ppermute(send, 'chan', pairs(chan_size, flip))  2.65 us
    pallas_call x1, Pallas kernels, fold_and_box(): pl.pallas_call(functools.partial(fold_kernel, periods, trials, owners, wi...  2.34 us
    ppermute x3, starting transfers between devices, per_device(): lax.ppermute(send, 'tm', pairs(owners, flip + 1))  1.93 us
  transfers between devices with their start and end apart: 7, of which 5 were waited for; matrix products, arithmetic and copies ran while one was open for 0% of the time, Pallas kernels for 22%

profile of v4, /device:TPU:0, one launch (start us, length us, event | category | flops | bytes accessed | tf_op | source)
XLA Modules:
  0.0 35.6 jit_solution(16801381670305238523)
XLA Ops:
  0.6 0.0 copy-start
  0.6 0.0 copy-start.1
  0.7 6.1 %subbands.1.refs_0_ = s16[528,128]{1,0:T(8,128)(2,1)S(1)} custom-call(s32[512]{0:T(512)} %delay_hbm.1, bf16[512,8192]{1,0:T(8,128)(2,1)} %x_hbm.1), custom_call_target="tpu_custom_call" | custom-call | tf_op jit(solution)/shard_map/subbands/pallas_call | solution.py:126
  6.7 3.1 %collective-permute-start = (s16[528,128]{1,0:T(8,128)(2,1)S(1)}, s16[528,128]{1,0:T(8,128)(2,1)S(1)}, u32[]{:S(2)}, u32[]{:S(2)}) collective-permute-start(s16[528,128]{1,0:T(8,128)(2,1)S(1)} %subbands.1.refs_0_), channel_id=1, source_target_pairs={{0,8},{4,12},{8,0},{12,4},{16,24},{20,28},{24,16},{28,20},{1,9},{5... | collective-permute-start | bytes 405512 | tf_op jit(solution)/shard_map/ppermute | solution.py:494
  9.8 1.5 %collective-permute-start.1 = (s16[528,128]{1,0:T(8,128)(2,1)S(1)}, s16[528,128]{1,0:T(8,128)(2,1)S(1)}, u32[]{:S(2)}, u32[]{:S(2)}) collective-permute-start(s16[528,128]{1,0:T(8,128)(2,1)S(1)} %subbands.1.refs_0_), channel_id=1, source_target_pairs={{0,4},{4,0},{8,12},{12,8},{16,20},{20,16},{24,28},{28,24},{1,5},{5... | collective-permute-start | bytes 405512 | tf_op jit(solution)/shard_map/ppermute | solution.py:494
  11.3 0.0 collective-permute-start.2
  11.4 2.1 %trials.4 = (f32[576,128]{1,0:T(8,128)S(1)}, f32[576,128]{1,0:T(8,128)S(1)}) custom-call(s32[64,64]{1,0:T(8,128)S(1)} %copy-done, s16[528,128]{1,0:T(8,128)(2,1)S(1)} %subbands.1.refs_0_), custom_call_target="tpu_custom_call" | custom-call | tf_op jit(solution)/shard_map/trials/pallas_call | solution.py:269
  13.5 0.4 %collective-permute-done.refs_0_ = s16[528,128]{1,0:T(8,128)(2,1)S(1)} collective-permute-done((s16[528,128]{1,0:T(8,128)(2,1)S(1)}, s16[528,128]{1,0:T(8,128)(2,1)S(1)}, u32[]{:S(2)}, u32[]{:S(2)}) %collective-permute-start) | collective-permute-done | bytes 135200 | tf_op jit(solution)/shard_map/ppermute | solution.py:494
  13.8 1.4 %trials.6.refs_1_ = f32[576,128]{1,0:T(8,128)S(1)} custom-call(s32[64,64]{1,0:T(8,128)S(1)} %copy-done, s16[528,128]{1,0:T(8,128)(2,1)S(1)} %collective-permute-done.refs_0_, f32[576,128]{1,0:T(8,128)S(1)} %get-tuple-element.17.refs_1_), custom_call_target="tpu_custom_call" | custom-call | tf_op jit(solution)/shard_map/trials/pallas_call | solution.py:269
  15.2 2.6 %collective-permute-done.1.refs_1_.refs_0_ = s16[528,128]{1,0:T(8,128)(2,1)S(1)} collective-permute-done((s16[528,128]{1,0:T(8,128)(2,1)S(1)}, s16[528,128]{1,0:T(8,128)(2,1)S(1)}, u32[]{:S(2)}, u32[]{:S(2)}) %collective-permute-start.1) | collective-permute-done | bytes 135200 | tf_op jit(solution)/shard_map/ppermute | solution.py:494
  17.8 1.4 %trials.7.refs_1_ = f32[576,128]{1,0:T(8,128)S(1)} custom-call(s32[64,64]{1,0:T(8,128)S(1)} %copy-done, s16[528,128]{1,0:T(8,128)(2,1)S(1)} %collective-permute-done.1.refs_1_.refs_0_, f32[576,128]{1,0:T(8,128)S(1)} %trials.6.refs_1_), custom_call_target="tpu_custom_call" | custom-call | tf_op jit(solution)/shard_map/trials/pallas_call | solution.py:269
  19.1 0.0 collective-permute-done.2.refs_2_.refs_0_
  19.1 1.4 %trials_coded.1 = s16[584,128]{1,0:T(8,128)(2,1)S(1)} custom-call(s32[64,64]{1,0:T(8,128)S(1)} %copy-done, s16[528,128]{1,0:T(8,128)(2,1)S(1)} %collective-permute-done.2.refs_2_.refs_0_, f32[576,128]{1,0:T(8,128)S(1)} %trials.7.refs_1_), custom_call_target="tpu_custom_call" | custom-call | tf_op jit(solution)/shard_map/trials_coded/pallas_call | solution.py:269
  20.6 2.7 %collective-permute-start.3 = (s16[584,128]{1,0:T(8,128)(2,1)S(1)}, s16[584,128]{1,0:T(8,128)(2,1)S(1)}, u32[]{:S(2)}, u32[]{:S(2)}) collective-permute-start(s16[584,128]{1,0:T(8,128)(2,1)S(1)} %trials_coded.1), channel_id=1, source_target_pairs={{0,16},{4,20},{8,24},{12,28},{16,0},{20,4},{24,8},{28,12},{1,17},{... | collective-permute-start | bytes 448520 | tf_op jit(solution)/shard_map/ppermute | solution.py:508
  23.3 3.1 %trials.5 = (f32[576,128]{1,0:T(8,128)S(1)}, bf16[256,512]{1,0:T(8,128)(2,1)S(1)}, f32[32,128]{1,0:T(8,128)S(1)}) custom-call(s32[64,64]{1,0:T(8,128)S(1)} %copy-done, s16[528,128]{1,0:T(8,128)(2,1)S(1)} %collective-permute-done.refs_0_, s16[528,128]{1,0:T(8,128)(2,1)S(1)} %collective-permute-done.1.refs_1_.refs_0_, ...), custom_call_target="tpu_custom_call" | custom-call | tf_op jit(solution)/shard_map/trials/pallas_call | solution.py:269
  26.4 1.3 %collective-permute-done.3.refs_0_ = s16[584,128]{1,0:T(8,128)(2,1)S(1)} collective-permute-done((s16[584,128]{1,0:T(8,128)(2,1)S(1)}, s16[584,128]{1,0:T(8,128)(2,1)S(1)}, u32[]{:S(2)}, u32[]{:S(2)}) %collective-permute-start.3) | collective-permute-done | bytes 149536 | tf_op jit(solution)/shard_map/ppermute | solution.py:508
  27.7 0.2 cut.1
  27.9 0.1 collective-permute-start.4
  28.0 1.6 %collective-permute-start.5 = (s16[208,128]{1,0:T(8,128)(2,1)S(1)}, s16[208,128]{1,0:T(8,128)(2,1)S(1)}, u32[]{:S(2)}, u32[]{:S(2)}) collective-permute-start(s16[208,128]{1,0:T(8,128)(2,1)S(1)} %get-tuple-element.20), channel_id=1, source_target_pairs={{0,2},{1,3},{2,0},{3,1},{4,6},{5,7},{6,4},{7,5},{8,10},{9,11},{10,... | collective-permute-start | bytes 159752 | tf_op jit(solution)/shard_map/ppermute | solution.py:517
  29.5 0.3 collective-permute-start.6
  29.8 0.0 collective-permute-done.4.refs_0_
  29.8 2.4 %collective-permute-done.5.refs_1_ = s16[208,128]{1,0:T(8,128)(2,1)S(1)} collective-permute-done((s16[208,128]{1,0:T(8,128)(2,1)S(1)}, s16[208,128]{1,0:T(8,128)(2,1)S(1)}, u32[]{:S(2)}, u32[]{:S(2)}) %collective-permute-start.5) | collective-permute-done | bytes 53280 | tf_op jit(solution)/shard_map/ppermute | solution.py:517
  32.2 1.1 %collective-permute-done.6.refs_2_ = s16[208,128]{1,0:T(8,128)(2,1)S(1)} collective-permute-done((s16[208,128]{1,0:T(8,128)(2,1)S(1)}, s16[208,128]{1,0:T(8,128)(2,1)S(1)}, u32[]{:S(2)}, u32[]{:S(2)}) %collective-permute-start.6) | collective-permute-done | bytes 53280 | tf_op jit(solution)/shard_map/ppermute | solution.py:517
  33.3 2.3 %fold.1 = (f32[512,128]{1,0:T(8,128)}, f32[2048,128]{1,0:T(8,128)}) custom-call(bf16[256,512]{1,0:T(8,128)(2,1)S(1)} %get-tuple-element.14.band_ref, f32[32,128]{1,0:T(8,128)S(1)} %get-tuple-element.15.weight_ref, f32[200,128]{1,0:T(8,128)S(1)} %get-tuple-element.18.mine_ref, s16[208,128]{1,0:T(8,128)(2,1)S(1)} %collective-permute-done.4.refs_0_, ...), custom_call_target="tpu_custom_call" | custom-call | tf_op jit(solution)/shard_map/fold/pallas_call | solution.py:460
  (2 shorter events, 0.0 us)
Async XLA Ops:
  0.6 10.7 %copy-start = (s32[64,64]{1,0:T(8,128)S(1)}, s32[64,64]{1,0:T(8,128)}, u32[]{:S(2)}) copy-start(s32[64,64]{1,0:T(8,128)} %delays.9) | copy-start | bytes 49156
  0.6 22.6 %copy-start.1 = (s32[4]{0:T(128)S(1)}, s32[4]{0:T(128)}, u32[]{:S(2)}) copy-start(s32[4]{0:T(128)} %refs_4_.1) | copy-start | bytes 52
  6.7 7.1 %collective-permute-start = (s16[528,128]{1,0:T(8,128)(2,1)S(1)}, s16[528,128]{1,0:T(8,128)(2,1)S(1)}, u32[]{:S(2)}, u32[]{:S(2)}) collective-permute-start(s16[528,128]{1,0:T(8,128)(2,1)S(1)} %subbands.1.refs_0_), channel_id=1, source_target_pairs={{0,8},{4,12},{8,0},{12,4},{16,24},{20,28},{24,16},{28,20},{1,9},{5... | collective-permute-start | bytes 405512 | tf_op jit(solution)/shard_map/ppermute | solution.py:494
  9.8 7.9 %collective-permute-start.1 = (s16[528,128]{1,0:T(8,128)(2,1)S(1)}, s16[528,128]{1,0:T(8,128)(2,1)S(1)}, u32[]{:S(2)}, u32[]{:S(2)}) collective-permute-start(s16[528,128]{1,0:T(8,128)(2,1)S(1)} %subbands.1.refs_0_), channel_id=1, source_target_pairs={{0,4},{4,0},{8,12},{12,8},{16,20},{20,16},{24,28},{28,24},{1,5},{5... | collective-permute-start | bytes 405512 | tf_op jit(solution)/shard_map/ppermute | solution.py:494
  11.3 7.8 %collective-permute-start.2 = (s16[528,128]{1,0:T(8,128)(2,1)S(1)}, s16[528,128]{1,0:T(8,128)(2,1)S(1)}, u32[]{:S(2)}, u32[]{:S(2)}) collective-permute-start(s16[528,128]{1,0:T(8,128)(2,1)S(1)} %subbands.1.refs_0_), channel_id=1, source_target_pairs={{0,12},{4,8},{8,4},{12,0},{16,28},{20,24},{24,20},{28,16},{1,13},{... | collective-permute-start | bytes 405512 | tf_op jit(solution)/shard_map/ppermute | solution.py:494
  20.6 7.1 %collective-permute-start.3 = (s16[584,128]{1,0:T(8,128)(2,1)S(1)}, s16[584,128]{1,0:T(8,128)(2,1)S(1)}, u32[]{:S(2)}, u32[]{:S(2)}) collective-permute-start(s16[584,128]{1,0:T(8,128)(2,1)S(1)} %trials_coded.1), channel_id=1, source_target_pairs={{0,16},{4,20},{8,24},{12,28},{16,0},{20,4},{24,8},{28,12},{1,17},{... | collective-permute-start | bytes 448520 | tf_op jit(solution)/shard_map/ppermute | solution.py:508
  27.9 1.9 %collective-permute-start.4 = (s16[208,128]{1,0:T(8,128)(2,1)S(1)}, s16[208,128]{1,0:T(8,128)(2,1)S(1)}, u32[]{:S(2)}, u32[]{:S(2)}) collective-permute-start(s16[208,128]{1,0:T(8,128)(2,1)S(1)} %get-tuple-element.19), channel_id=1, source_target_pairs={{0,1},{1,0},{2,3},{3,2},{4,5},{5,4},{6,7},{7,6},{8,9},{9,8},{10,11... | collective-permute-start | bytes 159752 | tf_op jit(solution)/shard_map/ppermute | solution.py:517
  28.0 4.2 %collective-permute-start.5 = (s16[208,128]{1,0:T(8,128)(2,1)S(1)}, s16[208,128]{1,0:T(8,128)(2,1)S(1)}, u32[]{:S(2)}, u32[]{:S(2)}) collective-permute-start(s16[208,128]{1,0:T(8,128)(2,1)S(1)} %get-tuple-element.20), channel_id=1, source_target_pairs={{0,2},{1,3},{2,0},{3,1},{4,6},{5,7},{6,4},{7,5},{8,10},{9,11},{10,... | collective-permute-start | bytes 159752 | tf_op jit(solution)/shard_map/ppermute | solution.py:517
  29.5 3.8 %collective-permute-start.6 = (s16[208,128]{1,0:T(8,128)(2,1)S(1)}, s16[208,128]{1,0:T(8,128)(2,1)S(1)}, u32[]{:S(2)}, u32[]{:S(2)}) collective-permute-start(s16[208,128]{1,0:T(8,128)(2,1)S(1)} %get-tuple-element.21), channel_id=1, source_target_pairs={{0,3},{1,2},{2,1},{3,0},{4,7},{5,6},{6,5},{7,4},{8,11},{9,10},{10,... | collective-permute-start | bytes 159752 | tf_op jit(solution)/shard_map/ppermute | solution.py:517

commit v5 on v4

--- a/solution.py
+++ b/solution.py
@@ -155,100 +155,121 @@
         weight_ref[8 * w : 8 * w + 8, :] = 1.0 / jnp.sqrt(count)
 
 
-def trial_kernel(
-    blocks, subs, trials, origins, flips, primed, coded, taps, delays, *refs
-):
+def trial_kernel(blocks, subs, trials, sides, primed, coded, taps, delays, *refs):
     refs = list(refs)
     take = lambda n: [refs.pop(0) for _ in range(n)]
-    parts = take(len(origins))
-    priors = take(len(flips)) if primed else []
+    n_in, n_out = (len(each) for each in sides[0])
+    parts = take(n_in)
+    priors = take(n_out) if primed else [None] * n_out
     width_ref = take(1)[0] if taps else None
-    outs = take(len(flips))
+    outs = take(n_out)
     if taps:
         box_taps(width_ref, *take(2))
     spread, late, acc, delay_ref, delay_sem = refs
     chan = lax.axis_index("chan")
+    out_blocks = LEAD + blocks
+    depth = out_blocks + LEAD
     fetched = delay_ref.shape[1]
-    copies, offset = [], []
-    for i, flip in enumerate(flips):
-        wanted = (chan ^ flip) * trials
-        first = wanted // fetched * fetched
-        offset.append(wanted - first)
-        copies.append(
-            pltpu.make_async_copy(
+    lane = lane_iota(8)
+    tiles = out_blocks // 8
+
+    def on_side(origins, flips):
+        copies, offset = {}, {}
+        for i, flip in enumerate(flips):
+            if flip is None:
+                continue
+            wanted = (chan ^ flip) * trials
+            first = wanted // fetched * fetched
+            offset[i] = wanted - first
+            copies[i] = pltpu.make_async_copy(
                 delays.at[pl.ds(pl.multiple_of(first, 8), fetched), :],
                 delay_ref.at[i],
                 delay_sem.at[i],
             )
-        )
-        copies[i].start()
-    out_blocks = LEAD + blocks
-    depth = out_blocks + LEAD
-    for at, part in enumerate(parts):
-        base = at * depth * subs
-        rows = (blocks + 1) * subs
-        scale = jnp.exp2(part[rows : rows + subs, :].astype(F32))
-        lead = (LEAD - 1) * subs
-        spread[base : base + lead, :] = jnp.zeros((lead, LANES), F32)
-        tail = base + lead + rows
-        spread[tail : base + depth * subs, :] = jnp.zeros(
-            (depth * subs - lead - rows, LANES), F32
-        )
-        values = part[0:rows, :].astype(F32).reshape(blocks + 1, subs, LANES)
-        spread[base + lead : tail, :] = (values * scale[None]).reshape(rows, LANES)
-
-    lane = lane_iota(8)
-    tiles = out_blocks // 8
-
-    for copy in copies:
-        copy.wait()
-
-    def one_trial(trial, i, prior, out):
-        here = [jnp.zeros((8, LANES), F32)] * tiles
-        before = [jnp.zeros((8, LANES), F32)] * tiles
-        for at, origin in enumerate(origins):
-            for sub in range(subs):
-                delay = delay_ref[i, offset[i] + trial, (chan ^ origin) * subs + sub]
-                shift = delay & (LANES - 1)
-                stays = lane < LANES - shift
-                back = (LANES - shift) & (LANES - 1)
-                for t in range(tiles):
-                    first = (at * depth + (delay >> 7) + 8 * t) * subs + sub
-                    value = spread[pl.ds(first, 8, stride=subs), :]
-                    value = pltpu.roll(value, back, 1)
-                    here[t] = here[t] + jnp.where(stays, value, 0.0)
-                    before[t] = before[t] + jnp.where(stays, 0.0, value)
-        for t in range(tiles):
-            late[8 * t : 8 * t + 8, :] = before[t]
-        late[out_blocks : out_blocks + 8, :] = jnp.zeros((8, LANES), F32)
-        for t in range(tiles):
-            rows = pl.ds(8 * t * trials + trial, 8, stride=trials)
-            value = here[t] + late[8 * t + 1 : 8 * t + 9, :]
-            out[rows, :] = value if prior is None else value + prior[rows, :]
-
-    rows = out_blocks * trials
-    for i, (flip, out) in enumerate(zip(flips, outs)):
-        target = acc if coded else out
-
-        @pl.loop(0, trials, unroll=trials)
-        def _(trial):
-            one_trial(trial, i, priors[i] if primed else None, target)
-
-        if coded:
-            values = acc[...].reshape(out_blocks, trials, LANES)
-            exponent = column_exponent(jnp.max(jnp.abs(values), axis=0))
-            out[0:rows, :] = to_i16(
-                scaled(values, exponent[None]).reshape(rows, LANES)
+            copies[i].start()
+        for at, (origin, part) in enumerate(zip(origins, parts)):
+            if origin is None:
+                continue
+            base = at * depth * subs
+            rows = (blocks + 1) * subs
+            scale = jnp.exp2(part[rows : rows + subs, :].astype(F32))
+            lead = (LEAD - 1) * subs
+            spread[base : base + lead, :] = jnp.zeros((lead, LANES), F32)
+            tail = base + lead + rows
+            spread[tail : base + depth * subs, :] = jnp.zeros(
+                (depth * subs - lead - rows, LANES), F32
             )
-            out[rows : rows + trials, :] = to_i16(exponent)
+            values = part[0:rows, :].astype(F32).reshape(blocks + 1, subs, LANES)
+            spread[base + lead : tail, :] = (values * scale[None]).reshape(rows, LANES)
+        for copy in copies.values():
+            copy.wait()
+
+        def one_trial(trial, i, prior, out):
+            here = [jnp.zeros((8, LANES), F32)] * tiles
+            before = [jnp.zeros((8, LANES), F32)] * tiles
+            for at, origin in enumerate(origins):
+                if origin is None:
+                    continue
+                for sub in range(subs):
+                    column = (chan ^ origin) * subs + sub
+                    delay = delay_ref[i, offset[i] + trial, column]
+                    shift = delay & (LANES - 1)
+                    stays = lane < LANES - shift
+                    back = (LANES - shift) & (LANES - 1)
+                    for t in range(tiles):
+                        first = (at * depth + (delay >> 7) + 8 * t) * subs + sub
+                        value = spread[pl.ds(first, 8, stride=subs), :]
+                        value = pltpu.roll(value, back, 1)
+                        here[t] = here[t] + jnp.where(stays, value, 0.0)
+                        before[t] = before[t] + jnp.where(stays, 0.0, value)
+            for t in range(tiles):
+                late[8 * t : 8 * t + 8, :] = before[t]
+            late[out_blocks : out_blocks + 8, :] = jnp.zeros((8, LANES), F32)
+            for t in range(tiles):
+                rows = pl.ds(8 * t * trials + trial, 8, stride=trials)
+                value = here[t] + late[8 * t + 1 : 8 * t + 9, :]
+                out[rows, :] = value if prior is None else value + prior[rows, :]
+
+        rows = out_blocks * trials
+        nothing_new = all(origin is None for origin in origins)
+        for i, (flip, prior, out) in enumerate(zip(flips, priors, outs)):
+            if flip is None:
+                continue
+            result = acc if coded else out
+            if nothing_new:
+                result = prior
+            else:
+
+                @pl.loop(0, trials, unroll=trials)
+                def _(trial):
+                    one_trial(trial, i, prior, result)
+
+            if coded:
+                values = result[...].reshape(out_blocks, trials, LANES)
+                exponent = column_exponent(jnp.max(jnp.abs(values), axis=0))
+                out[0:rows, :] = to_i16(
+                    scaled(values, exponent[None]).reshape(rows, LANES)
+                )
+                out[rows : rows + trials, :] = to_i16(exponent)
+            elif nothing_new:
+                out[...] = prior[...]
+
+    if sides[0] == sides[1]:
+        on_side(*sides[0])
+    else:
+        core = lax.axis_index("tm") & 1
+        for each, side in enumerate(sides):
+
+            @pl.when(core == each)
+            def _():
+                on_side(*side)
 
 
 def trial_sums(
     parts, origins, sub_delay, sizes, flips, priors=None, coded=False, box_width=None
 ):
-    if not flips:
-        return []
     blocks, subs, trials = sizes
+    n_out = len(flips[0])
     out_blocks = LEAD + blocks
     depth = out_blocks + LEAD
     rows = out_blocks * trials
@@ -258,7 +279,7 @@
     vmem = pl.BlockSpec(memory_space=pltpu.VMEM)
     arrays = [*parts, *(priors or [])]
     in_specs = [pl.BlockSpec(memory_space=pl.ANY)] + [vmem] * len(arrays)
-    outs = [out] * len(flips)
+    outs = [out] * n_out
     taps = box_width is not None
     if taps:
         widths = box_width.shape[0]
@@ -268,7 +289,7 @@
         outs.append(jax.ShapeDtypeStruct((widths * 8, LANES), F32))
     return pl.pallas_call(
         functools.partial(
-            trial_kernel, *sizes, tuple(origins), tuple(flips), bool(priors), coded, taps
+            trial_kernel, *sizes, tuple(zip(origins, flips)), bool(priors), coded, taps
         ),
         in_specs=in_specs,
         out_specs=[vmem] * len(outs),
@@ -277,8 +298,8 @@
             pltpu.VMEM((len(parts) * depth * subs, LANES), F32),
             pltpu.VMEM((out_blocks + 8, LANES), F32),
             pltpu.VMEM((rows, LANES), F32),
-            pltpu.SMEM((len(flips), max(trials, 8), sub_delay.shape[1]), jnp.int32),
-            pltpu.SemaphoreType.DMA((len(flips),)),
+            pltpu.SMEM((n_out, max(trials, 8), sub_delay.shape[1]), jnp.int32),
+            pltpu.SemaphoreType.DMA((n_out,)),
         ],
         compiler_params=pltpu.CompilerParams(vmem_limit_bytes=VMEM_LIMIT),
         name="trials_coded" if coded else "trials",
@@ -487,30 +508,47 @@
     samples = filterbank.shape[1]
     subs, trials = NSUB // chan_size, NDM // chan_size
     blocks, periods = samples // LANES, samples // NBIN
+    own = subband_sums(filterbank, chan_delay, subs)
+
     quad = math.gcd(chan_size, 4)
-    own = subband_sums(filterbank, chan_delay, subs)
-    part = {0: own}
-    for flip in range(1, quad):
-        part[flip] = lax.ppermute(own, "chan", pairs(chan_size, flip))
+    near_by, across = list(range(1, quad)), list(range(quad, chan_size, quad))
+    slots = max(len(near_by), len(across))
+    near_by += [None] * (slots - len(near_by))
+    across += [None] * (slots - len(across))
+    origins, targets = (across, near_by), (near_by, across)
+
+    def swapped(array, flips):
+        route = []
+        for tm in range(owners):
+            if flips[tm & 1] is not None:
+                for chan in range(chan_size):
+                    route.append(
+                        (chan * owners + tm, (chan ^ flips[tm & 1]) * owners + tm)
+                    )
+        return lax.ppermute(array, ("chan", "tm"), route)
+
+    got = [
+        swapped(own, (origins[0][slot], origins[1][slot])) for slot in range(slots)
+    ]
     sizes = (blocks, subs, trials)
-    flips = tuple(range(quad, chan_size, quad))
-    early, final = ((0, 2, 1), (3,)) if quad == 4 else ((0,), tuple(range(1, quad)))
-    far, near = None, None
-    for origin in early:
-        both = origin == 0
-        sums = trial_sums(
-            [part[origin]], (origin,), sub_delay, sizes, (*flips, 0) if both else flips, far
-        )
-        far, near = (sums[:-1], sums[-1:]) if both else (sums, near)
-    last = [part[origin] for origin in final]
-    far = trial_sums(last, final, sub_delay, sizes, flips, far, True)
+    sends = tuple(map(tuple, targets))
+    both = lambda *values: (values, values)
+    first = lambda at, until: tuple(tuple(each[at:until]) for each in origins)
+    *sums, near = trial_sums(
+        [own], both(0), sub_delay, sizes, tuple((*each, 0) for each in sends)
+    )
+    if slots > 1:
+        sums = trial_sums(got[:1], first(0, 1), sub_delay, sizes, sends, sums)
+    rest = min(slots - 1, 1)
+    sums = trial_sums(
+        got[rest:], first(rest, slots), sub_delay, sizes, sends, sums, True
+    )
     far = [
-        lax.ppermute(send, "chan", pairs(chan_size, flip))
-        for send, flip in zip(far, flips)
+        swapped(part, (targets[0][slot], targets[1][slot]))
+        for slot, part in enumerate(sums)
     ]
-    rest = (*early[1:], *final)
     near, *taps = trial_sums(
-        [part[o] for o in rest], rest, sub_delay, sizes, (0,), near, box_width=box_width
+        got, first(0, slots), sub_delay, sizes, both(0), [near], box_width=box_width
     )
     mine, *sends = cut_by_phase(near, far, blocks, trials, owners)
     got = [

time: 35.8 us -> 41 us (1.15)
  starting transfers between devices: 9.22 us -> 14.7 us
  waiting for transfers between devices: 7.71 us -> 6.93 us
    ppermute x4 -> x6, starting transfers between devices: 7.28 us -> 12.8 us  [swapped(): return lax.ppermute(array, ('chan', 'tm'), route)]
    ppermute x4 -> x6, waiting for transfers between devices: 4.23 us -> 3.46 us  [swapped(): return lax.ppermute(array, ('chan', 'tm'), route)]
    pallas_call x5 -> x4, Pallas kernels: 9.38 us -> 9.52 us  [trial_sums(): pl.pallas_call(functools.partial(trial_kernel, *sizes, tuple(zip(origins,...]
  transfers between devices with their start and end apart: 7 -> 9, of which waited for: 5 -> 4; matrix products, arithmetic and copies ran while one was open for 0% -> 0% of each run, Pallas kernels for 22% -> 21%
where the time goes in v5:
time: 41 us; the launch traced here: 40.8 us
  Pallas kernels  18.2 us (44%)
  starting transfers between devices  14.7 us (36%)
  waiting for transfers between devices  6.93 us (17%)
  between operations  0.95 us (2%)
    ppermute x6, starting transfers between devices, swapped(): return lax.ppermute(array, ('chan', 'tm'), route)  12.8 us
    pallas_call x4, Pallas kernels, trial_sums(): pl.pallas_call(functools.partial(trial_kernel, *sizes, tuple(zip(origins,...  9.52 us
    pallas_call x1, Pallas kernels, subband_sums(): pl.pallas_call(functools.partial(subband_kernel, chans, blocks, subs), in...  6.07 us
    ppermute x3, waiting for transfers between devices, per_device(): lax.ppermute(send, 'tm', pairs(owners, flip + 1))  3.48 us
    ppermute x6, waiting for transfers between devices, swapped(): return lax.ppermute(array, ('chan', 'tm'), route)  3.46 us
    pallas_call x1, Pallas kernels, fold_and_box(): pl.pallas_call(functools.partial(fold_kernel, periods, trials, owners, wi...  2.35 us
    ppermute x3, starting transfers between devices, per_device(): lax.ppermute(send, 'tm', pairs(owners, flip + 1))  1.93 us
  transfers between devices with their start and end apart: 9, of which 4 were waited for; matrix products, arithmetic and copies ran while one was open for 0% of the time, Pallas kernels for 21%

profile of v5, /device:TPU:0, one launch (start us, length us, event | category | flops | bytes accessed | tf_op | source)
XLA Modules:
  0.0 40.8 jit_solution(14358121698240622550)
XLA Ops:
  0.7 6.1 %subbands.1.refs_0_ = s16[528,128]{1,0:T(8,128)(2,1)S(1)} custom-call(s32[512]{0:T(512)} %delay_hbm.1, bf16[512,8192]{1,0:T(8,128)(2,1)} %x_hbm.1), custom_call_target="tpu_custom_call" | custom-call | tf_op jit(solution)/shard_map/subbands/pallas_call | solution.py:126
  6.7 4.1 %collective-permute-start = (s16[528,128]{1,0:T(8,128)(2,1)S(1)}, s16[528,128]{1,0:T(8,128)(2,1)S(1)}, u32[]{:S(2)}, u32[]{:S(2)}) collective-permute-start(s16[528,128]{1,0:T(8,128)(2,1)S(1)} %subbands.1.refs_0_), channel_id=1, source_target_pairs={{0,16},{4,20},{8,24},{12,28},{16,0},{20,4},{24,8},{28,12},{1,5},{5... | collective-permute-start | bytes 405512 | tf_op jit(solution)/shard_map/ppermute | solution.py:528
  10.8 0.7 %collective-permute-start.1 = (s16[528,128]{1,0:T(8,128)(2,1)S(1)}, s16[528,128]{1,0:T(8,128)(2,1)S(1)}, u32[]{:S(2)}, u32[]{:S(2)}) collective-permute-start(s16[528,128]{1,0:T(8,128)(2,1)S(1)} %subbands.1.refs_0_), channel_id=1, source_target_pairs={{1,9},{5,13},{9,1},{13,5},{17,25},{21,29},{25,17},{29,21},{3,11},{... | collective-permute-start | bytes 405512 | tf_op jit(solution)/shard_map/ppermute | solution.py:528
  11.5 0.7 %collective-permute-start.2 = (s16[528,128]{1,0:T(8,128)(2,1)S(1)}, s16[528,128]{1,0:T(8,128)(2,1)S(1)}, u32[]{:S(2)}, u32[]{:S(2)}) collective-permute-start(s16[528,128]{1,0:T(8,128)(2,1)S(1)} %subbands.1.refs_0_), channel_id=1, source_target_pairs={{1,13},{5,9},{9,5},{13,1},{17,29},{21,25},{25,21},{29,17},{3,15},{... | collective-permute-start | bytes 405512 | tf_op jit(solution)/shard_map/ppermute | solution.py:528
  12.2 3.5 %trials.3 = (f32[576,128]{1,0:T(8,128)S(1)}, f32[576,128]{1,0:T(8,128)S(1)}, f32[576,128]{1,0:T(8,128)S(1)}, f32[576,128]{1,0:T(8,128)S(1)}) custom-call(s32[64,64]{1,0:T(8,128)S(1)} %copy-done, s16[528,128]{1,0:T(8,128)(2,1)S(1)} %subbands.1.refs_0_), custom_call_target="tpu_custom_call" | custom-call | tf_op jit(solution)/shard_map/trials/pallas_call | solution.py:290
  15.7 0.0 collective-permute-done.refs_0_
  15.7 2.8 %trials.5 = (f32[576,128]{1,0:T(8,128)S(1)}, f32[576,128]{1,0:T(8,128)S(1)}, f32[576,128]{1,0:T(8,128)S(1)}) custom-call(s32[64,64]{1,0:T(8,128)S(1)} %copy-done, s16[528,128]{1,0:T(8,128)(2,1)S(1)} %collective-permute-done.refs_0_, f32[576,128]{1,0:T(8,128)S(1)} %get-tuple-element.25.refs_1_, f32[576,128]{1,0:T(8,128)S(1)} %get-tuple-element.26.refs_2_, ...), custom_call_target="tpu_custom_call" | custom-call | tf_op jit(solution)/shard_map/trials/pallas_call | solution.py:290
  18.6 0.0 collective-permute-done.1.refs_1_.refs_0_
  18.6 0.0 collective-permute-done.2.refs_2_.refs_1_
  18.6 1.0 %trials_coded.1 = (s16[584,128]{1,0:T(8,128)(2,1)S(1)}, s16[584,128]{1,0:T(8,128)(2,1)S(1)}, s16[584,128]{1,0:T(8,128)(2,1)S(1)}) custom-call(s32[64,64]{1,0:T(8,128)S(1)} %copy-done, s16[528,128]{1,0:T(8,128)(2,1)S(1)} %collective-permute-done.1.refs_1_.refs_0_, s16[528,128]{1,0:T(8,128)(2,1)S(1)} %collective-permute-done.2.refs_2_.refs_1_, ...), custom_call_target="tpu_custom_call" | custom-call | tf_op jit(solution)/shard_map/trials_coded/pallas_call | solution.py:290
  19.6 1.6 %collective-permute-start.3 = (s16[584,128]{1,0:T(8,128)(2,1)S(1)}, s16[584,128]{1,0:T(8,128)(2,1)S(1)}, u32[]{:S(2)}, u32[]{:S(2)}) collective-permute-start(s16[584,128]{1,0:T(8,128)(2,1)S(1)} %get-tuple-element.31), channel_id=1, source_target_pairs={{0,4},{4,0},{8,12},{12,8},{16,20},{20,16},{24,28},{28,24},{1,17},{... | collective-permute-start | bytes 448520 | tf_op jit(solution)/shard_map/ppermute | solution.py:528
  21.2 3.5 %collective-permute-start.4 = (s16[584,128]{1,0:T(8,128)(2,1)S(1)}, s16[584,128]{1,0:T(8,128)(2,1)S(1)}, u32[]{:S(2)}, u32[]{:S(2)}) collective-permute-start(s16[584,128]{1,0:T(8,128)(2,1)S(1)} %get-tuple-element.32), channel_id=1, source_target_pairs={{0,8},{4,12},{8,0},{12,4},{16,24},{20,28},{24,16},{28,20},{2,10},{... | collective-permute-start | bytes 448520 | tf_op jit(solution)/shard_map/ppermute | solution.py:528
  24.7 2.3 %collective-permute-start.5 = (s16[584,128]{1,0:T(8,128)(2,1)S(1)}, s16[584,128]{1,0:T(8,128)(2,1)S(1)}, u32[]{:S(2)}, u32[]{:S(2)}) collective-permute-start(s16[584,128]{1,0:T(8,128)(2,1)S(1)} %get-tuple-element.33), channel_id=1, source_target_pairs={{0,12},{4,8},{8,4},{12,0},{16,28},{20,24},{24,20},{28,16},{2,14},{... | collective-permute-start | bytes 448520 | tf_op jit(solution)/shard_map/ppermute | solution.py:528
  27.0 2.2 %trials.4 = (f32[576,128]{1,0:T(8,128)S(1)}, bf16[256,512]{1,0:T(8,128)(2,1)S(1)}, f32[32,128]{1,0:T(8,128)S(1)}) custom-call(s32[64,64]{1,0:T(8,128)S(1)} %copy-done, s16[528,128]{1,0:T(8,128)(2,1)S(1)} %collective-permute-done.refs_0_, s16[528,128]{1,0:T(8,128)(2,1)S(1)} %collective-permute-done.1.refs_1_.refs_0_, ...), custom_call_target="tpu_custom_call" | custom-call | tf_op jit(solution)/shard_map/trials/pallas_call | solution.py:290
  29.2 0.0 collective-permute-done.3.refs_0_
  29.2 0.4 %collective-permute-done.4.refs_1_ = s16[584,128]{1,0:T(8,128)(2,1)S(1)} collective-permute-done((s16[584,128]{1,0:T(8,128)(2,1)S(1)}, s16[584,128]{1,0:T(8,128)(2,1)S(1)}, u32[]{:S(2)}, u32[]{:S(2)}) %collective-permute-start.4) | collective-permute-done | bytes 149536 | tf_op jit(solution)/shard_map/ppermute | solution.py:528
  29.6 3.0 %collective-permute-done.5.refs_2_ = s16[584,128]{1,0:T(8,128)(2,1)S(1)} collective-permute-done((s16[584,128]{1,0:T(8,128)(2,1)S(1)}, s16[584,128]{1,0:T(8,128)(2,1)S(1)}, u32[]{:S(2)}, u32[]{:S(2)}) %collective-permute-start.5) | collective-permute-done | bytes 149536 | tf_op jit(solution)/shard_map/ppermute | solution.py:528
  32.6 0.2 cut.1
  32.9 0.1 collective-permute-start.6
  32.9 1.6 %collective-permute-start.7 = (s16[208,128]{1,0:T(8,128)(2,1)S(1)}, s16[208,128]{1,0:T(8,128)(2,1)S(1)}, u32[]{:S(2)}, u32[]{:S(2)}) collective-permute-start(s16[208,128]{1,0:T(8,128)(2,1)S(1)} %get-tuple-element.36), channel_id=1, source_target_pairs={{0,2},{1,3},{2,0},{3,1},{4,6},{5,7},{6,4},{7,5},{8,10},{9,11},{10,... | collective-permute-start | bytes 159752 | tf_op jit(solution)/shard_map/ppermute | solution.py:555
  34.5 0.3 collective-permute-start.8
  34.8 2.4 %collective-permute-done.7.refs_1_ = s16[208,128]{1,0:T(8,128)(2,1)S(1)} collective-permute-done((s16[208,128]{1,0:T(8,128)(2,1)S(1)}, s16[208,128]{1,0:T(8,128)(2,1)S(1)}, u32[]{:S(2)}, u32[]{:S(2)}) %collective-permute-start.7) | collective-permute-done | bytes 53280 | tf_op jit(solution)/shard_map/ppermute | solution.py:555
  37.2 1.1 %collective-permute-done.8.refs_2_ = s16[208,128]{1,0:T(8,128)(2,1)S(1)} collective-permute-done((s16[208,128]{1,0:T(8,128)(2,1)S(1)}, s16[208,128]{1,0:T(8,128)(2,1)S(1)}, u32[]{:S(2)}, u32[]{:S(2)}) %collective-permute-start.8) | collective-permute-done | bytes 53280 | tf_op jit(solution)/shard_map/ppermute | solution.py:555
  38.3 2.3 %fold.1 = (f32[512,128]{1,0:T(8,128)}, f32[2048,128]{1,0:T(8,128)}) custom-call(bf16[256,512]{1,0:T(8,128)(2,1)S(1)} %get-tuple-element.22.band_ref, f32[32,128]{1,0:T(8,128)S(1)} %get-tuple-element.23.weight_ref, f32[200,128]{1,0:T(8,128)S(1)} %get-tuple-element.34.mine_ref, s16[208,128]{1,0:T(8,128)(2,1)S(1)} %collective-permute-done.6.refs_0_, ...), custom_call_target="tpu_custom_call" | custom-call | tf_op jit(solution)/shard_map/fold/pallas_call | solution.py:481
  (5 shorter events, 0.0 us)
Async XLA Ops:
  0.6 11.5 %copy-start = (s32[64,64]{1,0:T(8,128)S(1)}, s32[64,64]{1,0:T(8,128)}, u32[]{:S(2)}) copy-start(s32[64,64]{1,0:T(8,128)} %delays.7) | copy-start | bytes 49156
  0.6 26.3 %copy-start.1 = (s32[4]{0:T(128)S(1)}, s32[4]{0:T(128)}, u32[]{:S(2)}) copy-start(s32[4]{0:T(128)} %refs_4_.1) | copy-start | bytes 52
  6.7 9.0 %collective-permute-start = (s16[528,128]{1,0:T(8,128)(2,1)S(1)}, s16[528,128]{1,0:T(8,128)(2,1)S(1)}, u32[]{:S(2)}, u32[]{:S(2)}) collective-permute-start(s16[528,128]{1,0:T(8,128)(2,1)S(1)} %subbands.1.refs_0_), channel_id=1, source_target_pairs={{0,16},{4,20},{8,24},{12,28},{16,0},{20,4},{24,8},{28,12},{1,5},{5... | collective-permute-start | bytes 405512 | tf_op jit(solution)/shard_map/ppermute | solution.py:528
  10.8 7.7 %collective-permute-start.1 = (s16[528,128]{1,0:T(8,128)(2,1)S(1)}, s16[528,128]{1,0:T(8,128)(2,1)S(1)}, u32[]{:S(2)}, u32[]{:S(2)}) collective-permute-start(s16[528,128]{1,0:T(8,128)(2,1)S(1)} %subbands.1.refs_0_), channel_id=1, source_target_pairs={{1,9},{5,13},{9,1},{13,5},{17,25},{21,29},{25,17},{29,21},{3,11},{... | collective-permute-start | bytes 405512 | tf_op jit(solution)/shard_map/ppermute | solution.py:528
  11.5 7.1 %collective-permute-start.2 = (s16[528,128]{1,0:T(8,128)(2,1)S(1)}, s16[528,128]{1,0:T(8,128)(2,1)S(1)}, u32[]{:S(2)}, u32[]{:S(2)}) collective-permute-start(s16[528,128]{1,0:T(8,128)(2,1)S(1)} %subbands.1.refs_0_), channel_id=1, source_target_pairs={{1,13},{5,9},{9,5},{13,1},{17,29},{21,25},{25,21},{29,17},{3,15},{... | collective-permute-start | bytes 405512 | tf_op jit(solution)/shard_map/ppermute | solution.py:528
  19.6 9.6 %collective-permute-start.3 = (s16[584,128]{1,0:T(8,128)(2,1)S(1)}, s16[584,128]{1,0:T(8,128)(2,1)S(1)}, u32[]{:S(2)}, u32[]{:S(2)}) collective-permute-start(s16[584,128]{1,0:T(8,128)(2,1)S(1)} %get-tuple-element.31), channel_id=1, source_target_pairs={{0,4},{4,0},{8,12},{12,8},{16,20},{20,16},{24,28},{28,24},{1,17},{... | collective-permute-start | bytes 448520 | tf_op jit(solution)/shard_map/ppermute | solution.py:528
  21.2 8.4 %collective-permute-start.4 = (s16[584,128]{1,0:T(8,128)(2,1)S(1)}, s16[584,128]{1,0:T(8,128)(2,1)S(1)}, u32[]{:S(2)}, u32[]{:S(2)}) collective-permute-start(s16[584,128]{1,0:T(8,128)(2,1)S(1)} %get-tuple-element.32), channel_id=1, source_target_pairs={{0,8},{4,12},{8,0},{12,4},{16,24},{20,28},{24,16},{28,20},{2,10},{... | collective-permute-start | bytes 448520 | tf_op jit(solution)/shard_map/ppermute | solution.py:528
  24.7 8.0 %collective-permute-start.5 = (s16[584,128]{1,0:T(8,128)(2,1)S(1)}, s16[584,128]{1,0:T(8,128)(2,1)S(1)}, u32[]{:S(2)}, u32[]{:S(2)}) collective-permute-start(s16[584,128]{1,0:T(8,128)(2,1)S(1)} %get-tuple-element.33), channel_id=1, source_target_pairs={{0,12},{4,8},{8,4},{12,0},{16,28},{20,24},{24,20},{28,16},{2,14},{... | collective-permute-start | bytes 448520 | tf_op jit(solution)/shard_map/ppermute | solution.py:528
  32.9 1.9 %collective-permute-start.6 = (s16[208,128]{1,0:T(8,128)(2,1)S(1)}, s16[208,128]{1,0:T(8,128)(2,1)S(1)}, u32[]{:S(2)}, u32[]{:S(2)}) collective-permute-start(s16[208,128]{1,0:T(8,128)(2,1)S(1)} %get-tuple-element.35), channel_id=1, source_target_pairs={{0,1},{1,0},{2,3},{3,2},{4,5},{5,4},{6,7},{7,6},{8,9},{9,8},{10,11... | collective-permute-start | bytes 159752 | tf_op jit(solution)/shard_map/ppermute | solution.py:555
  32.9 4.2 %collective-permute-start.7 = (s16[208,128]{1,0:T(8,128)(2,1)S(1)}, s16[208,128]{1,0:T(8,128)(2,1)S(1)}, u32[]{:S(2)}, u32[]{:S(2)}) collective-permute-start(s16[208,128]{1,0:T(8,128)(2,1)S(1)} %get-tuple-element.36), channel_id=1, source_target_pairs={{0,2},{1,3},{2,0},{3,1},{4,6},{5,7},{6,4},{7,5},{8,10},{9,11},{10,... | collective-permute-start | bytes 159752 | tf_op jit(solution)/shard_map/ppermute | solution.py:555
  34.5 3.8 %collective-permute-start.8 = (s16[208,128]{1,0:T(8,128)(2,1)S(1)}, s16[208,128]{1,0:T(8,128)(2,1)S(1)}, u32[]{:S(2)}, u32[]{:S(2)}) collective-permute-start(s16[208,128]{1,0:T(8,128)(2,1)S(1)} %get-tuple-element.37), channel_id=1, source_target_pairs={{0,3},{1,2},{2,1},{3,0},{4,7},{5,6},{6,5},{7,4},{8,11},{9,10},{10,... | collective-permute-start | bytes 159752 | tf_op jit(solution)/shard_map/ppermute | solution.py:555

commit v6 on v4

--- a/solution.py
+++ b/solution.py
@@ -22,7 +22,6 @@
 GROUP = 2**LEVELS
 ROW_BLOCKS = NBIN // LANES
 LEAD = (D1MAX + D2MAX) // LANES
-BOX_ROWS = 4
 VMEM_LIMIT = 48 << 20
 SCALE = 2.0 ** (-LEVELS / 2) / math.sqrt(NCHAN)
 
@@ -342,8 +341,8 @@
 
 
 def fold_kernel(periods, trials, owners, widths, band_ref, weight_ref, mine_ref, *refs):
-    parts, (ffa_hbm, box_hbm) = refs[: owners - 1], refs[owners - 1 : owners + 1]
-    rows_in, code, left, ffa_ref, box_ref, ffa_sem, box_sem = refs[owners + 1 :]
+    parts, (ffa_ref, box_ref) = refs[: owners - 1], refs[owners - 1 : owners + 1]
+    rows_in, code, left = refs[owners + 1 :]
     here = lax.axis_index("tm")
     bin_blocks = ROW_BLOCKS // owners
     row_len = (bin_blocks + 1) * trials
@@ -371,7 +370,6 @@
     weights = [weight_ref[8 * w : 8 * w + trials, :] for w in range(widths)]
     lane = lane_iota(trials)
     row_count = owners * periods
-    copies = []
 
     def moved(row, by):
         if by == 0:
@@ -382,15 +380,6 @@
             after = rolled[min(b + 1, bin_blocks)]
             out.append(jnp.where(lane < LANES - by, rolled[b], after))
         return out
-
-    def leave(held_ref, hbm, sem, per_trial, first, size):
-        for k in range(trials):
-            at = pl.ds(k * per_trial + first, size)
-            piece = k * (per_trial // size) + first // size
-            copies.append(
-                pltpu.make_async_copy(held_ref.at[at, :], hbm.at[at, :], sem.at[piece])
-            )
-            copies[-1].start()
 
     for group in range(row_count // GROUP):
         rows = []
@@ -420,31 +409,21 @@
                 first = (row // 8 * bin_blocks + b) * 8 + row % 8
                 step = row_count * bin_blocks
                 ffa_ref[pl.ds(first, trials, stride=step), :] = rows[r][b]
-        per_trial = row_count * bin_blocks
-        size = GROUP * bin_blocks
-        leave(ffa_ref, ffa_hbm, ffa_sem, per_trial, group * size, size)
-        for start in range(0, GROUP, BOX_ROWS):
-            lines = bin_blocks * trials
-            rest = left[start * lines : (start + BOX_ROWS) * lines, :]
-            product = None
-            for _ in range(2):
-                high = rest.astype(jnp.bfloat16)
-                rest = rest - high.astype(F32)
-                term = jnp.dot(high, band, preferred_element_type=F32)
-                product = term if product is None else product + term
-            step = row_count * bin_blocks * widths
-            for i in range(BOX_ROWS * bin_blocks):
-                for w in range(widths):
-                    value = product[
-                        i * trials : (i + 1) * trials, w * LANES : (w + 1) * LANES
-                    ]
-                    line = (group * GROUP + start) * bin_blocks + i
-                    first = line * widths + w
-                    box_ref[pl.ds(first, trials, stride=step), :] = value * weights[w]
-            size = BOX_ROWS * bin_blocks * widths
-            leave(box_ref, box_hbm, box_sem, step, (group * GROUP + start) // BOX_ROWS * size, size)
-    for copy in copies:
-        copy.wait()
+        rest = left[...]
+        product = None
+        for _ in range(2):
+            high = rest.astype(jnp.bfloat16)
+            rest = rest - high.astype(F32)
+            term = jnp.dot(high, band, preferred_element_type=F32)
+            product = term if product is None else product + term
+        step = row_count * bin_blocks * widths
+        for i in range(GROUP * bin_blocks):
+            for w in range(widths):
+                value = product[
+                    i * trials : (i + 1) * trials, w * LANES : (w + 1) * LANES
+                ]
+                first = (group * GROUP * bin_blocks + i) * widths + w
+                box_ref[pl.ds(first, trials, stride=step), :] = value * weights[w]
 
 
 def fold_and_box(mine, parts, taps, periods, trials, owners):
@@ -456,20 +435,15 @@
     ffa_shape = jax.ShapeDtypeStruct((ffa_rows, LANES), F32)
     box_shape = jax.ShapeDtypeStruct((ffa_rows * widths, LANES), F32)
     vmem = pl.BlockSpec(memory_space=pltpu.VMEM)
-    anywhere = pl.BlockSpec(memory_space=pl.ANY)
     ffa, box = pl.pallas_call(
         functools.partial(fold_kernel, periods, trials, owners, widths),
         in_specs=[vmem] * (2 + owners),
-        out_specs=[anywhere, anywhere],
+        out_specs=[vmem, vmem],
         out_shape=[ffa_shape, box_shape],
         scratch_shapes=[
             pltpu.VMEM(((row_count + 1) * row_len, LANES), F32),
             pltpu.VMEM((max(owners - 1, 1), (periods + 1) * row_len, LANES), F32),
             pltpu.VMEM((GROUP * bin_blocks * trials, 2 * LANES), F32),
-            pltpu.VMEM(ffa_shape.shape, F32),
-            pltpu.VMEM(box_shape.shape, F32),
-            pltpu.SemaphoreType.DMA((trials * row_count // GROUP,)),
-            pltpu.SemaphoreType.DMA((trials * row_count // BOX_ROWS,)),
         ],
         compiler_params=pltpu.CompilerParams(vmem_limit_bytes=VMEM_LIMIT),
         name="fold",

time: 35.8 us -> 35.6 us (level)
  no operation moved by 1% of the time
where the time goes in v6:
time: 35.6 us; the launch traced here: 35.5 us
  Pallas kernels  17.8 us (50%)
  starting transfers between devices  9.22 us (26%)
  waiting for transfers between devices  7.7 us (22%)
  between operations  0.72 us (2%)
    pallas_call x5, Pallas kernels, trial_sums(): pl.pallas_call(functools.partial(trial_kernel, *sizes, tuple(origins), tu...  9.38 us
    pallas_call x1, Pallas kernels, subband_sums(): pl.pallas_call(functools.partial(subband_kernel, chans, blocks, subs), in...  6.07 us
    ppermute x3, starting transfers between devices, per_device(): part[flip] = lax.ppermute(own, 'chan', pairs(chan_size, flip))  4.63 us
    ppermute x3, waiting for transfers between devices, per_device(): lax.ppermute(send, 'tm', pairs(owners, flip + 1))  3.48 us
    ppermute x3, waiting for transfers between devices, per_device(): part[flip] = lax.ppermute(own, 'chan', pairs(chan_size, flip))  2.94 us
    ppermute x1, starting transfers between devices, per_device(): lax.ppermute(send, 'chan', pairs(chan_size, flip))  2.66 us
    pallas_call x1, Pallas kernels, fold_and_box(): pl.pallas_call(functools.partial(fold_kernel, periods, trials, owners, wi...  2.2 us
    ppermute x3, starting transfers between devices, per_device(): lax.ppermute(send, 'tm', pairs(owners, flip + 1))  1.93 us
  transfers between devices with their start and end apart: 7, of which 5 were waited for; matrix products, arithmetic and copies ran while one was open for 0% of the time, Pallas kernels for 22%

profile of v6, /device:TPU:0, one launch (start us, length us, event | category | flops | bytes accessed | tf_op | source)
XLA Modules:
  0.0 35.5 jit_solution(1617665612864092540)
XLA Ops:
  0.6 0.0 copy-start
  0.7 6.1 %subbands.1.refs_0_ = s16[528,128]{1,0:T(8,128)(2,1)S(1)} custom-call(s32[512]{0:T(512)} %delay_hbm.1, bf16[512,8192]{1,0:T(8,128)(2,1)} %x_hbm.1), custom_call_target="tpu_custom_call" | custom-call | tf_op jit(solution)/shard_map/subbands/pallas_call | solution.py:125
  6.7 3.1 %collective-permute-start = (s16[528,128]{1,0:T(8,128)(2,1)S(1)}, s16[528,128]{1,0:T(8,128)(2,1)S(1)}, u32[]{:S(2)}, u32[]{:S(2)}) collective-permute-start(s16[528,128]{1,0:T(8,128)(2,1)S(1)} %subbands.1.refs_0_), channel_id=1, source_target_pairs={{0,8},{4,12},{8,0},{12,4},{16,24},{20,28},{24,16},{28,20},{1,9},{5... | collective-permute-start | bytes 405512 | tf_op jit(solution)/shard_map/ppermute | solution.py:468
  9.8 1.5 %collective-permute-start.1 = (s16[528,128]{1,0:T(8,128)(2,1)S(1)}, s16[528,128]{1,0:T(8,128)(2,1)S(1)}, u32[]{:S(2)}, u32[]{:S(2)}) collective-permute-start(s16[528,128]{1,0:T(8,128)(2,1)S(1)} %subbands.1.refs_0_), channel_id=1, source_target_pairs={{0,4},{4,0},{8,12},{12,8},{16,20},{20,16},{24,28},{28,24},{1,5},{5... | collective-permute-start | bytes 405512 | tf_op jit(solution)/shard_map/ppermute | solution.py:468
  11.3 0.0 collective-permute-start.2
  11.4 0.0 copy-done
  11.4 2.1 %trials.4 = (f32[576,128]{1,0:T(8,128)S(1)}, f32[576,128]{1,0:T(8,128)S(1)}) custom-call(s32[64,64]{1,0:T(8,128)S(1)} %copy-done, s16[528,128]{1,0:T(8,128)(2,1)S(1)} %subbands.1.refs_0_), custom_call_target="tpu_custom_call" | custom-call | tf_op jit(solution)/shard_map/trials/pallas_call | solution.py:268
  13.5 0.4 %collective-permute-done.refs_0_ = s16[528,128]{1,0:T(8,128)(2,1)S(1)} collective-permute-done((s16[528,128]{1,0:T(8,128)(2,1)S(1)}, s16[528,128]{1,0:T(8,128)(2,1)S(1)}, u32[]{:S(2)}, u32[]{:S(2)}) %collective-permute-start) | collective-permute-done | bytes 135200 | tf_op jit(solution)/shard_map/ppermute | solution.py:468
  13.8 1.4 %trials.6.refs_1_ = f32[576,128]{1,0:T(8,128)S(1)} custom-call(s32[64,64]{1,0:T(8,128)S(1)} %copy-done, s16[528,128]{1,0:T(8,128)(2,1)S(1)} %collective-permute-done.refs_0_, f32[576,128]{1,0:T(8,128)S(1)} %get-tuple-element.17.refs_1_), custom_call_target="tpu_custom_call" | custom-call | tf_op jit(solution)/shard_map/trials/pallas_call | solution.py:268
  15.2 2.6 %collective-permute-done.1.refs_1_.refs_0_ = s16[528,128]{1,0:T(8,128)(2,1)S(1)} collective-permute-done((s16[528,128]{1,0:T(8,128)(2,1)S(1)}, s16[528,128]{1,0:T(8,128)(2,1)S(1)}, u32[]{:S(2)}, u32[]{:S(2)}) %collective-permute-start.1) | collective-permute-done | bytes 135200 | tf_op jit(solution)/shard_map/ppermute | solution.py:468
  17.8 1.4 %trials.7.refs_1_ = f32[576,128]{1,0:T(8,128)S(1)} custom-call(s32[64,64]{1,0:T(8,128)S(1)} %copy-done, s16[528,128]{1,0:T(8,128)(2,1)S(1)} %collective-permute-done.1.refs_1_.refs_0_, f32[576,128]{1,0:T(8,128)S(1)} %trials.6.refs_1_), custom_call_target="tpu_custom_call" | custom-call | tf_op jit(solution)/shard_map/trials/pallas_call | solution.py:268
  19.1 0.0 collective-permute-done.2.refs_2_.refs_0_
  19.1 1.4 %trials_coded.1 = s16[584,128]{1,0:T(8,128)(2,1)S(1)} custom-call(s32[64,64]{1,0:T(8,128)S(1)} %copy-done, s16[528,128]{1,0:T(8,128)(2,1)S(1)} %collective-permute-done.2.refs_2_.refs_0_, f32[576,128]{1,0:T(8,128)S(1)} %trials.7.refs_1_), custom_call_target="tpu_custom_call" | custom-call | tf_op jit(solution)/shard_map/trials_coded/pallas_call | solution.py:268
  20.6 2.7 %collective-permute-start.3 = (s16[584,128]{1,0:T(8,128)(2,1)S(1)}, s16[584,128]{1,0:T(8,128)(2,1)S(1)}, u32[]{:S(2)}, u32[]{:S(2)}) collective-permute-start(s16[584,128]{1,0:T(8,128)(2,1)S(1)} %trials_coded.1), channel_id=1, source_target_pairs={{0,16},{4,20},{8,24},{12,28},{16,0},{20,4},{24,8},{28,12},{1,17},{... | collective-permute-start | bytes 448520 | tf_op jit(solution)/shard_map/ppermute | solution.py:482
  23.3 3.1 %trials.5 = (f32[576,128]{1,0:T(8,128)S(1)}, bf16[256,512]{1,0:T(8,128)(2,1)S(1)}, f32[32,128]{1,0:T(8,128)S(1)}) custom-call(s32[64,64]{1,0:T(8,128)S(1)} %copy-done, s16[528,128]{1,0:T(8,128)(2,1)S(1)} %collective-permute-done.refs_0_, s16[528,128]{1,0:T(8,128)(2,1)S(1)} %collective-permute-done.1.refs_1_.refs_0_, ...), custom_call_target="tpu_custom_call" | custom-call | tf_op jit(solution)/shard_map/trials/pallas_call | solution.py:268
  26.4 1.3 %collective-permute-done.3.refs_0_ = s16[584,128]{1,0:T(8,128)(2,1)S(1)} collective-permute-done((s16[584,128]{1,0:T(8,128)(2,1)S(1)}, s16[584,128]{1,0:T(8,128)(2,1)S(1)}, u32[]{:S(2)}, u32[]{:S(2)}) %collective-permute-start.3) | collective-permute-done | bytes 149536 | tf_op jit(solution)/shard_map/ppermute | solution.py:482
  27.7 0.2 cut.1
  27.9 0.1 collective-permute-start.4
  28.0 1.6 %collective-permute-start.5 = (s16[208,128]{1,0:T(8,128)(2,1)S(1)}, s16[208,128]{1,0:T(8,128)(2,1)S(1)}, u32[]{:S(2)}, u32[]{:S(2)}) collective-permute-start(s16[208,128]{1,0:T(8,128)(2,1)S(1)} %get-tuple-element.20), channel_id=1, source_target_pairs={{0,2},{1,3},{2,0},{3,1},{4,6},{5,7},{6,4},{7,5},{8,10},{9,11},{10,... | collective-permute-start | bytes 159752 | tf_op jit(solution)/shard_map/ppermute | solution.py:491
  29.5 0.3 collective-permute-start.6
  29.8 0.0 collective-permute-done.4.refs_0_
  29.8 2.4 %collective-permute-done.5.refs_1_ = s16[208,128]{1,0:T(8,128)(2,1)S(1)} collective-permute-done((s16[208,128]{1,0:T(8,128)(2,1)S(1)}, s16[208,128]{1,0:T(8,128)(2,1)S(1)}, u32[]{:S(2)}, u32[]{:S(2)}) %collective-permute-start.5) | collective-permute-done | bytes 53280 | tf_op jit(solution)/shard_map/ppermute | solution.py:491
  32.2 1.1 %collective-permute-done.6.refs_2_ = s16[208,128]{1,0:T(8,128)(2,1)S(1)} collective-permute-done((s16[208,128]{1,0:T(8,128)(2,1)S(1)}, s16[208,128]{1,0:T(8,128)(2,1)S(1)}, u32[]{:S(2)}, u32[]{:S(2)}) %collective-permute-start.6) | collective-permute-done | bytes 53280 | tf_op jit(solution)/shard_map/ppermute | solution.py:491
  33.3 2.2 %fold.1 = (f32[512,128]{1,0:T(8,128)}, f32[2048,128]{1,0:T(8,128)}) custom-call(bf16[256,512]{1,0:T(8,128)(2,1)S(1)} %get-tuple-element.14.band_ref, f32[32,128]{1,0:T(8,128)S(1)} %get-tuple-element.15.weight_ref, f32[200,128]{1,0:T(8,128)S(1)} %get-tuple-element.18.mine_ref, s16[208,128]{1,0:T(8,128)(2,1)S(1)} %collective-permute-done.4.refs_0_, ...), custom_call_target="tpu_custom_call" | custom-call | tf_op jit(solution)/shard_map/fold/pallas_call | solution.py:438
  (2 shorter events, 0.0 us)
Async XLA Ops:
  0.6 10.7 %copy-start = (s32[64,64]{1,0:T(8,128)S(1)}, s32[64,64]{1,0:T(8,128)}, u32[]{:S(2)}) copy-start(s32[64,64]{1,0:T(8,128)} %delays.9) | copy-start | bytes 49156
  0.6 22.6 %copy-start.1 = (s32[4]{0:T(128)S(1)}, s32[4]{0:T(128)}, u32[]{:S(2)}) copy-start(s32[4]{0:T(128)} %refs_4_.1) | copy-start | bytes 52
  6.7 7.1 %collective-permute-start = (s16[528,128]{1,0:T(8,128)(2,1)S(1)}, s16[528,128]{1,0:T(8,128)(2,1)S(1)}, u32[]{:S(2)}, u32[]{:S(2)}) collective-permute-start(s16[528,128]{1,0:T(8,128)(2,1)S(1)} %subbands.1.refs_0_), channel_id=1, source_target_pairs={{0,8},{4,12},{8,0},{12,4},{16,24},{20,28},{24,16},{28,20},{1,9},{5... | collective-permute-start | bytes 405512 | tf_op jit(solution)/shard_map/ppermute | solution.py:468
  9.8 7.9 %collective-permute-start.1 = (s16[528,128]{1,0:T(8,128)(2,1)S(1)}, s16[528,128]{1,0:T(8,128)(2,1)S(1)}, u32[]{:S(2)}, u32[]{:S(2)}) collective-permute-start(s16[528,128]{1,0:T(8,128)(2,1)S(1)} %subbands.1.refs_0_), channel_id=1, source_target_pairs={{0,4},{4,0},{8,12},{12,8},{16,20},{20,16},{24,28},{28,24},{1,5},{5... | collective-permute-start | bytes 405512 | tf_op jit(solution)/shard_map/ppermute | solution.py:468
  11.3 7.8 %collective-permute-start.2 = (s16[528,128]{1,0:T(8,128)(2,1)S(1)}, s16[528,128]{1,0:T(8,128)(2,1)S(1)}, u32[]{:S(2)}, u32[]{:S(2)}) collective-permute-start(s16[528,128]{1,0:T(8,128)(2,1)S(1)} %subbands.1.refs_0_), channel_id=1, source_target_pairs={{0,12},{4,8},{8,4},{12,0},{16,28},{20,24},{24,20},{28,16},{1,13},{... | collective-permute-start | bytes 405512 | tf_op jit(solution)/shard_map/ppermute | solution.py:468
  20.6 7.1 %collective-permute-start.3 = (s16[584,128]{1,0:T(8,128)(2,1)S(1)}, s16[584,128]{1,0:T(8,128)(2,1)S(1)}, u32[]{:S(2)}, u32[]{:S(2)}) collective-permute-start(s16[584,128]{1,0:T(8,128)(2,1)S(1)} %trials_coded.1), channel_id=1, source_target_pairs={{0,16},{4,20},{8,24},{12,28},{16,0},{20,4},{24,8},{28,12},{1,17},{... | collective-permute-start | bytes 448520 | tf_op jit(solution)/shard_map/ppermute | solution.py:482
  27.9 1.9 %collective-permute-start.4 = (s16[208,128]{1,0:T(8,128)(2,1)S(1)}, s16[208,128]{1,0:T(8,128)(2,1)S(1)}, u32[]{:S(2)}, u32[]{:S(2)}) collective-permute-start(s16[208,128]{1,0:T(8,128)(2,1)S(1)} %get-tuple-element.19), channel_id=1, source_target_pairs={{0,1},{1,0},{2,3},{3,2},{4,5},{5,4},{6,7},{7,6},{8,9},{9,8},{10,11... | collective-permute-start | bytes 159752 | tf_op jit(solution)/shard_map/ppermute | solution.py:491
  28.0 4.2 %collective-permute-start.5 = (s16[208,128]{1,0:T(8,128)(2,1)S(1)}, s16[208,128]{1,0:T(8,128)(2,1)S(1)}, u32[]{:S(2)}, u32[]{:S(2)}) collective-permute-start(s16[208,128]{1,0:T(8,128)(2,1)S(1)} %get-tuple-element.20), channel_id=1, source_target_pairs={{0,2},{1,3},{2,0},{3,1},{4,6},{5,7},{6,4},{7,5},{8,10},{9,11},{10,... | collective-permute-start | bytes 159752 | tf_op jit(solution)/shard_map/ppermute | solution.py:491
  29.5 3.8 %collective-permute-start.6 = (s16[208,128]{1,0:T(8,128)(2,1)S(1)}, s16[208,128]{1,0:T(8,128)(2,1)S(1)}, u32[]{:S(2)}, u32[]{:S(2)}) collective-permute-start(s16[208,128]{1,0:T(8,128)(2,1)S(1)} %get-tuple-element.21), channel_id=1, source_target_pairs={{0,3},{1,2},{2,1},{3,0},{4,7},{5,6},{6,5},{7,4},{8,11},{9,10},{10,... | collective-permute-start | bytes 159752 | tf_op jit(solution)/shard_map/ppermute | solution.py:491

commit v7 on v6

--- a/solution.py
+++ b/solution.py
@@ -469,22 +469,18 @@
     sizes = (blocks, subs, trials)
     flips = tuple(range(quad, chan_size, quad))
     early, final = ((0, 2, 1), (3,)) if quad == 4 else ((0,), tuple(range(1, quad)))
-    far, near = None, None
+    far = None
     for origin in early:
-        both = origin == 0
-        sums = trial_sums(
-            [part[origin]], (origin,), sub_delay, sizes, (*flips, 0) if both else flips, far
-        )
-        far, near = (sums[:-1], sums[-1:]) if both else (sums, near)
+        far = trial_sums([part[origin]], (origin,), sub_delay, sizes, flips, far)
     last = [part[origin] for origin in final]
     far = trial_sums(last, final, sub_delay, sizes, flips, far, True)
     far = [
         lax.ppermute(send, "chan", pairs(chan_size, flip))
         for send, flip in zip(far, flips)
     ]
-    rest = (*early[1:], *final)
+    rest = (*early, *final)
     near, *taps = trial_sums(
-        [part[o] for o in rest], rest, sub_delay, sizes, (0,), near, box_width=box_width
+        [part[o] for o in rest], rest, sub_delay, sizes, (0,), box_width=box_width
     )
     mine, *sends = cut_by_phase(near, far, blocks, trials, owners)
     got = [

time: 35.6 us -> 35.6 us (level)
    ppermute x3, waiting for transfers between devices: 2.94 us -> 3.66 us  [per_device(): part[flip] = lax.ppermute(own, 'chan', pairs(chan_size, flip))]
    ppermute x1, waiting for transfers between devices: 1.29 us -> 0.7 us  [per_device(): lax.ppermute(send, 'chan', pairs(chan_size, flip))]
where the time goes in v7:
time: 35.6 us; the launch traced here: 35.5 us
  Pallas kernels  17.7 us (50%)
  starting transfers between devices  9.22 us (26%)
  waiting for transfers between devices  7.84 us (22%)
  between operations  0.72 us (2%)
    pallas_call x5, Pallas kernels, trial_sums(): pl.pallas_call(functools.partial(trial_kernel, *sizes, tuple(origins), tu...  9.26 us
    pallas_call x1, Pallas kernels, subband_sums(): pl.pallas_call(functools.partial(subband_kernel, chans, blocks, subs), in...  6.07 us
    ppermute x3, starting transfers between devices, per_device(): part[flip] = lax.ppermute(own, 'chan', pairs(chan_size, flip))  4.63 us
    ppermute x3, waiting for transfers between devices, per_device(): part[flip] = lax.ppermute(own, 'chan', pairs(chan_size, flip))  3.66 us
    ppermute x3, waiting for transfers between devices, per_device(): lax.ppermute(send, 'tm', pairs(owners, flip + 1))  3.48 us
    ppermute x1, starting transfers between devices, per_device(): lax.ppermute(send, 'chan', pairs(chan_size, flip))  2.65 us
    pallas_call x1, Pallas kernels, fold_and_box(): pl.pallas_call(functools.partial(fold_kernel, periods, trials, owners, wi...  2.2 us
    ppermute x3, starting transfers between devices, per_device(): lax.ppermute(send, 'tm', pairs(owners, flip + 1))  1.93 us
  transfers between devices with their start and end apart: 7, of which 5 were waited for; matrix products, arithmetic and copies ran while one was open for 0% of the time, Pallas kernels for 22%

profile of v7, /device:TPU:0, one launch (start us, length us, event | category | flops | bytes accessed | tf_op | source)
XLA Modules:
  0.0 35.5 jit_solution(2442501550629623424)
XLA Ops:
  0.6 0.0 copy-start
  0.6 0.0 copy-start.1
  0.7 6.1 %subbands.1.refs_0_ = s16[528,128]{1,0:T(8,128)(2,1)S(1)} custom-call(s32[512]{0:T(512)} %delay_hbm.1, bf16[512,8192]{1,0:T(8,128)(2,1)} %x_hbm.1), custom_call_target="tpu_custom_call" | custom-call | tf_op jit(solution)/shard_map/subbands/pallas_call | solution.py:125
  6.7 3.1 %collective-permute-start = (s16[528,128]{1,0:T(8,128)(2,1)S(1)}, s16[528,128]{1,0:T(8,128)(2,1)S(1)}, u32[]{:S(2)}, u32[]{:S(2)}) collective-permute-start(s16[528,128]{1,0:T(8,128)(2,1)S(1)} %subbands.1.refs_0_), channel_id=1, source_target_pairs={{0,8},{4,12},{8,0},{12,4},{16,24},{20,28},{24,16},{28,20},{1,9},{5... | collective-permute-start | bytes 405512 | tf_op jit(solution)/shard_map/ppermute | solution.py:468
  9.8 1.5 %collective-permute-start.1 = (s16[528,128]{1,0:T(8,128)(2,1)S(1)}, s16[528,128]{1,0:T(8,128)(2,1)S(1)}, u32[]{:S(2)}, u32[]{:S(2)}) collective-permute-start(s16[528,128]{1,0:T(8,128)(2,1)S(1)} %subbands.1.refs_0_), channel_id=1, source_target_pairs={{0,4},{4,0},{8,12},{12,8},{16,20},{20,16},{24,28},{28,24},{1,5},{5... | collective-permute-start | bytes 405512 | tf_op jit(solution)/shard_map/ppermute | solution.py:468
  11.3 0.0 collective-permute-start.2
  11.4 1.4 %trials.5.refs_1_ = f32[576,128]{1,0:T(8,128)S(1)} custom-call(s32[64,64]{1,0:T(8,128)S(1)} %copy-done, s16[528,128]{1,0:T(8,128)(2,1)S(1)} %subbands.1.refs_0_), custom_call_target="tpu_custom_call" | custom-call | tf_op jit(solution)/shard_map/trials/pallas_call | solution.py:268
  12.7 1.1 %collective-permute-done.refs_1_.refs_0_ = s16[528,128]{1,0:T(8,128)(2,1)S(1)} collective-permute-done((s16[528,128]{1,0:T(8,128)(2,1)S(1)}, s16[528,128]{1,0:T(8,128)(2,1)S(1)}, u32[]{:S(2)}, u32[]{:S(2)}) %collective-permute-start) | collective-permute-done | bytes 135200 | tf_op jit(solution)/shard_map/ppermute | solution.py:468
  13.8 1.4 %trials.6.refs_1_ = f32[576,128]{1,0:T(8,128)S(1)} custom-call(s32[64,64]{1,0:T(8,128)S(1)} %copy-done, s16[528,128]{1,0:T(8,128)(2,1)S(1)} %collective-permute-done.refs_1_.refs_0_, f32[576,128]{1,0:T(8,128)S(1)} %trials.5.refs_1_), custom_call_target="tpu_custom_call" | custom-call | tf_op jit(solution)/shard_map/trials/pallas_call | solution.py:268
  15.2 2.6 %collective-permute-done.1.refs_2_.refs_0_ = s16[528,128]{1,0:T(8,128)(2,1)S(1)} collective-permute-done((s16[528,128]{1,0:T(8,128)(2,1)S(1)}, s16[528,128]{1,0:T(8,128)(2,1)S(1)}, u32[]{:S(2)}, u32[]{:S(2)}) %collective-permute-start.1) | collective-permute-done | bytes 135200 | tf_op jit(solution)/shard_map/ppermute | solution.py:468
  17.8 1.4 %trials.7.refs_1_ = f32[576,128]{1,0:T(8,128)S(1)} custom-call(s32[64,64]{1,0:T(8,128)S(1)} %copy-done, s16[528,128]{1,0:T(8,128)(2,1)S(1)} %collective-permute-done.1.refs_2_.refs_0_, f32[576,128]{1,0:T(8,128)S(1)} %trials.6.refs_1_), custom_call_target="tpu_custom_call" | custom-call | tf_op jit(solution)/shard_map/trials/pallas_call | solution.py:268
  19.1 0.0 collective-permute-done.2.refs_3_.refs_0_
  19.1 1.4 %trials_coded.1 = s16[584,128]{1,0:T(8,128)(2,1)S(1)} custom-call(s32[64,64]{1,0:T(8,128)S(1)} %copy-done, s16[528,128]{1,0:T(8,128)(2,1)S(1)} %collective-permute-done.2.refs_3_.refs_0_, f32[576,128]{1,0:T(8,128)S(1)} %trials.7.refs_1_), custom_call_target="tpu_custom_call" | custom-call | tf_op jit(solution)/shard_map/trials_coded/pallas_call | solution.py:268
  20.6 2.7 %collective-permute-start.3 = (s16[584,128]{1,0:T(8,128)(2,1)S(1)}, s16[584,128]{1,0:T(8,128)(2,1)S(1)}, u32[]{:S(2)}, u32[]{:S(2)}) collective-permute-start(s16[584,128]{1,0:T(8,128)(2,1)S(1)} %trials_coded.1), channel_id=1, source_target_pairs={{0,16},{4,20},{8,24},{12,28},{16,0},{20,4},{24,8},{28,12},{1,17},{... | collective-permute-start | bytes 448520 | tf_op jit(solution)/shard_map/ppermute | solution.py:478
  23.3 3.7 %trials.4 = (f32[576,128]{1,0:T(8,128)S(1)}, bf16[256,512]{1,0:T(8,128)(2,1)S(1)}, f32[32,128]{1,0:T(8,128)S(1)}) custom-call(s32[64,64]{1,0:T(8,128)S(1)} %copy-done, s16[528,128]{1,0:T(8,128)(2,1)S(1)} %subbands.1.refs_0_, s16[528,128]{1,0:T(8,128)(2,1)S(1)} %collective-permute-done.refs_1_.refs_0_, ...), custom_call_target="tpu_custom_call" | custom-call | tf_op jit(solution)/shard_map/trials/pallas_call | solution.py:268
  27.0 0.7 %collective-permute-done.3.refs_0_ = s16[584,128]{1,0:T(8,128)(2,1)S(1)} collective-permute-done((s16[584,128]{1,0:T(8,128)(2,1)S(1)}, s16[584,128]{1,0:T(8,128)(2,1)S(1)}, u32[]{:S(2)}, u32[]{:S(2)}) %collective-permute-start.3) | collective-permute-done | bytes 149536 | tf_op jit(solution)/shard_map/ppermute | solution.py:478
  27.7 0.2 cut.1
  27.9 0.1 collective-permute-start.4
  28.0 1.6 %collective-permute-start.5 = (s16[208,128]{1,0:T(8,128)(2,1)S(1)}, s16[208,128]{1,0:T(8,128)(2,1)S(1)}, u32[]{:S(2)}, u32[]{:S(2)}) collective-permute-start(s16[208,128]{1,0:T(8,128)(2,1)S(1)} %get-tuple-element.16), channel_id=1, source_target_pairs={{0,2},{1,3},{2,0},{3,1},{4,6},{5,7},{6,4},{7,5},{8,10},{9,11},{10,... | collective-permute-start | bytes 159752 | tf_op jit(solution)/shard_map/ppermute | solution.py:487
  29.5 0.3 collective-permute-start.6
  29.8 0.0 collective-permute-done.4.refs_0_
  29.8 2.4 %collective-permute-done.5.refs_1_ = s16[208,128]{1,0:T(8,128)(2,1)S(1)} collective-permute-done((s16[208,128]{1,0:T(8,128)(2,1)S(1)}, s16[208,128]{1,0:T(8,128)(2,1)S(1)}, u32[]{:S(2)}, u32[]{:S(2)}) %collective-permute-start.5) | collective-permute-done | bytes 53280 | tf_op jit(solution)/shard_map/ppermute | solution.py:487
  32.2 1.1 %collective-permute-done.6.refs_2_ = s16[208,128]{1,0:T(8,128)(2,1)S(1)} collective-permute-done((s16[208,128]{1,0:T(8,128)(2,1)S(1)}, s16[208,128]{1,0:T(8,128)(2,1)S(1)}, u32[]{:S(2)}, u32[]{:S(2)}) %collective-permute-start.6) | collective-permute-done | bytes 53280 | tf_op jit(solution)/shard_map/ppermute | solution.py:487
  33.3 2.2 %fold.1 = (f32[512,128]{1,0:T(8,128)}, f32[2048,128]{1,0:T(8,128)}) custom-call(bf16[256,512]{1,0:T(8,128)(2,1)S(1)} %get-tuple-element.11.band_ref, f32[32,128]{1,0:T(8,128)S(1)} %get-tuple-element.12.weight_ref, f32[200,128]{1,0:T(8,128)S(1)} %get-tuple-element.14.mine_ref, s16[208,128]{1,0:T(8,128)(2,1)S(1)} %collective-permute-done.4.refs_0_, ...), custom_call_target="tpu_custom_call" | custom-call | tf_op jit(solution)/shard_map/fold/pallas_call | solution.py:438
  (2 shorter events, 0.0 us)
Async XLA Ops:
  0.6 10.7 %copy-start = (s32[64,64]{1,0:T(8,128)S(1)}, s32[64,64]{1,0:T(8,128)}, u32[]{:S(2)}) copy-start(s32[64,64]{1,0:T(8,128)} %delays.9) | copy-start | bytes 49156
  0.6 22.6 %copy-start.1 = (s32[4]{0:T(128)S(1)}, s32[4]{0:T(128)}, u32[]{:S(2)}) copy-start(s32[4]{0:T(128)} %refs_4_.1) | copy-start | bytes 52
  6.7 7.1 %collective-permute-start = (s16[528,128]{1,0:T(8,128)(2,1)S(1)}, s16[528,128]{1,0:T(8,128)(2,1)S(1)}, u32[]{:S(2)}, u32[]{:S(2)}) collective-permute-start(s16[528,128]{1,0:T(8,128)(2,1)S(1)} %subbands.1.refs_0_), channel_id=1, source_target_pairs={{0,8},{4,12},{8,0},{12,4},{16,24},{20,28},{24,16},{28,20},{1,9},{5... | collective-permute-start | bytes 405512 | tf_op jit(solution)/shard_map/ppermute | solution.py:468
  9.8 7.9 %collective-permute-start.1 = (s16[528,128]{1,0:T(8,128)(2,1)S(1)}, s16[528,128]{1,0:T(8,128)(2,1)S(1)}, u32[]{:S(2)}, u32[]{:S(2)}) collective-permute-start(s16[528,128]{1,0:T(8,128)(2,1)S(1)} %subbands.1.refs_0_), channel_id=1, source_target_pairs={{0,4},{4,0},{8,12},{12,8},{16,20},{20,16},{24,28},{28,24},{1,5},{5... | collective-permute-start | bytes 405512 | tf_op jit(solution)/shard_map/ppermute | solution.py:468
  11.3 7.8 %collective-permute-start.2 = (s16[528,128]{1,0:T(8,128)(2,1)S(1)}, s16[528,128]{1,0:T(8,128)(2,1)S(1)}, u32[]{:S(2)}, u32[]{:S(2)}) collective-permute-start(s16[528,128]{1,0:T(8,128)(2,1)S(1)} %subbands.1.refs_0_), channel_id=1, source_target_pairs={{0,12},{4,8},{8,4},{12,0},{16,28},{20,24},{24,20},{28,16},{1,13},{... | collective-permute-start | bytes 405512 | tf_op jit(solution)/shard_map/ppermute | solution.py:468
  20.6 7.1 %collective-permute-start.3 = (s16[584,128]{1,0:T(8,128)(2,1)S(1)}, s16[584,128]{1,0:T(8,128)(2,1)S(1)}, u32[]{:S(2)}, u32[]{:S(2)}) collective-permute-start(s16[584,128]{1,0:T(8,128)(2,1)S(1)} %trials_coded.1), channel_id=1, source_target_pairs={{0,16},{4,20},{8,24},{12,28},{16,0},{20,4},{24,8},{28,12},{1,17},{... | collective-permute-start | bytes 448520 | tf_op jit(solution)/shard_map/ppermute | solution.py:478
  27.9 1.9 %collective-permute-start.4 = (s16[208,128]{1,0:T(8,128)(2,1)S(1)}, s16[208,128]{1,0:T(8,128)(2,1)S(1)}, u32[]{:S(2)}, u32[]{:S(2)}) collective-permute-start(s16[208,128]{1,0:T(8,128)(2,1)S(1)} %get-tuple-element.15), channel_id=1, source_target_pairs={{0,1},{1,0},{2,3},{3,2},{4,5},{5,4},{6,7},{7,6},{8,9},{9,8},{10,11... | collective-permute-start | bytes 159752 | tf_op jit(solution)/shard_map/ppermute | solution.py:487
  28.0 4.2 %collective-permute-start.5 = (s16[208,128]{1,0:T(8,128)(2,1)S(1)}, s16[208,128]{1,0:T(8,128)(2,1)S(1)}, u32[]{:S(2)}, u32[]{:S(2)}) collective-permute-start(s16[208,128]{1,0:T(8,128)(2,1)S(1)} %get-tuple-element.16), channel_id=1, source_target_pairs={{0,2},{1,3},{2,0},{3,1},{4,6},{5,7},{6,4},{7,5},{8,10},{9,11},{10,... | collective-permute-start | bytes 159752 | tf_op jit(solution)/shard_map/ppermute | solution.py:487
  29.5 3.8 %collective-permute-start.6 = (s16[208,128]{1,0:T(8,128)(2,1)S(1)}, s16[208,128]{1,0:T(8,128)(2,1)S(1)}, u32[]{:S(2)}, u32[]{:S(2)}) collective-permute-start(s16[208,128]{1,0:T(8,128)(2,1)S(1)} %get-tuple-element.17), channel_id=1, source_target_pairs={{0,3},{1,2},{2,1},{3,0},{4,7},{5,6},{6,5},{7,4},{8,11},{9,10},{10,... | collective-permute-start | bytes 159752 | tf_op jit(solution)/shard_map/ppermute | solution.py:487
